TPU v7x, 256 devices: a whole 4x4x8 slice. The times are simulated.
256 devices in a mesh: star: 8 (over x, core), row: 32 (over z, y).
Axes of the slice: x: 4, y: 4, z: 8, core: 2. Of those that a mesh axis runs over, the one named last changes fastest.
Arguments:
- feature_maps: bfloat16 [64, 1024, 1024], P(None, 'row'), may hold values from -6 to 6
- coef_table: bfloat16 [64, 64], replicated, may hold values from -0.119628906 to 0.119628906
- star_counts: int32 [8], replicated, may hold values from 1 to 12, 32 in all
- star_cells: int32 [8, 12], replicated, may hold values from 0 to 63
- star_bands: int32 [8, 12], replicated, may hold values from 0 to 7
- psf_cotangent: bfloat16 [96, 1024, 1024], P('star', 'row'), may hold values from -6 to 6
Outputs:
- map_grad: float32 [64, 1024, 1024], P('star', 'row')
- coef_grad: float32 [64, 64], replicated
Inputs may be any that keep to these rules, and one draw needn't show every extreme that they name: The live stars of group g fill its slots 0 to star_counts[g] - 1; the counts sum to 32, and some group has exactly 12.
All inputs are finite; a program needn't handle non-finite values.
Results may differ from a plain program's by a relative error of at most 0.008.
Values may be sent and summed in bfloat16 or wider, within the bound.
No kernel may reach another device: no remote copies, remote signals or barrier semaphores. Data moves between devices by JAX's collectives and lax.ppermute only.
A program may use at most 128 MiB of HBM per device.

v0:
```python
import jax
import jax.numpy as jnp
from jax import lax
from jax.sharding import PartitionSpec as P

BANDS = 8


def fourier_tables(pupil_size):
    index_row = jnp.arange(pupil_size, dtype=jnp.int32)
    products = index_row[:, None] * index_row[None, :] % pupil_size
    angles = 2.0 * jnp.pi / pupil_size * products.astype(jnp.float32)
    return (jnp.cos(angles).astype(jnp.bfloat16), (-jnp.sin(angles)).astype(jnp.bfloat16))


def aperture_rows(first_row, row_count, pupil_size):
    centre = 0.5 * (pupil_size - 1)
    row_pos = (first_row + jnp.arange(row_count, dtype=jnp.int32)).astype(jnp.float32) - centre
    col_pos = jnp.arange(pupil_size, dtype=jnp.int32).astype(jnp.float32) - centre
    radius = row_pos[:, None] * row_pos[:, None] + col_pos[None, :] * col_pos[None, :]
    return jnp.where(radius <= 0.25 * pupil_size * pupil_size, 1.0, 0.0).astype(jnp.float32)


def wave_numbers(band_ids):
    wavelength = 0.55 + 0.35 * band_ids.astype(jnp.float32) / (BANDS - 1)
    return 2.0 * jnp.pi / wavelength


def table_pick(values, indices):
    positions = jnp.arange(values.shape[0], dtype=jnp.int32)
    chosen = jnp.where(positions[None, :] == indices[:, None], values[None, :], 0)
    return jnp.sum(chosen, axis=1)


def per_device(feature_maps, coef_table, star_counts, star_cells, star_bands, psf_cotangent):
    groups = lax.axis_size("star")
    my_group = lax.axis_index("star")
    slot_count = psf_cotangent.shape[0]
    map_count, row_count, pupil_size = feature_maps.shape
    flat_cells = star_cells.reshape(-1)
    flat_bands = star_bands.reshape(-1)
    cell_count = coef_table.shape[0]
    within = jnp.arange(slot_count, dtype=jnp.int32)
    owner_group = jnp.zeros_like(within) + my_group
    live_mask = within < table_pick(star_counts, owner_group)
    owner_group, within, live_mask = (owner_group, within, live_mask)
    slot_index = owner_group * slot_count + within
    cell_ids = table_pick(flat_cells, slot_index)
    band_ids = table_pick(flat_bands, slot_index)
    cell_hot = cell_ids[:, None] == jnp.arange(cell_count, dtype=jnp.int32)[None, :]
    coef_rows = jnp.dot(
        cell_hot.astype(jnp.bfloat16), coef_table, preferred_element_type=jnp.float32
    ).astype(jnp.bfloat16)
    flat_maps = feature_maps.reshape(map_count, row_count * pupil_size)
    path_error = jnp.dot(coef_rows, flat_maps, preferred_element_type=jnp.float32).reshape(
        -1, row_count, pupil_size
    )
    wave_number = wave_numbers(band_ids)
    phase_angle = wave_number[:, None, None] * path_error
    aperture = aperture_rows(lax.axis_index("row") * row_count, row_count, pupil_size)
    cos_phase = jnp.cos(phase_angle)
    sin_phase = jnp.sin(phase_angle)
    pupil_field = jnp.stack([aperture * cos_phase, aperture * sin_phase], 1).astype(jnp.bfloat16)
    cos_table, sin_table = fourier_tables(pupil_size)
    inverse = 1.0 / pupil_size
    along_cos = jnp.einsum(
        "sarc,cv->sarv", pupil_field, cos_table, preferred_element_type=jnp.float32
    )
    along_sin = jnp.einsum(
        "sarc,cv->sarv", pupil_field, sin_table, preferred_element_type=jnp.float32
    )
    column_field = jnp.stack(
        [along_cos[:, 0] - along_sin[:, 1], along_sin[:, 0] + along_cos[:, 1]], 1
    ).astype(jnp.bfloat16)
    pieces = lax.all_to_all(column_field, "row", split_axis=3, concat_axis=2, tiled=True)
    row_cos = jnp.einsum("sarv,ru->savu", pieces, cos_table, preferred_element_type=jnp.float32)
    row_sin = jnp.einsum("sarv,ru->savu", pieces, sin_table, preferred_element_type=jnp.float32)
    real_part = (row_cos[:, 0] - row_sin[:, 1]) * inverse
    imag_part = (row_sin[:, 0] + row_cos[:, 1]) * inverse
    focal_field = jnp.stack([real_part, imag_part], 1)
    weight = jnp.where(live_mask, 2.0, 0.0).astype(jnp.float32)[:, None, None, None]
    focal_grad = (weight * psf_cotangent.astype(jnp.float32)[:, None] * focal_field).astype(
        jnp.bfloat16
    )
    back_cos = jnp.einsum(
        "savu,ur->savr", focal_grad, cos_table, preferred_element_type=jnp.float32
    )
    back_sin = jnp.einsum(
        "savu,ur->savr", focal_grad, sin_table, preferred_element_type=jnp.float32
    )
    spectrum_grad = jnp.stack(
        [(back_cos[:, 0] + back_sin[:, 1]) * inverse, (back_cos[:, 1] - back_sin[:, 0]) * inverse],
        1,
    ).astype(jnp.bfloat16)
    pieces = lax.all_to_all(spectrum_grad, "row", split_axis=3, concat_axis=2, tiled=True)
    col_cos = jnp.einsum("savr,vc->sarc", pieces, cos_table, preferred_element_type=jnp.float32)
    col_sin = jnp.einsum("savr,vc->sarc", pieces, sin_table, preferred_element_type=jnp.float32)
    pupil_grad = jnp.stack([col_cos[:, 0] + col_sin[:, 1], col_cos[:, 1] - col_sin[:, 0]], 1)
    phase_grad = aperture * (cos_phase * pupil_grad[:, 1] - sin_phase * pupil_grad[:, 0])
    path_grad = (
        (wave_number[:, None, None] * phase_grad)
        .astype(jnp.bfloat16)
        .reshape(-1, row_count * pupil_size)
    )
    map_scores = lax.dot_general(
        path_grad, flat_maps, (((1,), (1,)), ((), ())), preferred_element_type=jnp.float32
    )
    coef_part = lax.dot_general(
        cell_hot.astype(jnp.float32),
        map_scores * (1.0 / (8 * pupil_size)),
        (((0,), (0,)), ((), ())),
        precision=lax.Precision.HIGHEST,
    )
    coef_grad = lax.psum(coef_part, ("star", "row"))
    share = map_count // groups
    map_grad = lax.psum_scatter(
        lax.dot_general(
            coef_rows, path_grad, (((0,), (0,)), ((), ())), preferred_element_type=jnp.float32
        ),
        "star",
        scatter_dimension=0,
        tiled=True,
    )
    return (map_grad.reshape(share, row_count, pupil_size), coef_grad)


def solution(mesh):
    placed = (P(None, "row", None), P(), P(), P(), P(), P("star", "row", None))
    return jax.shard_map(
        per_device,
        mesh=mesh,
        in_specs=placed,
        out_specs=(P("star", "row", None), P()),
        check_vma=False,
    )
```

profile of v0, /device:TPU:1, one launch (start us, length us, event | category | flops | bytes accessed | tf_op | source)
XLA Modules:
  0.0 501.8 jit_solution(5607141360308045111)
XLA Ops:
  16.0 8.4 %fusion.54 = (bf16[12,1,32,1024]{3,0,2,1:T(8,128)(2,1)S(1)}, bf16[12,1,32,1024]{3,0,2,1:T(8,128)(2,1)S(1)}) fusion(f32[12,32,1024]{2,0,1:T(8,128)S(1)} %fusion.3, f32[32,1024]{1,0:T(8,128)S(1)} %fusion.56, f32[12]{0:T(128)S(1)} %add_divide_fusion), kind=kLoop, calls=%fused_computation.67 | loop fusion | flops 1966080 | bytes 3276848 | tf_op jit(solution)/shard_map/stack | solution.py:63
  24.7 17.9 %fusion.28 = f32[12,2,32,1024]{3,2,1,0:T(8,128)S(1)} fusion(bf16[12,2,32,1024]{3,0,2,1:T(8,128)(2,1)S(1)} %pad_maximum_fusion), kind=kOutput, calls=%fused_computation.36 | convolution fusion | flops 1627389952 | bytes 4718592 | tf_op jit(solution)/shard_map/sarc,cv->sarv/dot_general | solution.py:69
  42.5 17.3 %fusion.36 = f32[12,2,32,1024]{3,2,1,0:T(8,128)S(1)} fusion(bf16[12,2,32,1024]{3,0,2,1:T(8,128)(2,1)S(1)} %pad_maximum_fusion), kind=kOutput, calls=%fused_computation.40 | convolution fusion | flops 1626341376 | bytes 4718592 | tf_op jit(solution)/shard_map/sarc,cv->sarv/dot_general | solution.py:66
  62.4 15.1 %copy.45 = bf16[12,2,32,1024]{2,1,0,3:T(2,128)(2,1)} copy(bf16[12,2,32,1024]{3,2,1,0:T(8,128)(2,1)} %pad_maximum_fusion.1) | data formatting | bytes 3145728 | tf_op jit(solution)/shard_map/stack | solution.py:72
  77.5 13.8 %reshape.93 = bf16[32,2,12288]{2,1,0:T(2,128)(2,1)} reshape(bf16[1024,12,2,32]{3,2,1,0:T(2,128)(2,1)} %bitcast.93) | data formatting | bytes 3145728
  91.3 12.3 %all-to-all-start = ((bf16[32,2,12288]{2,1,0:T(2,128)(2,1)}), bf16[32,2,12288]{2,1,0:T(2,128)(2,1)}, u32[]{:S(2)}, u32[]{:S(2)}) async-start(bf16[32,2,12288]{2,1,0:T(2,128)(2,1)} %reshape.93), calls=%async_computation | async-start | bytes 3145728 | tf_op jit(solution)/shard_map/all_to_all | solution.py:75
  105.2 36.3 %all-to-all-done = bf16[32,2,12288]{2,1,0:T(2,128)(2,1)} async-done(((bf16[32,2,12288]{2,1,0:T(2,128)(2,1)}), bf16[32,2,12288]{2,1,0:T(2,128)(2,1)}, u32[]{:S(2)}, u32[]{:S(2)}) %all-to-all-start) | async-done | bytes 1572896 | tf_op jit(solution)/shard_map/all_to_all | solution.py:75
  141.5 14.3 %reshape.94 = bf16[1024,12,2,32]{3,2,1,0:T(2,128)(2,1)} reshape(bf16[32,2,12288]{2,1,0:T(2,128)(2,1)} %all-to-all-done) | data formatting | bytes 3145728
  155.7 9.5 %copy.107 = bf16[12,2,32,32,32]{2,3,4,1,0:T(8,128)(2,1)} copy(bf16[12,2,32,32,32]{2,1,0,4,3:T(2,128)(2,1)} %bitcast.89) | data formatting | bytes 3145728 | tf_op jit(solution)/shard_map/all_to_all | solution.py:75
  165.2 9.8 %all_to_all.29 = bf16[12,2,1024,32]{2,3,1,0:T(8,128)(2,1)} reshape(bf16[12,2,32,32,32]{3,2,4,1,0:T(8,128)(2,1)} %bitcast.90) | data formatting | bytes 3145728 | tf_op jit(solution)/shard_map/all_to_all | solution.py:75
  175.0 18.3 %fusion.26 = f32[12,2,32,1024]{3,2,1,0:T(8,128)S(1)} fusion(bf16[12,2,1024,32]{2,3,1,0:T(8,128)(2,1)} %all_to_all.29), kind=kOutput, calls=%fused_computation.35 | convolution fusion | flops 1627389952 | bytes 4718592 | tf_op jit(solution)/shard_map/sarv,ru->savu/dot_general | solution.py:77
  193.3 17.4 %fusion.34 = f32[12,2,32,1024]{3,2,1,0:T(8,128)S(1)} fusion(bf16[12,2,1024,32]{2,3,1,0:T(8,128)(2,1)S(1)} %copy-done.3), kind=kOutput, calls=%fused_computation.39 | convolution fusion | flops 1626341376 | bytes 4718592 | tf_op jit(solution)/shard_map/sarv,ru->savu/dot_general | solution.py:76
  212.1 16.4 %fusion.32 = f32[12,2,32,1024]{3,2,1,0:T(8,128)S(1)} fusion(f32[12,1,32,1024]{3,2,1,0:T(8,128)S(1)} %get-tuple-element.15, f32[12,1,32,1024]{3,2,1,0:T(8,128)S(1)} %get-tuple-element.14, f32[12,32,1024]{2,1,0:T(8,128)S(1)} %copy-done.2), kind=kOutput, calls=%fused_computation.38 | convolution fusion | flops 1628700672 | bytes 7864320 | tf_op jit(solution)/shard_map/savu,ur->savr/dot_general | solution.py:85
  228.5 16.7 %fusion.24 = f32[12,2,32,1024]{3,2,1,0:T(8,128)S(1)} fusion(f32[12,1,32,1024]{3,2,1,0:T(8,128)S(1)} %get-tuple-element.15, f32[12,1,32,1024]{3,2,1,0:T(8,128)S(1)} %get-tuple-element.14, f32[12,32,1024]{2,1,0:T(8,128)S(1)} %copy-done.2), kind=kOutput, calls=%fused_computation.34 | convolution fusion | flops 1629749248 | bytes 7864320 | tf_op jit(solution)/shard_map/savu,ur->savr/dot_general | solution.py:88
  247.2 15.1 %copy.47 = bf16[12,2,32,1024]{2,1,0,3:T(2,128)(2,1)} copy(bf16[12,2,32,1024]{3,2,1,0:T(8,128)(2,1)} %pad_maximum_fusion.2) | data formatting | bytes 3145728 | tf_op jit(solution)/shard_map/stack | solution.py:91
  262.3 14.2 %reshape.95 = bf16[32,2,12288]{2,1,0:T(2,128)(2,1)} reshape(bf16[1024,12,2,32]{3,2,1,0:T(2,128)(2,1)} %bitcast.94) | data formatting | bytes 3145728
  276.5 42.9 %all_to_all.36 = bf16[32,2,12288]{2,1,0:T(2,128)(2,1)} all-to-all(bf16[32,2,12288]{2,1,0:T(2,128)(2,1)} %reshape.95), channel_id=1, replica_groups=mesh['star'=8,'row'=32] {'row'}, dimensions={0} | all-to-all | bytes 3145728 | tf_op jit(solution)/shard_map/all_to_all | solution.py:95
  319.5 14.3 %reshape.96 = bf16[1024,12,2,32]{3,2,1,0:T(2,128)(2,1)} reshape(bf16[32,2,12288]{2,1,0:T(2,128)(2,1)} %all_to_all.36) | data formatting | bytes 3145728
  333.7 9.5 %copy.106 = bf16[12,2,32,32,32]{2,3,4,1,0:T(8,128)(2,1)} copy(bf16[12,2,32,32,32]{2,1,0,4,3:T(2,128)(2,1)} %bitcast.91) | data formatting | bytes 3145728 | tf_op jit(solution)/shard_map/all_to_all | solution.py:95
  343.2 9.8 %all_to_all.33 = bf16[12,2,1024,32]{2,3,1,0:T(8,128)(2,1)} reshape(bf16[12,2,32,32,32]{3,2,4,1,0:T(8,128)(2,1)} %bitcast.92) | data formatting | bytes 3145728 | tf_op jit(solution)/shard_map/all_to_all | solution.py:95
  353.0 18.3 %fusion.22 = f32[12,2,32,1024]{3,2,1,0:T(8,128)S(1)} fusion(bf16[12,2,1024,32]{2,3,1,0:T(8,128)(2,1)} %all_to_all.33), kind=kOutput, calls=%fused_computation.33 | convolution fusion | flops 1627389952 | bytes 4718592 | tf_op jit(solution)/shard_map/savr,vc->sarc/dot_general | solution.py:97
  371.3 17.0 %fusion.30 = f32[12,2,32,1024]{3,2,1,0:T(8,128)S(1)} fusion(bf16[12,2,1024,32]{2,3,1,0:T(8,128)(2,1)S(1)} %copy-done.4), kind=kOutput, calls=%fused_computation.37 | convolution fusion | flops 1626341376 | bytes 4718592 | tf_op jit(solution)/shard_map/savr,vc->sarc/dot_general | solution.py:96
  389.4 11.4 %fusion.19 = bf16[12,32,1024]{2,0,1:T(8,128)(2,1)S(1)} fusion(f32[12,1,32,1024]{3,2,1,0:T(8,128)S(1)} %get-tuple-element.24, f32[12,1,32,1024]{3,2,1,0:T(8,128)S(1)} %get-tuple-element.19, f32[12,1,32,1024]{3,2,1,0:T(8,128)S(1)} %get-tuple-element.25, f32[12,1,32,1024]{3,2,1,0:T(8,128)S(1)} %get-tuple-element.18, f32[12,32,1024]{2,0,1:T(8,128)S(1)} %fusion.3, ...), kind=kLoop, calls=%fused_computation.29 | loop fusion | flops 3538944 | bytes 8781872 | tf_op jit(solution)/shard_map/convert_element_type | solution.py:102
  413.6 78.1 %psum.7 = f32[64,64]{1,0:T(8,128)} all-reduce(f32[64,64]{1,0:T(8,128)S(1)} %fusion.57), channel_id=1, replica_groups=mesh['star'=8,'row'=32] {'star','row'}, use_global_device_ids=true, to_apply=%region_4.5 | all-reduce | flops 4096 | bytes 32768 | tf_op jit(solution)/shard_map/psum | solution.py:114
  (44 shorter events, 33.2 us)
Async XLA Ops:
  7.2 1.8 copy-start
  91.3 12.3 %copy-start.6 = (s32[8]{0:T(128)S(1)}, s32[8]{0:T(128)}, u32[]{:S(2)}) copy-start(s32[8]{0:T(128)} %param.8) | copy-start | bytes 100
  91.3 12.4 %copy-start.5 = (bf16[12,32,1024]{2,1,0:T(8,128)(2,1)S(1)}, bf16[12,32,1024]{2,1,0:T(8,128)(2,1)}, u32[]{:S(2)}) copy-start(bf16[12,32,1024]{2,1,0:T(8,128)(2,1)} %param.11) | copy-start | bytes 2359300
  91.3 50.2 %all-to-all-start = ((bf16[32,2,12288]{2,1,0:T(2,128)(2,1)}), bf16[32,2,12288]{2,1,0:T(2,128)(2,1)}, u32[]{:S(2)}, u32[]{:S(2)}) async-start(bf16[32,2,12288]{2,1,0:T(2,128)(2,1)} %reshape.93), calls=%async_computation | async-start | bytes 3145728 | tf_op jit(solution)/shard_map/all_to_all | solution.py:75
  103.6 388.1 %reduce-scatter.2.cloned.1.call-start = ((), (), s32[]{:S(2)}) async-start(), calls=%async_computation.3 | async-start | bytes 9437184 | tf_op jit(solution)/shard_map/reduce_scatter | solution.py:116
  175.0 18.3 %copy-start.3 = (bf16[12,2,1024,32]{2,3,1,0:T(8,128)(2,1)S(1)}, bf16[12,2,1024,32]{2,3,1,0:T(8,128)(2,1)}, u32[]{:S(2)}) copy-start(bf16[12,2,1024,32]{2,3,1,0:T(8,128)(2,1)} %all_to_all.29) | copy-start | bytes 4718596
  210.7 1.4 copy-start.2
  353.0 18.3 %copy-start.4 = (bf16[12,2,1024,32]{2,3,1,0:T(8,128)(2,1)S(1)}, bf16[12,2,1024,32]{2,3,1,0:T(8,128)(2,1)}, u32[]{:S(2)}) copy-start(bf16[12,2,1024,32]{2,3,1,0:T(8,128)(2,1)} %all_to_all.33) | copy-start | bytes 4718596
  406.5 88.0 %copy-start.1 = (bf16[64,64]{1,0:T(8,128)(2,1)S(1)}, bf16[64,64]{1,0:T(8,128)(2,1)}, u32[]{:S(2)}) copy-start(bf16[64,64]{1,0:T(8,128)(2,1)} %param.7) | copy-start | bytes 24580
Sparse Core Ops, SparseCore 0:
  406.6 54.6 reduce-scatter.1
where the time goes:
time: 509 us; the launch traced here: 502 us
  matrix products  158 us (31%)
  local copies, waits for them, and re-layouts  132 us (26%)
  blocking collectives  121 us (24%)
  waiting for transfers between devices  36.3 us (7%)
  other arithmetic  27.5 us (5%)
  between operations  14.7 us (3%)
  starting transfers between devices  12.3 us (2%)
    psum x1, blocking collectives, per_device(): coef_grad = lax.psum(coef_part, ('star', 'row'))  78.1 us
    unnamed x21, local copies, waits for them, and re-layouts  60.5 us
    all_to_all x1, blocking collectives, per_device(): lax.all_to_all(spectrum_grad, 'row', split_axis=3, concat_axis=2, tiled=T...  42.9 us
    all_to_all x1, waiting for transfers between devices, per_device(): lax.all_to_all(column_field, 'row', split_axis=3, concat_axis=2, tiled=True)  36.3 us
    all_to_all x2, local copies, waits for them, and re-layouts, per_device(): lax.all_to_all(spectrum_grad, 'row', split_axis=3, concat_axis=2, tiled=T...  19.3 us
    all_to_all x2, local copies, waits for them, and re-layouts, per_device(): lax.all_to_all(column_field, 'row', split_axis=3, concat_axis=2, tiled=True)  19.3 us
    dot_general x1, matrix products, per_device(): jnp.einsum('savr,vc->sarc', pieces, sin_table, preferred_element_type=jnp...  18.3 us
    dot_general x1, matrix products, per_device(): jnp.einsum('sarv,ru->savu', pieces, sin_table, preferred_element_type=jnp...  18.3 us
  transfers between devices with their start and end apart: 2, of which 1 were waited for; matrix products, arithmetic and copies ran while one was open for 2% of the time, Pallas kernels for 0%

commit v1 on v0

v1 whole, which is shorter than its diff:
```python
import jax
import jax.numpy as jnp
import numpy as np
from jax import lax
from jax.experimental import pallas as pl
from jax.experimental.pallas import tpu as pltpu
from jax.sharding import PartitionSpec as P

BF = jnp.bfloat16
F32 = jnp.float32
N = 1024
MAPS = 64
BLK = 32
GROUPS = 8
SLOT = 12
TOTAL = 32
MINE = 4
WAVES = [float(np.float32(2.0 * np.pi) / np.float32(0.55 + 0.35 * b / 7)) for b in range(8)]
TURNS = [float(1.0 / (0.55 + 0.35 * b / 7)) for b in range(8)]
VMEM_SPEC = pl.BlockSpec(memory_space=pltpu.VMEM)
SMEM_SPEC = pl.BlockSpec(memory_space=pltpu.SMEM)
ANY_SPEC = pl.BlockSpec(memory_space=pl.ANY)
NN = (((1,), (0,)), ((), ()))
NT = (((1,), (1,)), ((), ()))
TN = (((0,), (0,)), ((), ()))


def dot(a, b, dims=NN, precision=None):
    return lax.dot_general(a, b, dims, precision=precision, preferred_element_type=F32)


def iota(shape, axis):
    return lax.broadcasted_iota(jnp.int32, shape, axis)


def params(mib):
    return pltpu.CompilerParams(vmem_limit_bytes=mib << 20)


def table_seeds():
    b = np.arange(N, dtype=np.int64)
    low = (np.arange(32)[:, None] * b[None, :]) % N
    high = (32 * np.arange(32)[:, None] * b[None, :]) % N
    both = np.stack([low, high]) * (2.0 * np.pi / N)
    return np.stack([np.cos(both), -np.sin(both)], 1).astype(np.float32)


def fit_polynomials():
    x = 0.125 * (1.0 + np.cos(np.pi * (np.arange(4000) + 0.5) / 4000))
    f = np.sqrt(x)
    cheb = np.polynomial.chebyshev.Chebyshev
    poly = np.polynomial.polynomial.Polynomial
    c = cheb.fit(x, np.cos(2 * np.pi * f), 8, domain=[0, 0.25]).convert(kind=poly)
    s = cheb.fit(x, np.sin(2 * np.pi * f) / f, 8, domain=[0, 0.25]).convert(kind=poly)
    return [float(v) for v in c.coef], [float(v) for v in s.coef]


COS_POLY, SIN_POLY = fit_polynomials()


def cos_sin_turns(f):
    x = f * f
    c = jnp.full_like(f, COS_POLY[-1])
    s = jnp.full_like(f, SIN_POLY[-1])
    for k in range(len(COS_POLY) - 2, -1, -1):
        c = c * x + COS_POLY[k]
        s = s * x + SIN_POLY[k]
    return c, s * f


def my_bands(counts_ref, bands_ref, group):
    starts, total = [], jnp.int32(0)
    for g in range(GROUPS):
        starts.append(total)
        total = total + counts_ref[g]
    out = []
    for j in range(MINE):
        q = group * MINE + j
        owner, first = jnp.int32(0), jnp.int32(0)
        for g in range(1, GROUPS):
            here = q >= starts[g]
            owner = jnp.where(here, g, owner)
            first = jnp.where(here, starts[g], first)
        out.append(bands_ref[owner, q - first])
    return out


def pick(values, index):
    chosen = jnp.float32(values[0])
    for k in range(1, len(values)):
        chosen = jnp.where(index == k, jnp.float32(values[k]), chosen)
    return chosen


def aperture_mask(first_row, rows):
    centre = 0.5 * (N - 1)
    y = (first_row + iota((rows, N), 0)).astype(F32) - centre
    x = iota((rows, N), 1).astype(F32) - centre
    return y * y + x * x <= 0.25 * N * N


def pack_kernel(counts_ref, cells_ref, table_ref, psf_ref, packed_ref, coef_ref, hot_ref, held, in_sem, out_sem):
    me = lax.axis_index("star")
    load = pltpu.make_async_copy(psf_ref, held.at[pl.ds(0, SLOT)], in_sem)
    load.start()
    held[SLOT] = jnp.zeros((BLK, N), BF)
    row32 = iota((TOTAL, MAPS), 0)
    row64 = iota((2 * TOTAL, MAPS), 0)
    cell32 = jnp.full((TOTAL, MAPS), -1, jnp.int32)
    cell64 = jnp.full((2 * TOTAL, MAPS), -1, jnp.int32)
    total = jnp.int32(0)
    start = jnp.int32(0)
    for g in range(GROUPS):
        count = counts_ref[g]
        start = jnp.where(me == g, total, start)
        for j in range(SLOT):
            q = jnp.where(j < count, total + j, -1)
            cell = cells_ref[g, j]
            q64 = jnp.where(q < 0, -1, 2 * q - q % MINE)
            cell32 = jnp.where(row32 == q, cell, cell32)
            cell64 = jnp.where(row64 == q64, cell, cell64)
        total = total + count
    mine = counts_ref[me]
    hot32 = jnp.where(iota((TOTAL, MAPS), 1) == cell32, 1.0, 0.0).astype(BF)
    coef_ref[...] = dot(hot32, table_ref[...]).astype(BF)
    hot_ref[...] = jnp.where(iota((2 * TOTAL, MAPS), 1) == cell64, 1.0, 0.0)
    load.wait()
    copies = []
    for q in range(TOTAL):
        j = q - start
        source = jnp.where((j >= 0) & (j < mine), j, SLOT)
        copy = pltpu.make_async_copy(held.at[source], packed_ref.at[q], out_sem.at[q])
        copy.start()
        copies.append(copy)
    for copy in copies:
        copy.wait()


def pack(counts, cells, table, psf):
    return pl.pallas_call(
        pack_kernel,
        name="pack",
        out_shape=[
            jax.ShapeDtypeStruct((TOTAL, BLK, N), BF),
            jax.ShapeDtypeStruct((TOTAL, MAPS), BF),
            jax.ShapeDtypeStruct((2 * TOTAL, MAPS), F32),
        ],
        in_specs=[SMEM_SPEC, SMEM_SPEC, VMEM_SPEC, ANY_SPEC],
        out_specs=[ANY_SPEC, VMEM_SPEC, VMEM_SPEC],
        scratch_shapes=[
            pltpu.VMEM((SLOT + 1, BLK, N), BF),
            pltpu.SemaphoreType.DMA,
            pltpu.SemaphoreType.DMA((TOTAL,)),
        ],
        compiler_params=params(8),
    )(counts, cells, table, psf)


CHUNKS = 8


def pupil_kernel(
    counts_ref, bands_ref, coef_ref, seeds_ref, maps_ref, sent_ref, frac_ref, cos_ref, sin_ref,
    maps, spread, field, path, sem,
):
    group = lax.axis_index("star")
    depth = MAPS * BLK // CHUNKS
    loads = []
    for c in range(CHUNKS):
        rows = pl.ds(c * depth, depth)
        load = pltpu.make_async_copy(maps_ref.at[rows], maps.at[rows], sem.at[c])
        load.start()
        loads.append(load)
    mine = jnp.where(iota((MINE * BLK, TOTAL), 1) == group * MINE + iota((MINE * BLK, TOTAL), 0) // BLK, 1.0, 0.0)
    rows = dot(mine.astype(BF), coef_ref[...]).astype(BF)
    for c in range(CHUNKS):
        k = iota((MAPS, depth), 0)
        each = jnp.where(k == (c * depth + iota((MAPS, depth), 1)) // BLK, 1.0, 0.0).astype(BF)
        wide = dot(rows, each)
        same = iota(wide.shape, 0) % BLK == iota(wide.shape, 1) % BLK
        spread[:, c * depth : (c + 1) * depth] = jnp.where(same, wide, 0.0).astype(BF)

    def table_rows(a, carry):
        ca, sa = seeds_ref[1, 0, pl.ds(a, 1), :], seeds_ref[1, 1, pl.ds(a, 1), :]
        cb, sb = seeds_ref[0, 0], seeds_ref[0, 1]
        at = pl.ds(pl.multiple_of(a * 32, 32), 32)
        cos_ref[at, :] = (ca * cb - sa * sb).astype(BF)
        sin_ref[at, :] = (ca * sb + sa * cb).astype(BF)
        return carry

    lax.fori_loop(0, 32, table_rows, 0)
    for c in range(CHUNKS):
        loads[c].wait()
        part = dot(spread[:, c * depth : (c + 1) * depth], maps[c * depth : (c + 1) * depth, :])
        path[...] = part if c == 0 else path[...] + part
    bands = my_bands(counts_ref, bands_ref, group)
    first = lax.axis_index("row") * BLK
    for j in range(MINE):
        turn = pick(TURNS, bands[j])
        for h in range(BLK // 16):
            at = slice(j * BLK + h * 16, j * BLK + h * 16 + 16)
            t = path[at, :] * turn
            f = t - jnp.round(t)
            frac_ref[at, :] = f
            c, s = cos_sin_turns(f)
            inside = aperture_mask(first + h * 16, 16)
            field[at, :] = jnp.where(inside, c, 0.0).astype(BF)
            field[slice(at.start + 128, at.stop + 128), :] = jnp.where(inside, s, 0.0).astype(BF)
    for m in range(4):
        at = slice(m * 256, m * 256 + 256)
        by_cos = dot(cos_ref[at, :], field[...], NT)
        by_sin = dot(sin_ref[at, :], field[...], NT)
        sent_ref[at, :128] = (by_cos[:, :128] - by_sin[:, 128:]).astype(BF)
        sent_ref[at, 128:] = (by_sin[:, :128] + by_cos[:, 128:]).astype(BF)


def pupil(counts, bands, coef, seeds, maps):
    return pl.pallas_call(
        pupil_kernel,
        name="pupil",
        out_shape=[
            jax.ShapeDtypeStruct((N, 256), BF),
            jax.ShapeDtypeStruct((MINE * BLK, N), F32),
            jax.ShapeDtypeStruct((N, N), BF),
            jax.ShapeDtypeStruct((N, N), BF),
        ],
        in_specs=[SMEM_SPEC, SMEM_SPEC, VMEM_SPEC, VMEM_SPEC, ANY_SPEC],
        out_specs=[VMEM_SPEC] * 4,
        scratch_shapes=[
            pltpu.VMEM((MAPS * BLK, N), BF),
            pltpu.VMEM((MINE * BLK, MAPS * BLK), BF),
            pltpu.VMEM((256, N), BF),
            pltpu.VMEM((MINE * BLK, N), F32),
            pltpu.SemaphoreType.DMA((CHUNKS,)),
        ],
        compiler_params=params(32),
    )(counts, bands, coef, seeds, maps)


def gather_blocks(got_ref, out_ref):
    lane = iota((BLK, 128), 1)
    low = lane < 64
    even = lane % 64 < 32
    for part in range(2):
        for quad in range(8):
            x = [
                got_ref[(4 * quad + i) * BLK : (4 * quad + i + 1) * BLK, part * 128 : part * 128 + 128].astype(F32)
                for i in range(4)
            ]
            y = [None] * 4
            for i in range(2):
                y[i] = jnp.where(low, x[i], pltpu.roll(x[i + 2], 64, 1))
                y[i + 2] = jnp.where(low, pltpu.roll(x[i], 64, 1), x[i + 2])
            z = [None] * 4
            for i in (0, 2):
                z[i] = jnp.where(even, y[i], pltpu.roll(y[i + 1], 32, 1))
                z[i + 1] = jnp.where(even, pltpu.roll(y[i], 96, 1), y[i + 1])
            for s in range(4):
                at = part * 128 + s * BLK
                out_ref[at : at + BLK, quad * 128 : quad * 128 + 128] = z[s].astype(BF)


def focal_kernel(got_ref, cos_ref, sin_ref, cot_ref, sent_ref, field, grad):
    gather_blocks(got_ref, field)
    for n in range(4):
        at = slice(n * 256, n * 256 + 256)
        by_cos = dot(field[...], cos_ref[:, at])
        by_sin = dot(field[...], sin_ref[:, at])
        weight = cot_ref[:, at].astype(F32) * (2.0 / N)
        grad[:128, at] = (weight * (by_cos[:128] - by_sin[128:])).astype(BF)
        grad[128:, at] = (weight * (by_sin[:128] + by_cos[128:])).astype(BF)
    for m in range(4):
        at = slice(m * 256, m * 256 + 256)
        by_cos = dot(cos_ref[at, :], grad[...], NT)
        by_sin = dot(sin_ref[at, :], grad[...], NT)
        sent_ref[at, :128] = ((by_cos[:, :128] + by_sin[:, 128:]) * (1.0 / N)).astype(BF)
        sent_ref[at, 128:] = ((by_cos[:, 128:] - by_sin[:, :128]) * (1.0 / N)).astype(BF)


def focal(got, cos_table, sin_table, cot):
    return pl.pallas_call(
        focal_kernel,
        name="focal",
        out_shape=jax.ShapeDtypeStruct((N, 256), BF),
        in_specs=[VMEM_SPEC] * 4,
        out_specs=VMEM_SPEC,
        scratch_shapes=[pltpu.VMEM((256, N), BF), pltpu.VMEM((256, N), BF)],
        compiler_params=params(24),
    )(got, cos_table, sin_table, cot)


def back_kernel(
    counts_ref, bands_ref, got_ref, cos_ref, sin_ref, frac_ref, maps_ref, path_grad_ref, score_ref,
    maps, field, sem,
):
    group = lax.axis_index("star")
    load = pltpu.make_async_copy(maps_ref, maps, sem)
    load.start()
    gather_blocks(got_ref, field)
    bands = my_bands(counts_ref, bands_ref, group)
    first = lax.axis_index("row") * BLK
    inside = aperture_mask(first, BLK)
    waves = [pick(WAVES, b) for b in bands]
    for n in range(4):
        at = slice(n * 256, n * 256 + 256)
        by_cos = dot(field[...], cos_ref[:, at])
        by_sin = dot(field[...], sin_ref[:, at])
        real = by_cos[:128] + by_sin[128:]
        imag = by_cos[128:] - by_sin[:128]
        for j in range(MINE):
            rows = slice(j * BLK, j * BLK + BLK)
            c, s = cos_sin_turns(frac_ref[rows, at])
            grad = waves[j] * (c * imag[rows] - s * real[rows])
            path_grad_ref[rows, at] = jnp.where(inside[:, at], grad, 0.0).astype(BF)
    load.wait()
    parts = []
    for c in range(8):
        some = dot(maps[c * 256 : (c + 1) * 256, :], path_grad_ref[...], NT)
        same = iota(some.shape, 0) % BLK == iota(some.shape, 1) % BLK
        kept = jnp.where(same, some, 0.0)
        for k in range(8):
            parts.append(jnp.sum(kept[k * BLK : (k + 1) * BLK], axis=0, keepdims=True))
    by_lane = jnp.concatenate(parts, axis=0)
    pick_star = jnp.where(iota((8, 128), 1) // BLK == iota((8, 128), 0), 1.0, 0.0)
    scores = dot(pick_star, by_lane, NT, lax.Precision.HIGHEST)
    wide = jnp.concatenate([scores, jnp.zeros_like(scores)], axis=1)
    score_ref[...] = jnp.broadcast_to(wide[None], score_ref.shape)


def back(counts, bands, got, cos_table, sin_table, frac, maps):
    return pl.pallas_call(
        back_kernel,
        name="back",
        out_shape=[
            jax.ShapeDtypeStruct((MINE * BLK, N), BF),
            jax.ShapeDtypeStruct((32, 8, 128), F32),
        ],
        in_specs=[SMEM_SPEC, SMEM_SPEC, VMEM_SPEC, VMEM_SPEC, VMEM_SPEC, VMEM_SPEC, ANY_SPEC],
        out_specs=[VMEM_SPEC, VMEM_SPEC],
        scratch_shapes=[
            pltpu.VMEM((MAPS * BLK, N), BF),
            pltpu.VMEM((256, N), BF),
            pltpu.SemaphoreType.DMA,
        ],
        compiler_params=params(32),
    )(counts, bands, got, cos_table, sin_table, frac, maps)


def total_kernel(coef_ref, hot_ref, path_grad_ref, score_ref, map_grad_ref, coef_grad_ref):
    group = lax.axis_index("star")
    share = MAPS // GROUPS
    mine = jnp.where(iota((share * BLK, MAPS), 1) == group * share + iota((share * BLK, MAPS), 0) // BLK, 1.0, 0.0)
    rows = dot(mine.astype(BF), coef_ref[...], NT).astype(BF)
    each = jnp.where(iota((TOTAL, N), 0) == iota((TOTAL, N), 1) // BLK, 1.0, 0.0).astype(BF)
    wide = dot(rows, each)
    same = iota(wide.shape, 0) % BLK == iota(wide.shape, 1) % BLK
    spread = jnp.where(same, wide, 0.0).astype(BF)
    map_grad_ref[...] = dot(spread, path_grad_ref[...])
    scores = score_ref[...].reshape(64, 128)
    grad = dot(hot_ref[...], scores, TN, lax.Precision.HIGHEST) * (1.0 / (8 * N))
    coef_grad_ref[...] = grad[:, :MAPS]


def total(coef, hot, path_grads, scores):
    return pl.pallas_call(
        total_kernel,
        name="total",
        out_shape=[
            jax.ShapeDtypeStruct((MAPS // GROUPS * BLK, N), F32),
            jax.ShapeDtypeStruct((64, MAPS), F32),
        ],
        in_specs=[VMEM_SPEC] * 4,
        out_specs=[VMEM_SPEC, VMEM_SPEC],
        compiler_params=params(24),
    )(coef, hot, path_grads, scores)


def per_device(feature_maps, coef_table, star_counts, star_cells, star_bands, psf_cotangent):
    maps = feature_maps.reshape(MAPS * BLK, N)
    packed, coef, hot = pack(star_counts, star_cells, coef_table, psf_cotangent)
    cot = lax.psum_scatter(packed, "star", scatter_dimension=0, tiled=True).reshape(MINE * BLK, N)
    sent, frac, cos_table, sin_table = pupil(star_counts, star_bands, coef, jnp.asarray(table_seeds()), maps)
    got = lax.all_to_all(sent.reshape(32, BLK, 256), "row", 0, 0, tiled=True).reshape(N, 256)
    sent = focal(got, cos_table, sin_table, cot)
    got = lax.all_to_all(sent.reshape(32, BLK, 256), "row", 0, 0, tiled=True).reshape(N, 256)
    path_grad, score = back(star_counts, star_bands, got, cos_table, sin_table, frac, maps)
    path_grads = lax.all_gather(path_grad, "star", axis=0, tiled=True)
    score = lax.all_to_all(score, "row", 0, 0, tiled=True)
    score = jnp.broadcast_to(jnp.sum(score, 0)[None], (GROUPS, 8, 128))
    score = lax.all_to_all(score, "star", 0, 0, tiled=True)
    map_grad, coef_grad = total(coef, hot, path_grads, score)
    return map_grad.reshape(MAPS // GROUPS, BLK, N), coef_grad


def solution(mesh):
    placed = (P(None, "row", None), P(), P(), P(), P(), P("star", "row", None))
    return jax.shard_map(
        per_device,
        mesh=mesh,
        in_specs=placed,
        out_specs=(P("star", "row", None), P()),
        check_vma=False,
    )
```

time: 509 us -> 124 us (0.24); the launches traced: 502 us -> 124 us
  matrix products: 158 us -> 0 us
  local copies, waits for them, and re-layouts: 132 us -> 10.8 us
  blocking collectives: 121 us -> 80.1 us
  waiting for transfers between devices: 36.3 us -> 0.72 us
  other arithmetic: 27.5 us -> 0.04 us
  Pallas kernels: 0 us -> 17.8 us
  starting transfers between devices: 12.3 us -> 0.08 us
    dot_general x13 -> x0, matrix products: 158 us -> none  [the longest x1 18.3 us: per_device(): jnp.einsum('savr,vc->sarc', pieces, sin_table, preferred_element_type=jnp...]
    psum x1 -> x0, blocking collectives: 78.1 us -> none  [per_device(): coef_grad = lax.psum(coef_part, ('star', 'row'))]
    unnamed x21 -> x28, local copies, waits for them, and re-layouts: 60.5 us -> 10.8 us
    all_to_all x4 -> x0, local copies, waits for them, and re-layouts: 38.5 us -> none  [the longest x2 19.3 us: per_device(): lax.all_to_all(spectrum_grad, 'row', split_axis=3, concat_axis=2, tiled=T...]
    all_to_all x1 -> x4, blocking collectives: 42.9 us -> 80.1 us  [the longest x2 50.3 us: per_device(): lax.all_to_all(sent.reshape(32, BLK, 256), 'row', 0, 0, tiled=True)]
    all_to_all x1 -> x0, waiting for transfers between devices: 36.3 us -> none  [per_device(): lax.all_to_all(column_field, 'row', split_axis=3, concat_axis=2, tiled=True)]
    another operation x2 -> x0, local copies, waits for them, and re-layouts: 30.2 us -> none  [the longest x1 15.1 us: per_device(): jnp.stack([along_cos[:, 0] - along_sin[:, 1], along_sin[:, 0] + along_cos...]
    pallas_call x0 -> x5, Pallas kernels: none -> 17.8 us  [the longest x1 5.49 us: pupil(): pl.pallas_call(pupil_kernel, name='pupil', out_shape=[jax.ShapeDtypeStruc...]
  transfers between devices with their start and end apart: 2 -> 2, of which waited for: 1 -> 1; matrix products, arithmetic and copies ran while one was open for 2% -> 0% of each run, Pallas kernels for 0% -> 4%
where the time goes in v1:
time: 124 us
  blocking collectives  80.1 us (65%)
  Pallas kernels  17.8 us (14%)
  between operations  14.1 us (11%)
  local copies, waits for them, and re-layouts  10.8 us (9%)
    all_to_all x2, blocking collectives, per_device(): lax.all_to_all(sent.reshape(32, BLK, 256), 'row', 0, 0, tiled=True)  50.3 us
    all_to_all x1, blocking collectives, per_device(): score = lax.all_to_all(score, 'row', 0, 0, tiled=True)  15.4 us
    all_to_all x1, blocking collectives, per_device(): score = lax.all_to_all(score, 'star', 0, 0, tiled=True)  14.4 us
    unnamed x28, local copies, waits for them, and re-layouts  10.8 us
    pallas_call x1, Pallas kernels, pupil(): pl.pallas_call(pupil_kernel, name='pupil', out_shape=[jax.ShapeDtypeStruc...  5.49 us
    pallas_call x1, Pallas kernels, back(): pl.pallas_call(back_kernel, name='back', out_shape=[jax.ShapeDtypeStruct(...  4.66 us
    pallas_call x1, Pallas kernels, pack(): pl.pallas_call(pack_kernel, name='pack', out_shape=[jax.ShapeDtypeStruct(...  2.93 us
    pallas_call x1, Pallas kernels, focal(): pl.pallas_call(focal_kernel, name='focal', out_shape=jax.ShapeDtypeStruct...  2.83 us
  transfers between devices with their start and end apart: 2, of which 1 were waited for; matrix products, arithmetic and copies ran while one was open for 0% of the time, Pallas kernels for 4%

profile of v1, /device:TPU:1, one launch (start us, length us, event | category | flops | bytes accessed | tf_op | source)
XLA Modules:
  0.0 123.7 jit_solution(4771754739670637370)
XLA Ops:
  7.2 0.0 reduce-scatter.2.cloned.1.call-start
  7.2 1.1 copy-done.6
  8.3 0.7 copy-done.9
  9.1 0.7 copy-done.11
  9.7 0.7 copy-done.13
  10.4 2.9 %pack.1 = (bf16[32,32,1024]{2,1,0:T(8,128)(2,1)}, bf16[32,64]{1,0:T(8,128)(2,1)S(1)}, f32[64,64]{1,0:T(8,128)S(1)}) custom-call(s32[8]{0:T(128)S(1)} %copy-done.11, s32[8,12]{1,0:T(8,128)S(1)} %copy-done.13, bf16[64,64]{1,0:T(8,128)(2,1)S(1)} %copy-done.9, bf16[12,32,1024]{2,1,0:T(8,128)(2,1)S(1)} %copy-done.6), custom_call_target="tpu_custom_call" | custom-call | tf_op jit(solution)/shard_map/pack/pallas_call | solution.py:140
  13.4 0.0 reduce-scatter.2.cloned.1.call-update
  13.4 0.0 all-gather.2.cloned.1.call-start
  13.5 0.0 copy-start
  13.5 2.2 %copy-done = bf16[64,32,1024]{2,1,0:T(8,128)(2,1)S(1)} copy-done((bf16[64,32,1024]{2,1,0:T(8,128)(2,1)S(1)}, bf16[64,32,1024]{2,1,0:T(8,128)(2,1)}, u32[]{:S(2)}) %copy-start) | copy-done | bytes 4194328
  15.6 5.5 %pupil.1 = (bf16[1024,256]{1,0:T(8,128)(2,1)S(1)}, f32[128,1024]{1,0:T(8,128)S(1)}, bf16[1024,1024]{1,0:T(8,128)(2,1)S(1)}, bf16[1024,1024]{1,0:T(8,128)(2,1)S(1)}) custom-call(s32[8]{0:T(128)S(1)} %copy-done.12, s32[8,12]{1,0:T(8,128)S(1)} %copy-done.10, bf16[32,64]{1,0:T(8,128)(2,1)S(1)} %get-tuple-element.13.coef_ref, f32[2,2,32,1024]{3,2,1,0:T(8,128)S(1)} %copy-done.7, ...), custom_call_target="tpu_custom_call" | custom-call | tf_op jit(solution)/shard_map/pupil/pallas_call | solution.py:218
  21.2 1.3 %copy-done.2 = bf16[1024,1024]{1,0:T(8,128)(2,1)} copy-done((bf16[1024,1024]{1,0:T(8,128)(2,1)}, bf16[1024,1024]{1,0:T(8,128)(2,1)S(1)}, u32[]{:S(2)}) %copy-start.2) | copy-done | bytes 2097176
  22.5 28.0 %all_to_all.20 = bf16[32,32,256]{2,1,0:T(8,128)(2,1)S(1)} all-to-all(bf16[32,32,256]{2,1,0:T(8,128)(2,1)S(1)} %bitcast.12), channel_id=1, replica_groups=mesh['star'=8,'row'=32] {'row'}, dimensions={0} | all-to-all | bytes 1048576 | tf_op jit(solution)/shard_map/all_to_all | solution.py:383
  50.4 0.7 reduce-scatter.2.cloned.1.call-done
  51.1 1.6 %copy-done.3 = bf16[1024,1024]{1,0:T(8,128)(2,1)S(1)} copy-done((bf16[1024,1024]{1,0:T(8,128)(2,1)S(1)}, bf16[1024,1024]{1,0:T(8,128)(2,1)}, u32[]{:S(2)}) %copy-start.3) | copy-done | bytes 2097176
  52.7 0.9 copy-done.8
  53.7 2.8 %focal.1 = bf16[1024,256]{1,0:T(8,128)(2,1)S(1)} custom-call(bf16[1024,256]{1,0:T(8,128)(2,1)S(1)} %bitcast.10, bf16[1024,1024]{1,0:T(8,128)(2,1)S(1)} %get-tuple-element.16.cos_ref, bf16[1024,1024]{1,0:T(8,128)(2,1)S(1)} %copy-done.3, bf16[128,1024]{1,0:T(8,128)(2,1)S(1)} %bitcast.13), custom_call_target="tpu_custom_call" | custom-call | tf_op jit(solution)/shard_map/focal/pallas_call | solution.py:281
  56.5 22.3 %all_to_all.21 = bf16[32,32,256]{2,1,0:T(8,128)(2,1)S(1)} all-to-all(bf16[32,32,256]{2,1,0:T(8,128)(2,1)S(1)} %bitcast.11), channel_id=1, replica_groups=mesh['star'=8,'row'=32] {'row'}, dimensions={0} | all-to-all | bytes 1048576 | tf_op jit(solution)/shard_map/all_to_all | solution.py:385
  78.8 4.7 %back.1 = (bf16[128,1024]{1,0:T(8,128)(2,1)}, f32[32,8,128]{2,1,0:T(8,128)S(1)}) custom-call(s32[8]{0:T(128)S(1)} %copy-done.12, s32[8,12]{1,0:T(8,128)S(1)} %copy-done.10, bf16[1024,256]{1,0:T(8,128)(2,1)S(1)} %bitcast.9, bf16[1024,1024]{1,0:T(8,128)(2,1)S(1)} %get-tuple-element.16.cos_ref, bf16[1024,1024]{1,0:T(8,128)(2,1)S(1)} %copy-done.4, ...), custom_call_target="tpu_custom_call" | custom-call | tf_op jit(solution)/shard_map/back/pallas_call | solution.py:331
  83.5 0.0 all-gather.2.cloned.1.call-update
  83.5 15.4 %all_to_all.22 = f32[32,8,128]{2,1,0:T(8,128)S(1)} all-to-all(f32[32,8,128]{2,1,0:T(8,128)S(1)} %get-tuple-element.21), channel_id=1, replica_groups=mesh['star'=8,'row'=32] {'row'}, dimensions={0} | all-to-all | bytes 262144 | tf_op jit(solution)/shard_map/all_to_all | solution.py:388
  99.0 14.4 %all_to_all.23.score_ref = f32[8,8,128]{2,1,0:T(8,128)S(1)} all-to-all(f32[8,8,128]{2,1,0:T(8,128)S(1)} %broadcast_in_dim.2), channel_id=1, replica_groups=mesh['star'=8,'row'=32] {'star'}, dimensions={0} | all-to-all | bytes 65536 | tf_op jit(solution)/shard_map/all_to_all | solution.py:390
  113.4 1.6 %copy-done.5 = bf16[1024,1024]{1,0:T(8,128)(2,1)S(1)} copy-done((bf16[1024,1024]{1,0:T(8,128)(2,1)S(1)}, bf16[1024,1024]{1,0:T(8,128)(2,1)}, u32[]{:S(2)}) %copy-start.5) | copy-done | bytes 2097176
  115.0 1.9 %total.1 = (f32[256,1024]{1,0:T(8,128)}, f32[64,64]{1,0:T(8,128)}) custom-call(bf16[32,64]{1,0:T(8,128)(2,1)S(1)} %get-tuple-element.13.coef_ref, f32[64,64]{1,0:T(8,128)S(1)} %get-tuple-element.14.hot_ref, bf16[1024,1024]{1,0:T(8,128)(2,1)S(1)} %copy-done.5, f32[8,8,128]{2,1,0:T(8,128)S(1)} %all_to_all.23.score_ref), custom_call_target="tpu_custom_call" | custom-call | tf_op jit(solution)/shard_map/total/pallas_call | solution.py:365
  (21 shorter events, 0.1 us)
Async XLA Ops:
  7.2 44.0 %reduce-scatter.2.cloned.1.call-start = ((), (), s32[]{:S(2)}) async-start(), calls=%async_computation.5 | async-start | bytes 2359296 | tf_op jit(solution)/shard_map/reduce_scatter | solution.py:381
  7.2 1.1 copy-start.6
  8.3 0.7 copy-start.9
  9.1 0.7 copy-start.11
  9.7 0.7 copy-start.13
  10.4 3.0 %copy-start.7 = (f32[2,2,32,1024]{3,2,1,0:T(8,128)S(1)}, f32[2,2,32,1024]{3,2,1,0:T(8,128)}, u32[]{:S(2)}) copy-start(f32[2,2,32,1024]{3,2,1,0:T(8,128)} %constant.4.clone.seeds_ref) | copy-start | bytes 1572868
  10.4 3.0 %copy-start.10 = (s32[8,12]{1,0:T(8,128)S(1)}, s32[8,12]{1,0:T(8,128)}, u32[]{:S(2)}) copy-start(s32[8,12]{1,0:T(8,128)} %bands_ref.3) | copy-start | bytes 1156
  10.4 3.0 %copy-start.12 = (s32[8]{0:T(128)S(1)}, s32[8]{0:T(128)}, u32[]{:S(2)}) copy-start(s32[8]{0:T(128)} %counts_ref.5) | copy-start | bytes 100
  13.4 100.0 %all-gather.2.cloned.1.call-start = ((), (), s32[]{:S(2)}) async-start(), calls=%async_computation.6 | async-start | bytes 2359296 | tf_op jit(solution)/shard_map/all_gather | solution.py:387
  13.5 2.2 %copy-start = (bf16[64,32,1024]{2,1,0:T(8,128)(2,1)S(1)}, bf16[64,32,1024]{2,1,0:T(8,128)(2,1)}, u32[]{:S(2)}) copy-start(bf16[64,32,1024]{2,1,0:T(8,128)(2,1)} %param.7) | copy-start | bytes 12582916
  21.1 1.3 %copy-start.2 = (bf16[1024,1024]{1,0:T(8,128)(2,1)}, bf16[1024,1024]{1,0:T(8,128)(2,1)S(1)}, u32[]{:S(2)}) copy-start(bf16[1024,1024]{1,0:T(8,128)(2,1)S(1)} %get-tuple-element.17.sin_ref) | copy-start | bytes 6291460
  51.1 1.6 %copy-start.3 = (bf16[1024,1024]{1,0:T(8,128)(2,1)S(1)}, bf16[1024,1024]{1,0:T(8,128)(2,1)}, u32[]{:S(2)}) copy-start(bf16[1024,1024]{1,0:T(8,128)(2,1)} %copy-done.2) | copy-start | bytes 6291460
  52.7 0.9 copy-start.8
  53.7 25.1 %copy-start.1 = (bf16[64,32,1024]{2,1,0:T(8,128)(2,1)S(1)}, bf16[64,32,1024]{2,1,0:T(8,128)(2,1)}, u32[]{:S(2)}) copy-start(bf16[64,32,1024]{2,1,0:T(8,128)(2,1)} %param.7) | copy-start | bytes 12582916
  53.7 25.1 %copy-start.4 = (bf16[1024,1024]{1,0:T(8,128)(2,1)S(1)}, bf16[1024,1024]{1,0:T(8,128)(2,1)}, u32[]{:S(2)}) copy-start(bf16[1024,1024]{1,0:T(8,128)(2,1)} %copy-done.2) | copy-start | bytes 6291460
  113.4 1.6 %copy-start.5 = (bf16[1024,1024]{1,0:T(8,128)(2,1)S(1)}, bf16[1024,1024]{1,0:T(8,128)(2,1)}, u32[]{:S(2)}) copy-start(bf16[1024,1024]{1,0:T(8,128)(2,1)} %all-gather.2.cloned.1.call-done.path_grad_ref) | copy-start | bytes 6291460
Sparse Core Ops, SparseCore 0:
  13.5 37.5 reduce-scatter.1
  83.6 29.1 all-gather.1

commit v2 on v1

v2 whole, which is shorter than its diff:
```python
import jax
import jax.numpy as jnp
import numpy as np
from jax import lax
from jax.experimental import pallas as pl
from jax.experimental.pallas import tpu as pltpu
from jax.sharding import PartitionSpec as P

BF = jnp.bfloat16
F32 = jnp.float32
N = 1024
MAPS = 64
BLK = 32
GROUPS = 8
SLOT = 12
TOTAL = 32
MINE = 4
WAVES = [float(np.float32(2.0 * np.pi) / np.float32(0.55 + 0.35 * b / 7)) for b in range(8)]
TURNS = [float(1.0 / (0.55 + 0.35 * b / 7)) for b in range(8)]
VMEM_SPEC = pl.BlockSpec(memory_space=pltpu.VMEM)
SMEM_SPEC = pl.BlockSpec(memory_space=pltpu.SMEM)
HBM_SPEC = pl.BlockSpec(memory_space=pltpu.HBM)
ANY_SPEC = pl.BlockSpec(memory_space=pl.ANY)
NN = (((1,), (0,)), ((), ()))
NT = (((1,), (1,)), ((), ()))
TN = (((0,), (0,)), ((), ()))


def dot(a, b, dims=NN, precision=None):
    return lax.dot_general(a, b, dims, precision=precision, preferred_element_type=F32)


def iota(shape, axis):
    return lax.broadcasted_iota(jnp.int32, shape, axis)


def in_hbm(*arrays):
    return [pltpu.with_memory_space_constraint(a, pltpu.HBM) for a in arrays]


def params(mib):
    return pltpu.CompilerParams(vmem_limit_bytes=mib << 20)


def table_seeds():
    b = np.arange(N, dtype=np.int64)
    low = (np.arange(32)[:, None] * b[None, :]) % N
    high = (32 * (np.arange(32) % 16)[:, None] * b[None, :]) % N
    both = np.stack([low, high]) * (2.0 * np.pi / N)
    return np.stack([np.cos(both), -np.sin(both)], 1).astype(np.float32)


def fit_polynomials():
    x = 0.125 * (1.0 + np.cos(np.pi * (np.arange(4000) + 0.5) / 4000))
    f = np.sqrt(x)
    cheb = np.polynomial.chebyshev.Chebyshev
    poly = np.polynomial.polynomial.Polynomial
    c = cheb.fit(x, np.cos(2 * np.pi * f), 7, domain=[0, 0.25]).convert(kind=poly)
    s = cheb.fit(x, np.sin(2 * np.pi * f) / f, 6, domain=[0, 0.25]).convert(kind=poly)
    return [float(v) for v in c.coef], [float(v) for v in s.coef]


COS_POLY, SIN_POLY = fit_polynomials()


def cos_sin_turns(f):
    x = f * f
    c = jnp.full_like(f, COS_POLY[-1])
    s = jnp.full_like(f, SIN_POLY[-1])
    for a in COS_POLY[-2::-1]:
        c = c * x + a
    for a in SIN_POLY[-2::-1]:
        s = s * x + a
    return c, s * f


def assigned(h, t, counts):
    before, count, free = jnp.zeros_like(h), jnp.zeros_like(h), jnp.int32(0)
    for g in range(GROUPS):
        before = jnp.where(h == g, free, before)
        count = jnp.where(h == g, counts[g], count)
        free = free + jnp.maximum(MINE - counts[g], 0)
    e = before + t - count
    slot, first = jnp.zeros_like(h), jnp.int32(0)
    for g in range(GROUPS):
        after = first + jnp.maximum(counts[g] - MINE, 0)
        slot = jnp.where((e >= first) & (e < after), g * SLOT + MINE + e - first, slot)
        first = after
    return jnp.where(t < count, h * SLOT + t, slot)


def pick(values, index):
    chosen = jnp.float32(values[0])
    for k in range(1, len(values)):
        chosen = jnp.where(index == k, jnp.float32(values[k]), chosen)
    return chosen


def aperture_mask(first_row, rows):
    centre = 0.5 * (N - 1)
    y = (first_row + iota((rows, N), 0)).astype(F32) - centre
    x = iota((rows, N), 1).astype(F32) - centre
    return y * y + x * x <= 0.25 * N * N


def alternate(x):
    return x * jnp.where((iota((1, x.shape[1]), 1) & 1) == 0, 1.0, -1.0)


def same_pixel(shape):
    return ((iota(shape, 0) ^ iota(shape, 1)) & (BLK - 1)) == 0


def times_table(field, table, at):
    upper = dot(field[:, : N // 2], table[:, at])
    lower = dot(field[:, N // 2 :], table[:, at])
    return upper + alternate(lower)


def table_times(tables, both, at):
    return dot(tables[0, at, :], both[...], NT), dot(tables[1, at, :], both[...], NT)


CHUNKS = 2


def pupil_kernel(
    counts_hbm, cells_hbm, bands_hbm, table_hbm, seeds_hbm, maps_hbm,
    sent_hbm, frac_hbm, tables, hot_ref, coef_ref, meta_ref,
    counts_ref, cells_ref, bands_ref, table, seeds, maps, spread, field, path, sent_ref, frac_ref, sem, out_sem,
):
    group = lax.axis_index("star")
    depth = MAPS * BLK // CHUNKS
    small = [
        pltpu.make_async_copy(a, b, sem.at[CHUNKS + i])
        for i, (a, b) in enumerate(
            [(seeds_hbm, seeds), (counts_hbm, counts_ref), (cells_hbm, cells_ref), (bands_hbm, bands_ref), (table_hbm, table)]
        )
    ]
    for copy in small:
        copy.start()
    loads = []
    for c in range(CHUNKS):
        rows = pl.ds(c * depth, depth)
        load = pltpu.make_async_copy(maps_hbm.at[rows], maps.at[rows], sem.at[c])
        load.start()
        loads.append(load)
    small[0].wait()
    cb, sb = seeds[0, 0], seeds[0, 1]
    for a in range(16):
        ca, sa = seeds[1, 0, a : a + 1, :], seeds[1, 1, a : a + 1, :]
        tables[0, a * 32 : a * 32 + 32, :] = (ca * cb - sa * sb).astype(BF)
        tables[1, a * 32 : a * 32 + 32, :] = (ca * sb + sa * cb).astype(BF)
    for copy in small[1:]:
        copy.wait()
    counts = [counts_ref[g] for g in range(GROUPS)]
    place = iota((64, MAPS), 0)
    slots = jnp.where((place & 7) < MINE, assigned(place >> 3, place & 7, counts), -1)
    cell = jnp.full((64, MAPS), -1, jnp.int32)
    for g in range(GROUPS):
        for j in range(SLOT):
            cell = jnp.where(slots == g * SLOT + j, cells_ref[g, j], cell)
    hot = jnp.where(iota((64, MAPS), 1) == cell, 1.0, 0.0)
    hot_ref[...] = hot
    coef_ref[...] = dot(hot.astype(BF), table[...]).astype(BF)
    turns = []
    for t in range(MINE):
        slot = assigned(group, jnp.int32(t), counts)
        band = bands_ref[slot // SLOT, slot % SLOT]
        meta_ref[t] = slot
        meta_ref[MINE + t] = band
        turns.append(pick(TURNS, band))
    for k in range(1, 4):
        other = (group + 2 * k) & 7
        for t in range(1, MINE):
            slot = assigned(other, jnp.int32(t), counts)
            meta_ref[2 * MINE + 3 * (k - 1) + t - 1] = jnp.where((slot // SLOT) >> 1 == group >> 1, slot, -1)
    mine = jnp.where(iota((128, 64), 1) == group * 8 + (iota((128, 64), 0) >> 5), 1.0, 0.0)
    rows = dot(mine.astype(BF), coef_ref[...]).astype(BF)
    same = same_pixel((128, depth))
    k = iota((MAPS, depth), 0)
    for c in range(CHUNKS):
        each = jnp.where(k == c * (MAPS // CHUNKS) + (iota((MAPS, depth), 1) >> 5), 1.0, 0.0).astype(BF)
        wide = dot(rows, each)
        spread[:, c * depth : (c + 1) * depth] = jnp.where(same, wide, 0.0).astype(BF)
    for c in range(CHUNKS):
        loads[c].wait()
        part = dot(spread[:, c * depth : (c + 1) * depth], maps[c * depth : (c + 1) * depth, :])
        path[...] = part if c == 0 else path[...] + part
    first = lax.axis_index("row") * BLK
    for h in range(BLK // 16):
        inside = aperture_mask(first + h * 16, 16)
        for t in range(MINE):
            at = slice(t * BLK + h * 16, t * BLK + h * 16 + 16)
            x = path[at, :] * turns[t]
            f = x - jnp.round(x)
            frac_ref[at, :] = f
            c, s = cos_sin_turns(f)
            for part, value in enumerate((c, s)):
                value = jnp.where(inside, value, 0.0)
                field[slice(at.start + part * 128, at.stop + part * 128), :] = value.astype(BF)
                field[slice(at.start + part * 128 + 256, at.stop + part * 128 + 256), :] = alternate(value).astype(BF)
    stores = [pltpu.make_async_copy(frac_ref, frac_hbm, out_sem.at[4])]
    stores[0].start()
    for m in range(2):
        by_cos, by_sin = table_times(tables, field, slice(m * 256, m * 256 + 256))
        for half in range(2):
            at = slice(half * 512 + m * 256, half * 512 + m * 256 + 256)
            re, im = slice(half * 256, half * 256 + 128), slice(half * 256 + 128, half * 256 + 256)
            sent_ref[at, :128] = (by_cos[:, re] - by_sin[:, im]).astype(BF)
            sent_ref[at, 128:] = (by_sin[:, re] + by_cos[:, im]).astype(BF)
            stores.append(pltpu.make_async_copy(sent_ref.at[at], sent_hbm.at[at], out_sem.at[2 * m + half]))
            stores[-1].start()
    for store in stores:
        store.wait()


def pupil(counts, cells, bands, table, seeds, maps):
    return pl.pallas_call(
        pupil_kernel,
        name="pupil",
        out_shape=[
            pltpu.HBM((N, 256), BF),
            pltpu.HBM((MINE * BLK, N), F32),
            jax.ShapeDtypeStruct((2, N // 2, N), BF),
            jax.ShapeDtypeStruct((64, MAPS), F32),
            jax.ShapeDtypeStruct((64, MAPS), BF),
            jax.ShapeDtypeStruct((2 * MINE + 9,), jnp.int32),
        ],
        in_specs=[HBM_SPEC] * 6,
        out_specs=[HBM_SPEC] * 2 + [VMEM_SPEC] * 3 + [SMEM_SPEC],
        scratch_shapes=[
            pltpu.SMEM((GROUPS,), jnp.int32),
            pltpu.SMEM((GROUPS, SLOT), jnp.int32),
            pltpu.SMEM((GROUPS, SLOT), jnp.int32),
            pltpu.VMEM((64, MAPS), BF),
            pltpu.VMEM((2, 2, 32, N), F32),
            pltpu.VMEM((MAPS * BLK, N), BF),
            pltpu.VMEM((MINE * BLK, MAPS * BLK), BF),
            pltpu.VMEM((512, N), BF),
            pltpu.VMEM((MINE * BLK, N), F32),
            pltpu.VMEM((N, 256), BF),
            pltpu.VMEM((MINE * BLK, N), F32),
            pltpu.SemaphoreType.DMA((CHUNKS + 5,)),
            pltpu.SemaphoreType.DMA((5,)),
        ],
        compiler_params=params(20),
    )(*in_hbm(counts, cells, bands, table, seeds, maps))


def gather_blocks(got_ref, out_ref):
    lane = iota((BLK, 128), 1)
    low = lane < 64
    even = (lane & 63) < 32
    for part in range(2):
        for quad in range(8):
            x = [
                got_ref[(4 * quad + i) * BLK : (4 * quad + i + 1) * BLK, part * 128 : part * 128 + 128].astype(F32)
                for i in range(4)
            ]
            y = [None] * 4
            for i in range(2):
                y[i] = jnp.where(low, x[i], pltpu.roll(x[i + 2], 64, 1))
                y[i + 2] = jnp.where(low, pltpu.roll(x[i], 64, 1), x[i + 2])
            z = [None] * 4
            for i in (0, 2):
                z[i] = jnp.where(even, y[i], pltpu.roll(y[i + 1], 32, 1))
                z[i + 1] = jnp.where(even, pltpu.roll(y[i], 96, 1), y[i + 1])
            for s in range(4):
                at = part * 128 + s * BLK
                out_ref[at : at + BLK, quad * 128 : quad * 128 + 128] = z[s].astype(BF)


def pack_kernel(meta_ref, own_hbm, twin_hbm, one_hbm, two_hbm, three_hbm, sem):
    group = lax.axis_index("star")
    sent = (one_hbm, two_hbm, three_hbm)
    for i in range(9):
        slot = meta_ref[2 * MINE + i]
        place = jnp.maximum(slot, 0) % SLOT
        mine = slot // SLOT == group

        @pl.when((slot >= 0) & mine)
        def _():
            pltpu.make_async_copy(own_hbm.at[place], sent[i // 3].at[i % 3], sem.at[i]).start()

        @pl.when((slot >= 0) & jnp.logical_not(mine))
        def _():
            pltpu.make_async_copy(twin_hbm.at[place], sent[i // 3].at[i % 3], sem.at[i]).start()

    for i in range(9):

        @pl.when(meta_ref[2 * MINE + i] >= 0)
        def _():
            pltpu.make_async_copy(own_hbm.at[0], sent[i // 3].at[i % 3], sem.at[i]).wait()


def pack(meta, own, twin):
    return pl.pallas_call(
        pack_kernel,
        name="pack",
        out_shape=[pltpu.HBM((3, BLK, N), BF)] * 3,
        in_specs=[SMEM_SPEC, HBM_SPEC, ANY_SPEC],
        out_specs=[HBM_SPEC] * 3,
        scratch_shapes=[pltpu.SemaphoreType.DMA((9,))],
        compiler_params=params(4),
    )(meta, *in_hbm(own), twin)


def focal_kernel(
    meta_ref, got_ref, tables, own_hbm, twin_hbm, one_hbm, two_hbm, three_hbm, sent_ref, cot, field, grad, sem
):
    group = lax.axis_index("star")
    for t in range(MINE):
        slot = meta_ref[t]
        owner = slot // SLOT
        place = slot % SLOT
        hop = ((group >> 1) - (owner >> 1)) & 3

        @pl.when((hop == 0) & (owner == group))
        def _():
            pltpu.make_async_copy(own_hbm.at[place], cot.at[t], sem.at[t]).start()

        @pl.when((hop == 0) & (owner != group))
        def _():
            pltpu.make_async_copy(twin_hbm.at[place], cot.at[t], sem.at[t]).start()

        for k, got in ((1, one_hbm), (2, two_hbm), (3, three_hbm)):

            @pl.when(hop == k)
            def _():
                pltpu.make_async_copy(got.at[max(t - 1, 0)], cot.at[t], sem.at[t]).start()

    gather_blocks(got_ref, field)
    for n in range(4):
        at = slice(n * 256, n * 256 + 256)
        by_cos = times_table(field, tables.at[0], at)
        by_sin = times_table(field, tables.at[1], at)
        if n == 0:
            for t in range(MINE):
                pltpu.make_async_copy(own_hbm.at[t], cot.at[t], sem.at[t]).wait()
        weight = cot[:, :, at].reshape(128, 256).astype(F32) * (2.0 / N)
        for part, value in enumerate((by_cos[:128] - by_sin[128:], by_sin[:128] + by_cos[128:])):
            value = weight * value
            grad[slice(part * 128, part * 128 + 128), at] = value.astype(BF)
            grad[slice(part * 128 + 256, part * 128 + 384), at] = alternate(value).astype(BF)
    for m in range(2):
        by_cos, by_sin = table_times(tables, grad, slice(m * 256, m * 256 + 256))
        for half in range(2):
            at = slice(half * 512 + m * 256, half * 512 + m * 256 + 256)
            re, im = slice(half * 256, half * 256 + 128), slice(half * 256 + 128, half * 256 + 256)
            sent_ref[at, :128] = ((by_cos[:, re] + by_sin[:, im]) * (1.0 / N)).astype(BF)
            sent_ref[at, 128:] = ((by_cos[:, im] - by_sin[:, re]) * (1.0 / N)).astype(BF)


def focal(meta, got, tables, own, twin, moved):
    return pl.pallas_call(
        focal_kernel,
        name="focal",
        out_shape=jax.ShapeDtypeStruct((N, 256), BF),
        in_specs=[SMEM_SPEC, VMEM_SPEC, VMEM_SPEC] + [HBM_SPEC] * 5,
        out_specs=VMEM_SPEC,
        scratch_shapes=[
            pltpu.VMEM((MINE, BLK, N), BF),
            pltpu.VMEM((256, N), BF),
            pltpu.VMEM((512, N), BF),
            pltpu.SemaphoreType.DMA((MINE,)),
        ],
        compiler_params=params(16),
    )(meta, got, tables, *in_hbm(own, twin, *moved))


def back_kernel(meta_ref, got_ref, tables, frac_hbm, path_grad_hbm, path_grad_ref, frac_ref, field, sem, in_sem):
    load = pltpu.make_async_copy(frac_hbm, frac_ref, in_sem)
    load.start()
    gather_blocks(got_ref, field)
    waves = [pick(WAVES, meta_ref[MINE + t]) for t in range(MINE)]
    inside = aperture_mask(lax.axis_index("row") * BLK, BLK)
    copies = []
    for n in range(4):
        at = slice(n * 256, n * 256 + 256)
        by_cos = times_table(field, tables.at[0], at)
        by_sin = times_table(field, tables.at[1], at)
        real = by_cos[:128] + by_sin[128:]
        imag = by_cos[128:] - by_sin[:128]
        if n == 0:
            load.wait()
        for t in range(MINE):
            rows = slice(t * BLK, t * BLK + BLK)
            c, s = cos_sin_turns(frac_ref[rows, at])
            grad = waves[t] * (c * imag[rows] - s * real[rows])
            path_grad_ref[rows, at] = jnp.where(inside[:, at], grad, 0.0).astype(BF)
        copy = pltpu.make_async_copy(path_grad_ref.at[:, at], path_grad_hbm.at[:, at], sem.at[n])
        copy.start()
        copies.append(copy)
    for copy in copies:
        copy.wait()


def back(meta, got, tables, frac):
    return pl.pallas_call(
        back_kernel,
        name="back",
        out_shape=[pltpu.HBM((MINE * BLK, N), BF), jax.ShapeDtypeStruct((MINE * BLK, N), BF)],
        in_specs=[SMEM_SPEC, VMEM_SPEC, VMEM_SPEC, HBM_SPEC],
        out_specs=[HBM_SPEC, VMEM_SPEC],
        scratch_shapes=[
            pltpu.VMEM((MINE * BLK, N), F32),
            pltpu.VMEM((256, N), BF),
            pltpu.SemaphoreType.DMA((4,)),
            pltpu.SemaphoreType.DMA,
        ],
        compiler_params=params(16),
    )(meta, got, tables, *in_hbm(frac))


def score_kernel(path_grad_ref, maps_hbm, score_ref, maps_ref, sem):
    loads = []
    for c in range(2):
        rows = pl.ds(c * 1024, 1024)
        loads.append(pltpu.make_async_copy(maps_hbm.at[rows], maps_ref.at[rows], sem.at[c]))
        loads[-1].start()
    parts = []
    same = same_pixel((256, 128))
    for c in range(8):
        if c % 4 == 0:
            loads[c // 4].wait()
        some = dot(maps_ref[c * 256 : (c + 1) * 256, :], path_grad_ref[...], NT)
        kept = jnp.where(same, some, 0.0)
        for k in range(8):
            parts.append(jnp.sum(kept[k * BLK : (k + 1) * BLK], axis=0, keepdims=True))
    by_lane = jnp.concatenate(parts, axis=0)
    pick_star = jnp.where((iota((8, 128), 1) >> 5) == iota((8, 128), 0), 1.0, 0.0)
    scores = dot(pick_star, by_lane, NT, lax.Precision.HIGHEST)
    wide = jnp.concatenate([scores, jnp.zeros_like(scores)], axis=1)
    score_ref[...] = jnp.broadcast_to(wide[None], score_ref.shape)


def score_of(path_grad, maps):
    return pl.pallas_call(
        score_kernel,
        name="score",
        out_shape=jax.ShapeDtypeStruct((32, 8, 128), F32),
        in_specs=[VMEM_SPEC, HBM_SPEC],
        out_specs=VMEM_SPEC,
        scratch_shapes=[pltpu.VMEM((MAPS * BLK, N), BF), pltpu.SemaphoreType.DMA((2,))],
        compiler_params=params(16),
    )(path_grad, *in_hbm(maps))


def total_kernel(coef_ref, hot_ref, path_grad_hbm, score_ref, map_grad_hbm, coef_grad_ref, path_grad, map_grad, in_sem, out_sem):
    group = lax.axis_index("star")
    loads = []
    for n in range(2):
        at = pl.ds(n * 512, 512)
        load = pltpu.make_async_copy(path_grad_hbm.at[at], path_grad.at[at], in_sem.at[n])
        load.start()
        loads.append(load)
    share = MAPS // GROUPS
    mine = jnp.where(iota((share * BLK, MAPS), 1) == group * share + (iota((share * BLK, MAPS), 0) >> 5), 1.0, 0.0)
    rows = dot(mine.astype(BF), coef_ref[...], NT).astype(BF)
    q = iota((64, N), 1) >> 5
    each = jnp.where(iota((64, N), 0) == ((q >> 2) << 3) + (q & 3), 1.0, 0.0).astype(BF)
    wide = dot(rows, each)
    spread = jnp.where(same_pixel(wide.shape), wide, 0.0).astype(BF)
    stores = []
    for n in range(2):
        loads[n].wait()
        some = slice(n * 512, n * 512 + 512)
        for m in range(2):
            at = slice(m * 128, m * 128 + 128)
            part = dot(spread[at, some], path_grad[some, :])
            map_grad[at, :] = part if n == 0 else map_grad[at, :] + part
            if n == 1:
                store = pltpu.make_async_copy(map_grad.at[at], map_grad_hbm.at[at], out_sem.at[m])
                store.start()
                stores.append(store)
    scores = score_ref[...].reshape(64, 128)
    grad = dot(hot_ref[...], scores, TN, lax.Precision.HIGHEST) * (1.0 / (8 * N))
    coef_grad_ref[...] = grad[:, :MAPS]
    for store in stores:
        store.wait()


def total(coef, hot, path_grads, scores):
    rows = MAPS // GROUPS * BLK
    return pl.pallas_call(
        total_kernel,
        name="total",
        out_shape=[pltpu.HBM((rows, N), F32), jax.ShapeDtypeStruct((64, MAPS), F32)],
        in_specs=[VMEM_SPEC, VMEM_SPEC, HBM_SPEC, VMEM_SPEC],
        out_specs=[HBM_SPEC, VMEM_SPEC],
        scratch_shapes=[
            pltpu.VMEM((N, N), BF),
            pltpu.VMEM((rows, N), F32),
            pltpu.SemaphoreType.DMA((2,)),
            pltpu.SemaphoreType.DMA((2,)),
        ],
        compiler_params=params(16),
    )(coef, hot, *in_hbm(path_grads), scores)


def per_device(feature_maps, coef_table, star_counts, star_cells, star_bands, psf_cotangent):
    maps = feature_maps.reshape(MAPS * BLK, N)
    twin = lax.ppermute(psf_cotangent, "star", [(g, g ^ 1) for g in range(GROUPS)])
    sent, frac, tables, hot, coef, meta = pupil(
        star_counts, star_cells, star_bands, coef_table, jnp.asarray(table_seeds()), maps
    )
    sent, *packed = lax.optimization_barrier((sent, *pack(meta, psf_cotangent, twin)))
    moved = [
        lax.ppermute(packed[k - 1], "star", [(g, (g + 2 * k) % GROUPS) for g in range(GROUPS)]) for k in (1, 2, 3)
    ]
    got = lax.all_to_all(sent.reshape(32, BLK, 256), "row", 0, 0, tiled=True).reshape(N, 256)
    sent = focal(meta, got, tables, psf_cotangent, twin, moved)
    got = lax.all_to_all(sent.reshape(32, BLK, 256), "row", 0, 0, tiled=True).reshape(N, 256)
    path_grad, held = back(meta, got, tables, frac)
    path_grads = lax.all_gather(path_grad, "star", axis=0, tiled=True)
    score = lax.all_to_all(score_of(held, maps), "row", 0, 0, tiled=True)
    score = jnp.broadcast_to(jnp.sum(score, 0)[None], (GROUPS, 8, 128))
    score = lax.all_to_all(score, "star", 0, 0, tiled=True)
    map_grad, coef_grad = total(coef, hot, path_grads, score)
    return map_grad.reshape(MAPS // GROUPS, BLK, N), coef_grad


def solution(mesh):
    placed = (P(None, "row", None), P(), P(), P(), P(), P("star", "row", None))
    return jax.shard_map(
        per_device,
        mesh=mesh,
        in_specs=placed,
        out_specs=(P("star", "row", None), P()),
        check_vma=False,
    )
```

time: 124 us -> 114 us (0.919)
  blocking collectives: 80.1 us -> 44.5 us
  starting transfers between devices: 0.08 us -> 15.6 us
  Pallas kernels: 17.8 us -> 30.6 us
  local copies, waits for them, and re-layouts: 10.8 us -> 1.37 us
  waiting for transfers between devices: 0.72 us -> 8.53 us
    all_to_all x2 -> x1, blocking collectives: 50.3 us -> 19.5 us  [per_device(): lax.all_to_all(sent.reshape(32, BLK, 256), 'row', 0, 0, tiled=True)]
    pallas_call x4 -> x5, Pallas kernels: 15 us -> 26.5 us  [the longest x1 9.7 us: pack(): pl.pallas_call(pack_kernel, name='pack', out_shape=[pltpu.HBM((3, BLK, N)...]
    all_to_all x0 -> x1, starting transfers between devices: none -> 9.48 us  [per_device(): lax.all_to_all(sent.reshape(32, BLK, 256), 'row', 0, 0, tiled=True)]
    unnamed x28 -> x6, local copies, waits for them, and re-layouts: 10.8 us -> 1.36 us
    ppermute x0 -> x4, starting transfers between devices: none -> 6.07 us  [the longest x1 3.33 us: per_device(): lax.ppermute(psf_cotangent, 'star', [(g, g ^ 1) for g in range(GROUPS)])]
    ppermute x0 -> x4, waiting for transfers between devices: none -> 5.38 us  [the longest x3 5.37 us: per_device(): lax.ppermute(packed[k - 1], 'star', [(g, (g + 2 * k) % GROUPS) for g in r...]
    all_to_all x0 -> x1, waiting for transfers between devices: none -> 3.14 us  [per_device(): lax.all_to_all(sent.reshape(32, BLK, 256), 'row', 0, 0, tiled=True)]
    all_to_all x1, blocking collectives: 15.4 us -> 12.9 us  [per_device(): score = lax.all_to_all(score_of(held, maps), 'row', 0, 0, tiled=True)]
  transfers between devices with their start and end apart: 2 -> 6, of which waited for: 1 -> 2; matrix products, arithmetic and copies ran while one was open for 0% -> 0% of each run, Pallas kernels for 4% -> 8%
where the time goes in v2:
time: 114 us; the launch traced here: 115 us
  blocking collectives  44.5 us (39%)
  Pallas kernels  30.6 us (27%)
  starting transfers between devices  15.6 us (14%)
  between operations  14.1 us (12%)
  waiting for transfers between devices  8.53 us (7%)
  local copies, waits for them, and re-layouts  1.37 us (1%)
    all_to_all x1, blocking collectives, per_device(): lax.all_to_all(sent.reshape(32, BLK, 256), 'row', 0, 0, tiled=True)  19.5 us
    all_to_all x1, blocking collectives, per_device(): score = lax.all_to_all(score_of(held, maps), 'row', 0, 0, tiled=True)  12.9 us
    all_to_all x1, blocking collectives, per_device(): score = lax.all_to_all(score, 'star', 0, 0, tiled=True)  12.1 us
    pallas_call x1, Pallas kernels, pack(): pl.pallas_call(pack_kernel, name='pack', out_shape=[pltpu.HBM((3, BLK, N)...  9.7 us
    all_to_all x1, starting transfers between devices, per_device(): lax.all_to_all(sent.reshape(32, BLK, 256), 'row', 0, 0, tiled=True)  9.48 us
    pallas_call x1, Pallas kernels, pupil(): pl.pallas_call(pupil_kernel, name='pupil', out_shape=[pltpu.HBM((N, 256),...  6.28 us
    ppermute x3, waiting for transfers between devices, per_device(): lax.ppermute(packed[k - 1], 'star', [(g, (g + 2 * k) % GROUPS) for g in r...  5.37 us
    pallas_call x1, Pallas kernels, focal(): pl.pallas_call(focal_kernel, name='focal', out_shape=jax.ShapeDtypeStruct...  4.08 us
  transfers between devices with their start and end apart: 6, of which 2 were waited for; matrix products, arithmetic and copies ran while one was open for 0% of the time, Pallas kernels for 8%

profile of v2, /device:TPU:1, one launch (start us, length us, event | category | flops | bytes accessed | tf_op | source)
XLA Modules:
  0.0 114.8 jit_solution(7483919628936939647)
XLA Ops:
  7.2 3.3 %collective-permute-start = (bf16[12,32,1024]{2,1,0:T(8,128)(2,1)}, bf16[12,32,1024]{2,1,0:T(8,128)(2,1)S(1)}, u32[]{:S(2)}, u32[]{:S(2)}) collective-permute-start(bf16[12,32,1024]{2,1,0:T(8,128)(2,1)} %own_hbm.3), channel_id=1, source_target_pairs={{0,32},{32,0},{64,96},{96,64},{128,160},{160,128},{192,224},{224,1... | collective-permute-start | bytes 2359304 | tf_op jit(solution)/shard_map/ppermute | solution.py:504
  10.5 6.3 %pupil.1 = (bf16[1024,256]{1,0:T(8,128)(2,1)}, f32[128,1024]{1,0:T(8,128)}, bf16[2,512,1024]{2,1,0:T(8,128)(2,1)S(1)}, f32[64,64]{1,0:T(8,128)S(1)}, bf16[64,64]{1,0:T(8,128)(2,1)S(1)}, /*index=5*/s32[17]{0:T(128)S(1)}) custom-call(s32[8]{0:T(128)} %counts_hbm.1, s32[8,12]{1,0:T(8,128)} %cells_hbm.1, s32[8,12]{1,0:T(8,128)} %bands_hbm.1, ...), custom_call_target="tpu_custom_call" | custom-call | tf_op jit(solution)/shard_map/pupil/pallas_call | solution.py:219
  16.8 0.0 collective-permute-done.twin_hbm
  16.8 0.0 copy-start
  16.8 9.7 %pack.1 = (bf16[3,32,1024]{2,1,0:T(8,128)(2,1)}, bf16[3,32,1024]{2,1,0:T(8,128)(2,1)}, bf16[3,32,1024]{2,1,0:T(8,128)(2,1)}) custom-call(s32[17]{0:T(128)S(1)} %get-tuple-element.21.meta_ref, bf16[12,32,1024]{2,1,0:T(8,128)(2,1)} %own_hbm.3, bf16[12,32,1024]{2,1,0:T(8,128)(2,1)S(1)} %collective-permute-done.twin_hbm), custom_call_target="tpu_custom_call" | custom-call | tf_op jit(solution)/shard_map/pack/pallas_call | solution.py:298
  26.5 9.5 %all-to-all-start = ((bf16[32,32,256]{2,1,0:T(8,128)(2,1)}), bf16[32,32,256]{2,1,0:T(8,128)(2,1)S(1)}, u32[]{:S(2)}, u32[]{:S(2)}) async-start(bf16[32,32,256]{2,1,0:T(8,128)(2,1)} %bitcast.11), calls=%async_computation | async-start | bytes 1048576 | tf_op jit(solution)/shard_map/all_to_all | solution.py:512
  36.0 0.0 all-gather.2.cloned.1.call-start
  36.1 0.1 collective-permute-start.1
  36.1 0.1 collective-permute-start.2
  36.2 2.6 %collective-permute-start.3 = (bf16[3,32,1024]{2,1,0:T(8,128)(2,1)}, bf16[3,32,1024]{2,1,0:T(8,128)(2,1)}, u32[]{:S(2)}, u32[]{:S(2)}) collective-permute-start(bf16[3,32,1024]{2,1,0:T(8,128)(2,1)} %get-tuple-element.30), channel_id=1, source_target_pairs={{0,192},{32,224},{64,0},{96,32},{128,64},{160,96},{192,128},{224,1... | collective-permute-start | bytes 589832 | tf_op jit(solution)/shard_map/ppermute | solution.py:510
  38.8 5.4 %collective-permute-done.1.one_hbm = bf16[3,32,1024]{2,1,0:T(8,128)(2,1)S(1)} collective-permute-done((bf16[3,32,1024]{2,1,0:T(8,128)(2,1)}, bf16[3,32,1024]{2,1,0:T(8,128)(2,1)S(1)}, u32[]{:S(2)}, u32[]{:S(2)}) %collective-permute-start.1) | collective-permute-done | bytes 196640 | tf_op jit(solution)/shard_map/ppermute | solution.py:510
  44.2 0.0 collective-permute-done.2.two_hbm
  44.2 0.7 copy-done.1
  44.9 0.7 copy-done.2
  45.5 0.0 collective-permute-done.3.three_hbm
  45.5 3.1 %all-to-all-done = bf16[32,32,256]{2,1,0:T(8,128)(2,1)S(1)} async-done(((bf16[32,32,256]{2,1,0:T(8,128)(2,1)}), bf16[32,32,256]{2,1,0:T(8,128)(2,1)S(1)}, u32[]{:S(2)}, u32[]{:S(2)}) %all-to-all-start) | async-done | bytes 524320 | tf_op jit(solution)/shard_map/all_to_all | solution.py:512
  48.7 4.1 %focal.1 = bf16[1024,256]{1,0:T(8,128)(2,1)S(1)} custom-call(s32[17]{0:T(128)S(1)} %get-tuple-element.21.meta_ref, bf16[1024,256]{1,0:T(8,128)(2,1)S(1)} %bitcast.7, bf16[2,512,1024]{2,1,0:T(8,128)(2,1)S(1)} %get-tuple-element.27.tables, bf16[12,32,1024]{2,1,0:T(8,128)(2,1)} %own_hbm.3, bf16[12,32,1024]{2,1,0:T(8,128)(2,1)} %copy-done, ...), custom_call_target="tpu_custom_call" | custom-call | tf_op jit(solution)/shard_map/focal/pallas_call | solution.py:356
  52.8 19.5 %all_to_all.20 = bf16[32,32,256]{2,1,0:T(8,128)(2,1)S(1)} all-to-all(bf16[32,32,256]{2,1,0:T(8,128)(2,1)S(1)} %bitcast.8), channel_id=1, replica_groups=mesh['star'=8,'row'=32] {'row'}, dimensions={0} | all-to-all | bytes 1048576 | tf_op jit(solution)/shard_map/all_to_all | solution.py:514
  72.3 3.6 %back.1 = (bf16[128,1024]{1,0:T(8,128)(2,1)}, bf16[128,1024]{1,0:T(8,128)(2,1)S(1)}) custom-call(s32[17]{0:T(128)S(1)} %get-tuple-element.21.meta_ref, bf16[1024,256]{1,0:T(8,128)(2,1)S(1)} %bitcast.6, bf16[2,512,1024]{2,1,0:T(8,128)(2,1)S(1)} %get-tuple-element.27.tables, f32[128,1024]{1,0:T(8,128)} %get-tuple-element.31.frac_hbm), custom_call_target="tpu_custom_call" | custom-call | tf_op jit(solution)/shard_map/back/pallas_call | solution.py:400
  75.9 0.0 all-gather.2.cloned.1.call-update
  75.9 3.3 %score.1 = f32[32,8,128]{2,1,0:T(8,128)S(1)} custom-call(bf16[128,1024]{1,0:T(8,128)(2,1)S(1)} %get-tuple-element.33.path_grad_ref, bf16[2048,1024]{1,0:T(8,128)(2,1)} %bitcast.10), custom_call_target="tpu_custom_call" | custom-call | tf_op jit(solution)/shard_map/score/pallas_call | solution.py:439
  79.2 12.9 %all_to_all.21 = f32[32,8,128]{2,1,0:T(8,128)S(1)} all-to-all(f32[32,8,128]{2,1,0:T(8,128)S(1)} %score.1), channel_id=1, replica_groups=mesh['star'=8,'row'=32] {'row'}, dimensions={0} | all-to-all | bytes 262144 | tf_op jit(solution)/shard_map/all_to_all | solution.py:517
  92.2 12.1 %all_to_all.22.score_ref = f32[8,8,128]{2,1,0:T(8,128)S(1)} all-to-all(f32[8,8,128]{2,1,0:T(8,128)S(1)} %broadcast_in_dim.2), channel_id=1, replica_groups=mesh['star'=8,'row'=32] {'star'}, dimensions={0} | all-to-all | bytes 65536 | tf_op jit(solution)/shard_map/all_to_all | solution.py:519
  104.3 3.6 %total.1 = (f32[256,1024]{1,0:T(8,128)}, f32[64,64]{1,0:T(8,128)}) custom-call(bf16[64,64]{1,0:T(8,128)(2,1)S(1)} %get-tuple-element.19.coef_ref, f32[64,64]{1,0:T(8,128)S(1)} %get-tuple-element.20.hot_ref, bf16[1024,1024]{1,0:T(8,128)(2,1)} %all-gather.2.cloned.1.call-done.path_grad_hbm, f32[8,8,128]{2,1,0:T(8,128)S(1)} %all_to_all.22.score_ref), custom_call_target="tpu_custom_call" | custom-call | tf_op jit(solution)/shard_map/total/pallas_call | solution.py:486
  (6 shorter events, 0.0 us)
Async XLA Ops:
  7.2 9.6 %collective-permute-start = (bf16[12,32,1024]{2,1,0:T(8,128)(2,1)}, bf16[12,32,1024]{2,1,0:T(8,128)(2,1)S(1)}, u32[]{:S(2)}, u32[]{:S(2)}) collective-permute-start(bf16[12,32,1024]{2,1,0:T(8,128)(2,1)} %own_hbm.3), channel_id=1, source_target_pairs={{0,32},{32,0},{64,96},{96,64},{128,160},{160,128},{192,224},{224,1... | collective-permute-start | bytes 2359304 | tf_op jit(solution)/shard_map/ppermute | solution.py:504
  16.8 31.9 %copy-start = (bf16[12,32,1024]{2,1,0:T(8,128)(2,1)}, bf16[12,32,1024]{2,1,0:T(8,128)(2,1)S(1)}, u32[]{:S(2)}) copy-start(bf16[12,32,1024]{2,1,0:T(8,128)(2,1)S(1)} %collective-permute-done.twin_hbm) | copy-start | bytes 2359300
  26.5 22.2 %all-to-all-start = ((bf16[32,32,256]{2,1,0:T(8,128)(2,1)}), bf16[32,32,256]{2,1,0:T(8,128)(2,1)S(1)}, u32[]{:S(2)}, u32[]{:S(2)}) async-start(bf16[32,32,256]{2,1,0:T(8,128)(2,1)} %bitcast.11), calls=%async_computation | async-start | bytes 1048576 | tf_op jit(solution)/shard_map/all_to_all | solution.py:512
  36.0 68.3 %all-gather.2.cloned.1.call-start = ((), (), s32[]{:S(2)}) async-start(), calls=%async_computation.4 | async-start | bytes 2359296 | tf_op jit(solution)/shard_map/all_gather | solution.py:516
  36.1 8.1 %collective-permute-start.1 = (bf16[3,32,1024]{2,1,0:T(8,128)(2,1)}, bf16[3,32,1024]{2,1,0:T(8,128)(2,1)S(1)}, u32[]{:S(2)}, u32[]{:S(2)}) collective-permute-start(bf16[3,32,1024]{2,1,0:T(8,128)(2,1)} %get-tuple-element.28), channel_id=1, source_target_pairs={{0,64},{32,96},{64,128},{96,160},{128,192},{160,224},{192,0},{224,... | collective-permute-start | bytes 589832 | tf_op jit(solution)/shard_map/ppermute | solution.py:510
  36.1 8.0 %collective-permute-start.2 = (bf16[3,32,1024]{2,1,0:T(8,128)(2,1)}, bf16[3,32,1024]{2,1,0:T(8,128)(2,1)S(1)}, u32[]{:S(2)}, u32[]{:S(2)}) collective-permute-start(bf16[3,32,1024]{2,1,0:T(8,128)(2,1)} %get-tuple-element.29), channel_id=1, source_target_pairs={{0,128},{32,160},{64,192},{96,224},{128,0},{160,32},{192,64},{224,... | collective-permute-start | bytes 589832 | tf_op jit(solution)/shard_map/ppermute | solution.py:510
  36.2 9.3 %collective-permute-start.3 = (bf16[3,32,1024]{2,1,0:T(8,128)(2,1)}, bf16[3,32,1024]{2,1,0:T(8,128)(2,1)}, u32[]{:S(2)}, u32[]{:S(2)}) collective-permute-start(bf16[3,32,1024]{2,1,0:T(8,128)(2,1)} %get-tuple-element.30), channel_id=1, source_target_pairs={{0,192},{32,224},{64,0},{96,32},{128,64},{160,96},{192,128},{224,1... | collective-permute-start | bytes 589832 | tf_op jit(solution)/shard_map/ppermute | solution.py:510
  44.2 0.7 copy-start.1
  44.9 0.7 copy-start.2
Sparse Core Ops, SparseCore 0:
  76.0 24.2 all-gather.1

commit v3 on v2

--- a/solution.py
+++ b/solution.py
@@ -369,13 +369,12 @@
     )(meta, got, tables, *in_hbm(own, twin, *moved))
 
 
-def back_kernel(meta_ref, got_ref, tables, frac_hbm, path_grad_hbm, path_grad_ref, frac_ref, field, sem, in_sem):
+def back_kernel(meta_ref, got_ref, tables, frac_hbm, path_grad_ref, frac_ref, field, in_sem):
     load = pltpu.make_async_copy(frac_hbm, frac_ref, in_sem)
     load.start()
     gather_blocks(got_ref, field)
     waves = [pick(WAVES, meta_ref[MINE + t]) for t in range(MINE)]
     inside = aperture_mask(lax.axis_index("row") * BLK, BLK)
-    copies = []
     for n in range(4):
         at = slice(n * 256, n * 256 + 256)
         by_cos = times_table(field, tables.at[0], at)
@@ -389,24 +388,18 @@
             c, s = cos_sin_turns(frac_ref[rows, at])
             grad = waves[t] * (c * imag[rows] - s * real[rows])
             path_grad_ref[rows, at] = jnp.where(inside[:, at], grad, 0.0).astype(BF)
-        copy = pltpu.make_async_copy(path_grad_ref.at[:, at], path_grad_hbm.at[:, at], sem.at[n])
-        copy.start()
-        copies.append(copy)
-    for copy in copies:
-        copy.wait()
 
 
 def back(meta, got, tables, frac):
     return pl.pallas_call(
         back_kernel,
         name="back",
-        out_shape=[pltpu.HBM((MINE * BLK, N), BF), jax.ShapeDtypeStruct((MINE * BLK, N), BF)],
+        out_shape=jax.ShapeDtypeStruct((MINE * BLK, N), BF),
         in_specs=[SMEM_SPEC, VMEM_SPEC, VMEM_SPEC, HBM_SPEC],
-        out_specs=[HBM_SPEC, VMEM_SPEC],
+        out_specs=VMEM_SPEC,
         scratch_shapes=[
             pltpu.VMEM((MINE * BLK, N), F32),
             pltpu.VMEM((256, N), BF),
-            pltpu.SemaphoreType.DMA((4,)),
             pltpu.SemaphoreType.DMA,
         ],
         compiler_params=params(16),
@@ -447,14 +440,13 @@
     )(path_grad, *in_hbm(maps))
 
 
-def total_kernel(coef_ref, hot_ref, path_grad_hbm, score_ref, map_grad_hbm, coef_grad_ref, path_grad, map_grad, in_sem, out_sem):
+def total_kernel(coef_ref, hot_ref, score_ref, *refs):
+    blocks = refs[: 2 * MINE]
+    map_grad_hbm, coef_grad_ref, path_grad, map_grad, out_sem = refs[2 * MINE :]
     group = lax.axis_index("star")
-    loads = []
-    for n in range(2):
-        at = pl.ds(n * 512, 512)
-        load = pltpu.make_async_copy(path_grad_hbm.at[at], path_grad.at[at], in_sem.at[n])
-        load.start()
-        loads.append(load)
+    for i, block in enumerate(blocks):
+        h = (group ^ (i // MINE)) - 2 * (i % MINE) & (GROUPS - 1)
+        path_grad[pl.ds(pl.multiple_of(h * 128, 128), 128), :] = block[...]
     share = MAPS // GROUPS
     mine = jnp.where(iota((share * BLK, MAPS), 1) == group * share + (iota((share * BLK, MAPS), 0) >> 5), 1.0, 0.0)
     rows = dot(mine.astype(BF), coef_ref[...], NT).astype(BF)
@@ -463,17 +455,12 @@
     wide = dot(rows, each)
     spread = jnp.where(same_pixel(wide.shape), wide, 0.0).astype(BF)
     stores = []
-    for n in range(2):
-        loads[n].wait()
-        some = slice(n * 512, n * 512 + 512)
-        for m in range(2):
-            at = slice(m * 128, m * 128 + 128)
-            part = dot(spread[at, some], path_grad[some, :])
-            map_grad[at, :] = part if n == 0 else map_grad[at, :] + part
-            if n == 1:
-                store = pltpu.make_async_copy(map_grad.at[at], map_grad_hbm.at[at], out_sem.at[m])
-                store.start()
-                stores.append(store)
+    for m in range(2):
+        at = slice(m * 128, m * 128 + 128)
+        map_grad[at, :] = dot(spread[at], path_grad[...])
+        store = pltpu.make_async_copy(map_grad.at[at], map_grad_hbm.at[at], out_sem.at[m])
+        store.start()
+        stores.append(store)
     scores = score_ref[...].reshape(64, 128)
     grad = dot(hot_ref[...], scores, TN, lax.Precision.HIGHEST) * (1.0 / (8 * N))
     coef_grad_ref[...] = grad[:, :MAPS]
@@ -481,43 +468,50 @@
         store.wait()
 
 
-def total(coef, hot, path_grads, scores):
+def total(coef, hot, scores, blocks):
     rows = MAPS // GROUPS * BLK
     return pl.pallas_call(
         total_kernel,
         name="total",
         out_shape=[pltpu.HBM((rows, N), F32), jax.ShapeDtypeStruct((64, MAPS), F32)],
-        in_specs=[VMEM_SPEC, VMEM_SPEC, HBM_SPEC, VMEM_SPEC],
+        in_specs=[VMEM_SPEC] * 11,
         out_specs=[HBM_SPEC, VMEM_SPEC],
         scratch_shapes=[
             pltpu.VMEM((N, N), BF),
             pltpu.VMEM((rows, N), F32),
             pltpu.SemaphoreType.DMA((2,)),
-            pltpu.SemaphoreType.DMA((2,)),
         ],
         compiler_params=params(16),
-    )(coef, hot, *in_hbm(path_grads), scores)
+    )(coef, hot, scores, *blocks)
+
+
+def swap_cores(x):
+    return lax.ppermute(x, "star", [(g, g ^ 1) for g in range(GROUPS)])
+
+
+def along_x(x, k):
+    return lax.ppermute(x, "star", [(g, (g + 2 * k) % GROUPS) for g in range(GROUPS)])
 
 
 def per_device(feature_maps, coef_table, star_counts, star_cells, star_bands, psf_cotangent):
     maps = feature_maps.reshape(MAPS * BLK, N)
-    twin = lax.ppermute(psf_cotangent, "star", [(g, g ^ 1) for g in range(GROUPS)])
+    twin = swap_cores(psf_cotangent)
     sent, frac, tables, hot, coef, meta = pupil(
         star_counts, star_cells, star_bands, coef_table, jnp.asarray(table_seeds()), maps
     )
     sent, *packed = lax.optimization_barrier((sent, *pack(meta, psf_cotangent, twin)))
-    moved = [
-        lax.ppermute(packed[k - 1], "star", [(g, (g + 2 * k) % GROUPS) for g in range(GROUPS)]) for k in (1, 2, 3)
-    ]
+    moved = [along_x(packed[k - 1], k) for k in (1, 2, 3)]
     got = lax.all_to_all(sent.reshape(32, BLK, 256), "row", 0, 0, tiled=True).reshape(N, 256)
     sent = focal(meta, got, tables, psf_cotangent, twin, moved)
     got = lax.all_to_all(sent.reshape(32, BLK, 256), "row", 0, 0, tiled=True).reshape(N, 256)
-    path_grad, held = back(meta, got, tables, frac)
-    path_grads = lax.all_gather(path_grad, "star", axis=0, tiled=True)
-    score = lax.all_to_all(score_of(held, maps), "row", 0, 0, tiled=True)
+    path_grad = back(meta, got, tables, frac)
+    blocks = [path_grad] + [along_x(path_grad, k) for k in (1, 2, 3)]
+    score = lax.all_to_all(score_of(path_grad, maps), "row", 0, 0, tiled=True)
+    score, *blocks = lax.optimization_barrier((score, *blocks))
+    blocks = blocks + [swap_cores(block) for block in blocks]
     score = jnp.broadcast_to(jnp.sum(score, 0)[None], (GROUPS, 8, 128))
     score = lax.all_to_all(score, "star", 0, 0, tiled=True)
-    map_grad, coef_grad = total(coef, hot, path_grads, score)
+    map_grad, coef_grad = total(coef, hot, score, blocks)
     return map_grad.reshape(MAPS // GROUPS, BLK, N), coef_grad
 
 

time: 114 us -> 106 us (0.930); the launches traced: 115 us -> 105 us
  starting transfers between devices: 15.6 us -> 34.9 us
  between operations: 14.1 us -> 0.89 us
  Pallas kernels: 30.6 us -> 20.1 us
  blocking collectives: 44.5 us -> 39 us
    ppermute x4 -> x11, starting transfers between devices: 6.07 us -> 25.4 us  [the longest x5 13.2 us: swap_cores(): return lax.ppermute(x, 'star', [(g, g ^ 1) for g in range(GROUPS)])]
    pallas_call x1, Pallas kernels: 9.7 us -> 0.82 us  [pack(): pl.pallas_call(pack_kernel, name='pack', out_shape=[pltpu.HBM((3, BLK, N)...]
    all_to_all x1, blocking collectives: 12.1 us -> 8.2 us  [per_device(): score = lax.all_to_all(score, 'star', 0, 0, tiled=True)]
    all_to_all x1, waiting for transfers between devices: 3.14 us -> 5.27 us  [per_device(): lax.all_to_all(sent.reshape(32, BLK, 256), 'row', 0, 0, tiled=True)]
    all_to_all x1, blocking collectives: 19.5 us -> 17.4 us  [per_device(): lax.all_to_all(sent.reshape(32, BLK, 256), 'row', 0, 0, tiled=True)]
    ppermute x4 -> x11, waiting for transfers between devices: 5.38 us -> 4.06 us  [the longest x6 4.04 us: along_x(): lax.ppermute(x, 'star', [(g, (g + 2 * k) % GROUPS) for g in range(GROUPS)])]
  transfers between devices with their start and end apart: 6 -> 12, of which waited for: 2 -> 3; matrix products, arithmetic and copies ran while one was open for 0% -> 0% of each run, Pallas kernels for 8% -> 9%
where the time goes in v3:
time: 106 us; the launch traced here: 105 us
  blocking collectives  39 us (37%)
  starting transfers between devices  34.9 us (33%)
  Pallas kernels  20.1 us (19%)
  waiting for transfers between devices  9.32 us (9%)
    all_to_all x1, blocking collectives, per_device(): lax.all_to_all(sent.reshape(32, BLK, 256), 'row', 0, 0, tiled=True)  17.4 us
    all_to_all x1, blocking collectives, per_device(): score = lax.all_to_all(score_of(path_grad, maps), 'row', 0, 0, tiled=True)  13.4 us
    ppermute x5, starting transfers between devices, swap_cores(): return lax.ppermute(x, 'star', [(g, g ^ 1) for g in range(GROUPS)])  13.2 us
    ppermute x6, starting transfers between devices, along_x(): lax.ppermute(x, 'star', [(g, (g + 2 * k) % GROUPS) for g in range(GROUPS)])  12.2 us
    all_to_all x1, starting transfers between devices, per_device(): lax.all_to_all(sent.reshape(32, BLK, 256), 'row', 0, 0, tiled=True)  9.49 us
    all_to_all x1, blocking collectives, per_device(): score = lax.all_to_all(score, 'star', 0, 0, tiled=True)  8.2 us
    pallas_call x1, Pallas kernels, pupil(): pl.pallas_call(pupil_kernel, name='pupil', out_shape=[pltpu.HBM((N, 256),...  6.3 us
    all_to_all x1, waiting for transfers between devices, per_device(): lax.all_to_all(sent.reshape(32, BLK, 256), 'row', 0, 0, tiled=True)  5.27 us
  transfers between devices with their start and end apart: 12, of which 3 were waited for; matrix products, arithmetic and copies ran while one was open for 0% of the time, Pallas kernels for 9%

profile of v3, /device:TPU:1, one launch (start us, length us, event | category | flops | bytes accessed | tf_op | source)
XLA Modules:
  0.0 105.0 jit_solution(17140335464888483829)
XLA Ops:
  0.6 3.3 %collective-permute-start = (bf16[12,32,1024]{2,1,0:T(8,128)(2,1)}, bf16[12,32,1024]{2,1,0:T(8,128)(2,1)S(1)}, u32[]{:S(2)}, u32[]{:S(2)}) collective-permute-start(bf16[12,32,1024]{2,1,0:T(8,128)(2,1)} %own_hbm.3), channel_id=1, source_target_pairs={{0,32},{32,0},{64,96},{96,64},{128,160},{160,128},{192,224},{224,1... | collective-permute-start | bytes 2359304 | tf_op jit(solution)/shard_map/ppermute | solution.py:489
  4.0 6.3 %pupil.1 = (bf16[1024,256]{1,0:T(8,128)(2,1)}, f32[128,1024]{1,0:T(8,128)}, bf16[2,512,1024]{2,1,0:T(8,128)(2,1)S(1)}, f32[64,64]{1,0:T(8,128)S(1)}, bf16[64,64]{1,0:T(8,128)(2,1)S(1)}, /*index=5*/s32[17]{0:T(128)S(1)}) custom-call(s32[8]{0:T(128)} %counts_hbm.1, s32[8,12]{1,0:T(8,128)} %cells_hbm.1, s32[8,12]{1,0:T(8,128)} %bands_hbm.1, ...), custom_call_target="tpu_custom_call" | custom-call | tf_op jit(solution)/shard_map/pupil/pallas_call | solution.py:219
  10.3 0.0 copy-start
  10.3 0.8 pack.1
  11.1 9.5 %all-to-all-start = ((bf16[32,32,256]{2,1,0:T(8,128)(2,1)}), bf16[32,32,256]{2,1,0:T(8,128)(2,1)S(1)}, u32[]{:S(2)}, u32[]{:S(2)}) async-start(bf16[32,32,256]{2,1,0:T(8,128)(2,1)} %bitcast.11), calls=%async_computation | async-start | bytes 1048576 | tf_op jit(solution)/shard_map/all_to_all | solution.py:504
  20.6 4.3 %collective-permute-start.1 = (bf16[3,32,1024]{2,1,0:T(8,128)(2,1)}, bf16[3,32,1024]{2,1,0:T(8,128)(2,1)S(1)}, u32[]{:S(2)}, u32[]{:S(2)}) collective-permute-start(bf16[3,32,1024]{2,1,0:T(8,128)(2,1)} %get-tuple-element.31), channel_id=1, source_target_pairs={{0,64},{32,96},{64,128},{96,160},{128,192},{160,224},{192,0},{224,... | collective-permute-start | bytes 589832 | tf_op jit(solution)/shard_map/ppermute | solution.py:493
  24.9 2.5 %collective-permute-start.3 = (bf16[3,32,1024]{2,1,0:T(8,128)(2,1)}, bf16[3,32,1024]{2,1,0:T(8,128)(2,1)}, u32[]{:S(2)}, u32[]{:S(2)}) collective-permute-start(bf16[3,32,1024]{2,1,0:T(8,128)(2,1)} %get-tuple-element.33), channel_id=1, source_target_pairs={{0,192},{32,224},{64,0},{96,32},{128,64},{160,96},{192,128},{224,1... | collective-permute-start | bytes 589832 | tf_op jit(solution)/shard_map/ppermute | solution.py:493
  27.4 0.9 collective-permute-done.1.one_hbm
  28.3 3.2 %collective-permute-done.2.two_hbm = bf16[3,32,1024]{2,1,0:T(8,128)(2,1)S(1)} collective-permute-done((bf16[3,32,1024]{2,1,0:T(8,128)(2,1)}, bf16[3,32,1024]{2,1,0:T(8,128)(2,1)S(1)}, u32[]{:S(2)}, u32[]{:S(2)}) %collective-permute-start.2) | collective-permute-done | bytes 196640 | tf_op jit(solution)/shard_map/ppermute | solution.py:493
  31.5 0.7 copy-done.2
  32.1 5.3 %all-to-all-done = bf16[32,32,256]{2,1,0:T(8,128)(2,1)S(1)} async-done(((bf16[32,32,256]{2,1,0:T(8,128)(2,1)}), bf16[32,32,256]{2,1,0:T(8,128)(2,1)S(1)}, u32[]{:S(2)}, u32[]{:S(2)}) %all-to-all-start) | async-done | bytes 524320 | tf_op jit(solution)/shard_map/all_to_all | solution.py:504
  37.4 4.1 %focal.1 = bf16[1024,256]{1,0:T(8,128)(2,1)S(1)} custom-call(s32[17]{0:T(128)S(1)} %get-tuple-element.24.meta_ref, bf16[1024,256]{1,0:T(8,128)(2,1)S(1)} %bitcast.7, bf16[2,512,1024]{2,1,0:T(8,128)(2,1)S(1)} %get-tuple-element.30.tables, bf16[12,32,1024]{2,1,0:T(8,128)(2,1)} %own_hbm.3, bf16[12,32,1024]{2,1,0:T(8,128)(2,1)} %copy-done, ...), custom_call_target="tpu_custom_call" | custom-call | tf_op jit(solution)/shard_map/focal/pallas_call | solution.py:356
  41.5 17.4 %all_to_all.20 = bf16[32,32,256]{2,1,0:T(8,128)(2,1)S(1)} all-to-all(bf16[32,32,256]{2,1,0:T(8,128)(2,1)S(1)} %bitcast.8), channel_id=1, replica_groups=mesh['star'=8,'row'=32] {'row'}, dimensions={0} | all-to-all | bytes 1048576 | tf_op jit(solution)/shard_map/all_to_all | solution.py:506
  58.9 2.9 %back.1.path_grad_ref.refs_0_ = bf16[128,1024]{1,0:T(8,128)(2,1)S(1)} custom-call(s32[17]{0:T(128)S(1)} %get-tuple-element.24.meta_ref, bf16[1024,256]{1,0:T(8,128)(2,1)S(1)} %bitcast.6, bf16[2,512,1024]{2,1,0:T(8,128)(2,1)S(1)} %get-tuple-element.30.tables, f32[128,1024]{1,0:T(8,128)} %get-tuple-element.34.frac_hbm), custom_call_target="tpu_custom_call" | custom-call | tf_op jit(solution)/shard_map/back/pallas_call | solution.py:394
  61.9 2.7 %collective-permute-start.6 = (bf16[128,1024]{1,0:T(8,128)(2,1)S(1)}, bf16[128,1024]{1,0:T(8,128)(2,1)S(1)}, u32[]{:S(2)}, u32[]{:S(2)}) collective-permute-start(bf16[128,1024]{1,0:T(8,128)(2,1)S(1)} %back.1.path_grad_ref.refs_0_), channel_id=1, source_target_pairs={{0,192},{32,224},{64,0},{96,32},{128,64},{160,96},{192,128},{224,1... | collective-permute-start | bytes 786440 | tf_op jit(solution)/shard_map/ppermute | solution.py:493
  64.6 2.6 %collective-permute-start.5 = (bf16[128,1024]{1,0:T(8,128)(2,1)S(1)}, bf16[128,1024]{1,0:T(8,128)(2,1)S(1)}, u32[]{:S(2)}, u32[]{:S(2)}) collective-permute-start(bf16[128,1024]{1,0:T(8,128)(2,1)S(1)} %back.1.path_grad_ref.refs_0_), channel_id=1, source_target_pairs={{0,128},{32,160},{64,192},{96,224},{128,0},{160,32},{192,64},{224,... | collective-permute-start | bytes 786440 | tf_op jit(solution)/shard_map/ppermute | solution.py:493
  67.3 3.3 %score.1 = f32[32,8,128]{2,1,0:T(8,128)S(1)} custom-call(bf16[128,1024]{1,0:T(8,128)(2,1)S(1)} %back.1.path_grad_ref.refs_0_, bf16[2048,1024]{1,0:T(8,128)(2,1)} %bitcast.10), custom_call_target="tpu_custom_call" | custom-call | tf_op jit(solution)/shard_map/score/pallas_call | solution.py:432
  70.6 13.4 %all_to_all.21 = f32[32,8,128]{2,1,0:T(8,128)S(1)} all-to-all(f32[32,8,128]{2,1,0:T(8,128)S(1)} %score.1), channel_id=1, replica_groups=mesh['star'=8,'row'=32] {'row'}, dimensions={0} | all-to-all | bytes 262144 | tf_op jit(solution)/shard_map/all_to_all | solution.py:509
  84.0 9.3 %collective-permute-start.7 = (bf16[128,1024]{1,0:T(8,128)(2,1)S(1)}, bf16[128,1024]{1,0:T(8,128)(2,1)S(1)}, u32[]{:S(2)}, u32[]{:S(2)}) collective-permute-start(bf16[128,1024]{1,0:T(8,128)(2,1)S(1)} %back.1.path_grad_ref.refs_0_), channel_id=1, source_target_pairs={{0,32},{32,0},{64,96},{96,64},{128,160},{160,128},{192,224},{224,1... | collective-permute-start | bytes 786440 | tf_op jit(solution)/shard_map/ppermute | solution.py:489
  93.3 0.1 collective-permute-start.8
  93.4 0.4 collective-permute-start.9
  93.8 0.1 collective-permute-start.10
  93.9 8.2 %all_to_all.22.score_ref = f32[8,8,128]{2,1,0:T(8,128)S(1)} all-to-all(f32[8,8,128]{2,1,0:T(8,128)S(1)} %broadcast_in_dim.2), channel_id=1, replica_groups=mesh['star'=8,'row'=32] {'star'}, dimensions={0} | all-to-all | bytes 65536 | tf_op jit(solution)/shard_map/all_to_all | solution.py:513
  102.1 2.7 %total.1 = (f32[256,1024]{1,0:T(8,128)}, f32[64,64]{1,0:T(8,128)}) custom-call(bf16[64,64]{1,0:T(8,128)(2,1)S(1)} %get-tuple-element.22.coef_ref, f32[64,64]{1,0:T(8,128)S(1)} %get-tuple-element.23.hot_ref, f32[8,8,128]{2,1,0:T(8,128)S(1)} %all_to_all.22.score_ref, bf16[128,1024]{1,0:T(8,128)(2,1)S(1)} %back.1.path_grad_ref.refs_0_, ...), custom_call_target="tpu_custom_call" | custom-call | tf_op jit(solution)/shard_map/total/pallas_call | solution.py:473
  (17 shorter events, 0.1 us)
Async XLA Ops:
  0.6 9.6 %collective-permute-start = (bf16[12,32,1024]{2,1,0:T(8,128)(2,1)}, bf16[12,32,1024]{2,1,0:T(8,128)(2,1)S(1)}, u32[]{:S(2)}, u32[]{:S(2)}) collective-permute-start(bf16[12,32,1024]{2,1,0:T(8,128)(2,1)} %own_hbm.3), channel_id=1, source_target_pairs={{0,32},{32,0},{64,96},{96,64},{128,160},{160,128},{192,224},{224,1... | collective-permute-start | bytes 2359304 | tf_op jit(solution)/shard_map/ppermute | solution.py:489
  10.3 27.1 %copy-start = (bf16[12,32,1024]{2,1,0:T(8,128)(2,1)}, bf16[12,32,1024]{2,1,0:T(8,128)(2,1)S(1)}, u32[]{:S(2)}) copy-start(bf16[12,32,1024]{2,1,0:T(8,128)(2,1)S(1)} %collective-permute-done.twin_hbm) | copy-start | bytes 2359300
  11.1 26.3 %all-to-all-start = ((bf16[32,32,256]{2,1,0:T(8,128)(2,1)}), bf16[32,32,256]{2,1,0:T(8,128)(2,1)S(1)}, u32[]{:S(2)}, u32[]{:S(2)}) async-start(bf16[32,32,256]{2,1,0:T(8,128)(2,1)} %bitcast.11), calls=%async_computation | async-start | bytes 1048576 | tf_op jit(solution)/shard_map/all_to_all | solution.py:504
  20.6 7.7 %collective-permute-start.1 = (bf16[3,32,1024]{2,1,0:T(8,128)(2,1)}, bf16[3,32,1024]{2,1,0:T(8,128)(2,1)S(1)}, u32[]{:S(2)}, u32[]{:S(2)}) collective-permute-start(bf16[3,32,1024]{2,1,0:T(8,128)(2,1)} %get-tuple-element.31), channel_id=1, source_target_pairs={{0,64},{32,96},{64,128},{96,160},{128,192},{160,224},{192,0},{224,... | collective-permute-start | bytes 589832 | tf_op jit(solution)/shard_map/ppermute | solution.py:493
  24.9 6.5 %collective-permute-start.2 = (bf16[3,32,1024]{2,1,0:T(8,128)(2,1)}, bf16[3,32,1024]{2,1,0:T(8,128)(2,1)S(1)}, u32[]{:S(2)}, u32[]{:S(2)}) collective-permute-start(bf16[3,32,1024]{2,1,0:T(8,128)(2,1)} %get-tuple-element.32), channel_id=1, source_target_pairs={{0,128},{32,160},{64,192},{96,224},{128,0},{160,32},{192,64},{224,... | collective-permute-start | bytes 589832 | tf_op jit(solution)/shard_map/ppermute | solution.py:493
  24.9 7.2 %collective-permute-start.3 = (bf16[3,32,1024]{2,1,0:T(8,128)(2,1)}, bf16[3,32,1024]{2,1,0:T(8,128)(2,1)}, u32[]{:S(2)}, u32[]{:S(2)}) collective-permute-start(bf16[3,32,1024]{2,1,0:T(8,128)(2,1)} %get-tuple-element.33), channel_id=1, source_target_pairs={{0,192},{32,224},{64,0},{96,32},{128,64},{160,96},{192,128},{224,1... | collective-permute-start | bytes 589832 | tf_op jit(solution)/shard_map/ppermute | solution.py:493
  28.3 3.2 %copy-start.1 = (bf16[3,32,1024]{2,1,0:T(8,128)(2,1)}, bf16[3,32,1024]{2,1,0:T(8,128)(2,1)S(1)}, u32[]{:S(2)}) copy-start(bf16[3,32,1024]{2,1,0:T(8,128)(2,1)S(1)} %collective-permute-done.1.one_hbm) | copy-start | bytes 589828
  31.5 0.7 copy-start.2
  61.9 22.1 %collective-permute-start.6 = (bf16[128,1024]{1,0:T(8,128)(2,1)S(1)}, bf16[128,1024]{1,0:T(8,128)(2,1)S(1)}, u32[]{:S(2)}, u32[]{:S(2)}) collective-permute-start(bf16[128,1024]{1,0:T(8,128)(2,1)S(1)} %back.1.path_grad_ref.refs_0_), channel_id=1, source_target_pairs={{0,192},{32,224},{64,0},{96,32},{128,64},{160,96},{192,128},{224,1... | collective-permute-start | bytes 786440 | tf_op jit(solution)/shard_map/ppermute | solution.py:493
  64.6 19.3 %collective-permute-start.5 = (bf16[128,1024]{1,0:T(8,128)(2,1)S(1)}, bf16[128,1024]{1,0:T(8,128)(2,1)S(1)}, u32[]{:S(2)}, u32[]{:S(2)}) collective-permute-start(bf16[128,1024]{1,0:T(8,128)(2,1)S(1)} %back.1.path_grad_ref.refs_0_), channel_id=1, source_target_pairs={{0,128},{32,160},{64,192},{96,224},{128,0},{160,32},{192,64},{224,... | collective-permute-start | bytes 786440 | tf_op jit(solution)/shard_map/ppermute | solution.py:493
  67.3 16.7 %collective-permute-start.4 = (bf16[128,1024]{1,0:T(8,128)(2,1)S(1)}, bf16[128,1024]{1,0:T(8,128)(2,1)S(1)}, u32[]{:S(2)}, u32[]{:S(2)}) collective-permute-start(bf16[128,1024]{1,0:T(8,128)(2,1)S(1)} %back.1.path_grad_ref.refs_0_), channel_id=1, source_target_pairs={{0,64},{32,96},{64,128},{96,160},{128,192},{160,224},{192,0},{224,... | collective-permute-start | bytes 786440 | tf_op jit(solution)/shard_map/ppermute | solution.py:493
  84.0 18.2 %collective-permute-start.7 = (bf16[128,1024]{1,0:T(8,128)(2,1)S(1)}, bf16[128,1024]{1,0:T(8,128)(2,1)S(1)}, u32[]{:S(2)}, u32[]{:S(2)}) collective-permute-start(bf16[128,1024]{1,0:T(8,128)(2,1)S(1)} %back.1.path_grad_ref.refs_0_), channel_id=1, source_target_pairs={{0,32},{32,0},{64,96},{96,64},{128,160},{160,128},{192,224},{224,1... | collective-permute-start | bytes 786440 | tf_op jit(solution)/shard_map/ppermute | solution.py:489
  93.3 8.9 %collective-permute-start.8 = (bf16[128,1024]{1,0:T(8,128)(2,1)S(1)}, bf16[128,1024]{1,0:T(8,128)(2,1)S(1)}, u32[]{:S(2)}, u32[]{:S(2)}) collective-permute-start(bf16[128,1024]{1,0:T(8,128)(2,1)S(1)} %collective-permute-done.4.refs_1_), channel_id=1, source_target_pairs={{0,32},{32,0},{64,96},{96,64},{128,160},{160,128},{192,224},{224,1... | collective-permute-start | bytes 786440 | tf_op jit(solution)/shard_map/ppermute | solution.py:489
  93.4 8.8 %collective-permute-start.9 = (bf16[128,1024]{1,0:T(8,128)(2,1)S(1)}, bf16[128,1024]{1,0:T(8,128)(2,1)S(1)}, u32[]{:S(2)}, u32[]{:S(2)}) collective-permute-start(bf16[128,1024]{1,0:T(8,128)(2,1)S(1)} %collective-permute-done.5.refs_2_), channel_id=1, source_target_pairs={{0,32},{32,0},{64,96},{96,64},{128,160},{160,128},{192,224},{224,1... | collective-permute-start | bytes 786440 | tf_op jit(solution)/shard_map/ppermute | solution.py:489
  93.8 8.4 %collective-permute-start.10 = (bf16[128,1024]{1,0:T(8,128)(2,1)S(1)}, bf16[128,1024]{1,0:T(8,128)(2,1)S(1)}, u32[]{:S(2)}, u32[]{:S(2)}) collective-permute-start(bf16[128,1024]{1,0:T(8,128)(2,1)S(1)} %collective-permute-done.6.refs_3_), channel_id=1, source_target_pairs={{0,32},{32,0},{64,96},{96,64},{128,160},{160,128},{192,224},{224,1... | collective-permute-start | bytes 786440 | tf_op jit(solution)/shard_map/ppermute | solution.py:489

commit v4 on v3

--- a/solution.py
+++ b/solution.py
@@ -271,7 +271,7 @@
                 out_ref[at : at + BLK, quad * 128 : quad * 128 + 128] = z[s].astype(BF)
 
 
-def pack_kernel(meta_ref, own_hbm, twin_hbm, one_hbm, two_hbm, three_hbm, sem):
+def pack_kernel(meta_ref, own_hbm, twin_hbm, one_hbm, two_hbm, three_hbm, held, in_sem, out_sem):
     group = lax.axis_index("star")
     sent = (one_hbm, two_hbm, three_hbm)
     for i in range(9):
@@ -281,17 +281,24 @@
 
         @pl.when((slot >= 0) & mine)
         def _():
-            pltpu.make_async_copy(own_hbm.at[place], sent[i // 3].at[i % 3], sem.at[i]).start()
+            pltpu.make_async_copy(own_hbm.at[place], held.at[i], in_sem.at[i]).start()
 
         @pl.when((slot >= 0) & jnp.logical_not(mine))
         def _():
-            pltpu.make_async_copy(twin_hbm.at[place], sent[i // 3].at[i % 3], sem.at[i]).start()
+            pltpu.make_async_copy(twin_hbm.at[place], held.at[i], in_sem.at[i]).start()
 
     for i in range(9):
 
         @pl.when(meta_ref[2 * MINE + i] >= 0)
         def _():
-            pltpu.make_async_copy(own_hbm.at[0], sent[i // 3].at[i % 3], sem.at[i]).wait()
+            pltpu.make_async_copy(own_hbm.at[0], held.at[i], in_sem.at[i]).wait()
+            pltpu.make_async_copy(held.at[i], sent[i // 3].at[i % 3], out_sem.at[i]).start()
+
+    for i in range(9):
+
+        @pl.when(meta_ref[2 * MINE + i] >= 0)
+        def _():
+            pltpu.make_async_copy(held.at[i], sent[i // 3].at[i % 3], out_sem.at[i]).wait()
 
 
 def pack(meta, own, twin):
@@ -301,7 +308,11 @@
         out_shape=[pltpu.HBM((3, BLK, N), BF)] * 3,
         in_specs=[SMEM_SPEC, HBM_SPEC, ANY_SPEC],
         out_specs=[HBM_SPEC] * 3,
-        scratch_shapes=[pltpu.SemaphoreType.DMA((9,))],
+        scratch_shapes=[
+            pltpu.VMEM((9, BLK, N), BF),
+            pltpu.SemaphoreType.DMA((9,)),
+            pltpu.SemaphoreType.DMA((9,)),
+        ],
         compiler_params=params(4),
     )(meta, *in_hbm(own), twin)
 
@@ -406,17 +417,10 @@
     )(meta, got, tables, *in_hbm(frac))
 
 
-def score_kernel(path_grad_ref, maps_hbm, score_ref, maps_ref, sem):
-    loads = []
-    for c in range(2):
-        rows = pl.ds(c * 1024, 1024)
-        loads.append(pltpu.make_async_copy(maps_hbm.at[rows], maps_ref.at[rows], sem.at[c]))
-        loads[-1].start()
+def score_kernel(path_grad_ref, maps_ref, score_ref):
     parts = []
     same = same_pixel((256, 128))
     for c in range(8):
-        if c % 4 == 0:
-            loads[c // 4].wait()
         some = dot(maps_ref[c * 256 : (c + 1) * 256, :], path_grad_ref[...], NT)
         kept = jnp.where(same, some, 0.0)
         for k in range(8):
@@ -433,11 +437,10 @@
         score_kernel,
         name="score",
         out_shape=jax.ShapeDtypeStruct((32, 8, 128), F32),
-        in_specs=[VMEM_SPEC, HBM_SPEC],
+        in_specs=[VMEM_SPEC, VMEM_SPEC],
         out_specs=VMEM_SPEC,
-        scratch_shapes=[pltpu.VMEM((MAPS * BLK, N), BF), pltpu.SemaphoreType.DMA((2,))],
         compiler_params=params(16),
-    )(path_grad, *in_hbm(maps))
+    )(path_grad, maps)
 
 
 def total_kernel(coef_ref, hot_ref, score_ref, *refs):

time: 106 us -> 103 us (0.972); the launches traced: 105 us -> 103 us
  starting transfers between devices: 34.9 us -> 25.3 us
  blocking collectives: 39 us -> 43 us
  waiting for transfers between devices: 9.32 us -> 13.2 us
    ppermute x5, starting transfers between devices: 13.2 us -> 7.56 us  [swap_cores(): return lax.ppermute(x, 'star', [(g, g ^ 1) for g in range(GROUPS)])]
    ppermute x6, waiting for transfers between devices: 4.04 us -> 8.6 us  [along_x(): lax.ppermute(x, 'star', [(g, (g + 2 * k) % GROUPS) for g in range(GROUPS)])]
    ppermute x6, starting transfers between devices: 12.2 us -> 8.29 us  [along_x(): lax.ppermute(x, 'star', [(g, (g + 2 * k) % GROUPS) for g in range(GROUPS)])]
    all_to_all x1, blocking collectives: 17.4 us -> 19.8 us  [per_device(): lax.all_to_all(sent.reshape(32, BLK, 256), 'row', 0, 0, tiled=True)]
    pallas_call x1, Pallas kernels: 3.29 us -> 1.48 us  [score_of(): pl.pallas_call(score_kernel, name='score', out_shape=jax.ShapeDtypeStruct...]
    pallas_call x1, Pallas kernels: 0.82 us -> 2.34 us  [pack(): pl.pallas_call(pack_kernel, name='pack', out_shape=[pltpu.HBM((3, BLK, N)...]
  transfers between devices with their start and end apart: 12 -> 12, of which waited for: 3 -> 4; matrix products, arithmetic and copies ran while one was open for 0% -> 0% of each run, Pallas kernels for 9% -> 8%
where the time goes in v4:
time: 103 us
  blocking collectives  43 us (42%)
  starting transfers between devices  25.3 us (25%)
  Pallas kernels  20.1 us (20%)
  waiting for transfers between devices  13.2 us (13%)
    all_to_all x1, blocking collectives, per_device(): lax.all_to_all(sent.reshape(32, BLK, 256), 'row', 0, 0, tiled=True)  19.8 us
    all_to_all x1, blocking collectives, per_device(): score = lax.all_to_all(score_of(path_grad, maps), 'row', 0, 0, tiled=True)  14.3 us
    all_to_all x1, starting transfers between devices, per_device(): lax.all_to_all(sent.reshape(32, BLK, 256), 'row', 0, 0, tiled=True)  9.49 us
    all_to_all x1, blocking collectives, per_device(): score = lax.all_to_all(score, 'star', 0, 0, tiled=True)  8.92 us
    ppermute x6, waiting for transfers between devices, along_x(): lax.ppermute(x, 'star', [(g, (g + 2 * k) % GROUPS) for g in range(GROUPS)])  8.6 us
    ppermute x6, starting transfers between devices, along_x(): lax.ppermute(x, 'star', [(g, (g + 2 * k) % GROUPS) for g in range(GROUPS)])  8.29 us
    ppermute x5, starting transfers between devices, swap_cores(): return lax.ppermute(x, 'star', [(g, g ^ 1) for g in range(GROUPS)])  7.56 us
    pallas_call x1, Pallas kernels, pupil(): pl.pallas_call(pupil_kernel, name='pupil', out_shape=[pltpu.HBM((N, 256),...  6.3 us
  transfers between devices with their start and end apart: 12, of which 4 were waited for; matrix products, arithmetic and copies ran while one was open for 0% of the time, Pallas kernels for 8%

profile of v4, /device:TPU:1, one launch (start us, length us, event | category | flops | bytes accessed | tf_op | source)
XLA Modules:
  0.0 103.3 jit_solution(7717919143114298869)
XLA Ops:
  0.6 3.3 %collective-permute-start = (bf16[12,32,1024]{2,1,0:T(8,128)(2,1)}, bf16[12,32,1024]{2,1,0:T(8,128)(2,1)S(1)}, u32[]{:S(2)}, u32[]{:S(2)}) collective-permute-start(bf16[12,32,1024]{2,1,0:T(8,128)(2,1)} %own_hbm.3), channel_id=1, source_target_pairs={{0,32},{32,0},{64,96},{96,64},{128,160},{160,128},{192,224},{224,1... | collective-permute-start | bytes 2359304 | tf_op jit(solution)/shard_map/ppermute | solution.py:492
  4.0 6.3 %pupil.1 = (bf16[1024,256]{1,0:T(8,128)(2,1)}, f32[128,1024]{1,0:T(8,128)}, bf16[2,512,1024]{2,1,0:T(8,128)(2,1)S(1)}, f32[64,64]{1,0:T(8,128)S(1)}, bf16[64,64]{1,0:T(8,128)(2,1)S(1)}, /*index=5*/s32[17]{0:T(128)S(1)}) custom-call(s32[8]{0:T(128)} %counts_hbm.1, s32[8,12]{1,0:T(8,128)} %cells_hbm.1, s32[8,12]{1,0:T(8,128)} %bands_hbm.1, ...), custom_call_target="tpu_custom_call" | custom-call | tf_op jit(solution)/shard_map/pupil/pallas_call | solution.py:219
  10.3 2.3 %pack.1 = (bf16[3,32,1024]{2,1,0:T(8,128)(2,1)}, bf16[3,32,1024]{2,1,0:T(8,128)(2,1)}, bf16[3,32,1024]{2,1,0:T(8,128)(2,1)}) custom-call(s32[17]{0:T(128)S(1)} %get-tuple-element.24.meta_ref, bf16[12,32,1024]{2,1,0:T(8,128)(2,1)} %own_hbm.3, bf16[12,32,1024]{2,1,0:T(8,128)(2,1)S(1)} %collective-permute-done.twin_hbm), custom_call_target="tpu_custom_call" | custom-call | tf_op jit(solution)/shard_map/pack/pallas_call | solution.py:305
  12.6 9.5 %all-to-all-start = ((bf16[32,32,256]{2,1,0:T(8,128)(2,1)}), bf16[32,32,256]{2,1,0:T(8,128)(2,1)S(1)}, u32[]{:S(2)}, u32[]{:S(2)}) async-start(bf16[32,32,256]{2,1,0:T(8,128)(2,1)} %bitcast.11), calls=%async_computation | async-start | bytes 1048576 | tf_op jit(solution)/shard_map/all_to_all | solution.py:507
  22.2 2.3 %collective-permute-start.2 = (bf16[3,32,1024]{2,1,0:T(8,128)(2,1)}, bf16[3,32,1024]{2,1,0:T(8,128)(2,1)S(1)}, u32[]{:S(2)}, u32[]{:S(2)}) collective-permute-start(bf16[3,32,1024]{2,1,0:T(8,128)(2,1)} %get-tuple-element.32), channel_id=1, source_target_pairs={{0,128},{32,160},{64,192},{96,224},{128,0},{160,32},{192,64},{224,... | collective-permute-start | bytes 589832 | tf_op jit(solution)/shard_map/ppermute | solution.py:496
  24.5 1.2 %collective-permute-start.3 = (bf16[3,32,1024]{2,1,0:T(8,128)(2,1)}, bf16[3,32,1024]{2,1,0:T(8,128)(2,1)}, u32[]{:S(2)}, u32[]{:S(2)}) collective-permute-start(bf16[3,32,1024]{2,1,0:T(8,128)(2,1)} %get-tuple-element.33), channel_id=1, source_target_pairs={{0,192},{32,224},{64,0},{96,32},{128,64},{160,96},{192,128},{224,1... | collective-permute-start | bytes 589832 | tf_op jit(solution)/shard_map/ppermute | solution.py:496
  25.7 5.3 %collective-permute-done.1.one_hbm = bf16[3,32,1024]{2,1,0:T(8,128)(2,1)S(1)} collective-permute-done((bf16[3,32,1024]{2,1,0:T(8,128)(2,1)}, bf16[3,32,1024]{2,1,0:T(8,128)(2,1)S(1)}, u32[]{:S(2)}, u32[]{:S(2)}) %collective-permute-start.1) | collective-permute-done | bytes 196640 | tf_op jit(solution)/shard_map/ppermute | solution.py:496
  30.9 2.8 %collective-permute-done.2.two_hbm = bf16[3,32,1024]{2,1,0:T(8,128)(2,1)S(1)} collective-permute-done((bf16[3,32,1024]{2,1,0:T(8,128)(2,1)}, bf16[3,32,1024]{2,1,0:T(8,128)(2,1)S(1)}, u32[]{:S(2)}, u32[]{:S(2)}) %collective-permute-start.2) | collective-permute-done | bytes 196640 | tf_op jit(solution)/shard_map/ppermute | solution.py:496
  33.7 0.7 copy-done.3
  34.4 0.6 collective-permute-done.3.three_hbm
  34.9 4.6 %all-to-all-done = bf16[32,32,256]{2,1,0:T(8,128)(2,1)S(1)} async-done(((bf16[32,32,256]{2,1,0:T(8,128)(2,1)}), bf16[32,32,256]{2,1,0:T(8,128)(2,1)S(1)}, u32[]{:S(2)}, u32[]{:S(2)}) %all-to-all-start) | async-done | bytes 524320 | tf_op jit(solution)/shard_map/all_to_all | solution.py:507
  39.5 4.3 %focal.1 = bf16[1024,256]{1,0:T(8,128)(2,1)S(1)} custom-call(s32[17]{0:T(128)S(1)} %get-tuple-element.24.meta_ref, bf16[1024,256]{1,0:T(8,128)(2,1)S(1)} %bitcast.9, bf16[2,512,1024]{2,1,0:T(8,128)(2,1)S(1)} %get-tuple-element.30.tables, bf16[12,32,1024]{2,1,0:T(8,128)(2,1)} %own_hbm.3, bf16[12,32,1024]{2,1,0:T(8,128)(2,1)} %copy-done.1, ...), custom_call_target="tpu_custom_call" | custom-call | tf_op jit(solution)/shard_map/focal/pallas_call | solution.py:367
  43.9 19.8 %all_to_all.20 = bf16[32,32,256]{2,1,0:T(8,128)(2,1)S(1)} all-to-all(bf16[32,32,256]{2,1,0:T(8,128)(2,1)S(1)} %bitcast.10), channel_id=1, replica_groups=mesh['star'=8,'row'=32] {'row'}, dimensions={0} | all-to-all | bytes 1048576 | tf_op jit(solution)/shard_map/all_to_all | solution.py:509
  63.7 2.9 %back.1.path_grad_ref.refs_0_ = bf16[128,1024]{1,0:T(8,128)(2,1)S(1)} custom-call(s32[17]{0:T(128)S(1)} %get-tuple-element.24.meta_ref, bf16[1024,256]{1,0:T(8,128)(2,1)S(1)} %bitcast.8, bf16[2,512,1024]{2,1,0:T(8,128)(2,1)S(1)} %get-tuple-element.30.tables, f32[128,1024]{1,0:T(8,128)} %get-tuple-element.34.frac_hbm), custom_call_target="tpu_custom_call" | custom-call | tf_op jit(solution)/shard_map/back/pallas_call | solution.py:405
  66.7 4.1 %collective-permute-start.6 = (bf16[128,1024]{1,0:T(8,128)(2,1)S(1)}, bf16[128,1024]{1,0:T(8,128)(2,1)S(1)}, u32[]{:S(2)}, u32[]{:S(2)}) collective-permute-start(bf16[128,1024]{1,0:T(8,128)(2,1)S(1)} %back.1.path_grad_ref.refs_0_), channel_id=1, source_target_pairs={{0,192},{32,224},{64,0},{96,32},{128,64},{160,96},{192,128},{224,1... | collective-permute-start | bytes 786440 | tf_op jit(solution)/shard_map/ppermute | solution.py:496
  70.8 0.2 collective-permute-start.5
  70.9 0.5 collective-permute-start.4
  71.4 1.5 %score.1 = f32[32,8,128]{2,1,0:T(8,128)S(1)} custom-call(bf16[128,1024]{1,0:T(8,128)(2,1)S(1)} %back.1.path_grad_ref.refs_0_, bf16[2048,1024]{1,0:T(8,128)(2,1)S(1)} %bitcast.7), custom_call_target="tpu_custom_call" | custom-call | tf_op jit(solution)/shard_map/score/pallas_call | solution.py:436
  72.9 14.3 %all_to_all.21 = f32[32,8,128]{2,1,0:T(8,128)S(1)} all-to-all(f32[32,8,128]{2,1,0:T(8,128)S(1)} %score.1), channel_id=1, replica_groups=mesh['star'=8,'row'=32] {'row'}, dimensions={0} | all-to-all | bytes 262144 | tf_op jit(solution)/shard_map/all_to_all | solution.py:512
  87.2 3.6 %collective-permute-start.7 = (bf16[128,1024]{1,0:T(8,128)(2,1)S(1)}, bf16[128,1024]{1,0:T(8,128)(2,1)S(1)}, u32[]{:S(2)}, u32[]{:S(2)}) collective-permute-start(bf16[128,1024]{1,0:T(8,128)(2,1)S(1)} %back.1.path_grad_ref.refs_0_), channel_id=1, source_target_pairs={{0,32},{32,0},{64,96},{96,64},{128,160},{160,128},{192,224},{224,1... | collective-permute-start | bytes 786440 | tf_op jit(solution)/shard_map/ppermute | solution.py:492
  90.8 0.1 collective-permute-start.8
  90.9 0.4 collective-permute-start.9
  91.5 8.9 %all_to_all.22.score_ref = f32[8,8,128]{2,1,0:T(8,128)S(1)} all-to-all(f32[8,8,128]{2,1,0:T(8,128)S(1)} %broadcast_in_dim.2), channel_id=1, replica_groups=mesh['star'=8,'row'=32] {'star'}, dimensions={0} | all-to-all | bytes 65536 | tf_op jit(solution)/shard_map/all_to_all | solution.py:516
  100.4 2.7 %total.1 = (f32[256,1024]{1,0:T(8,128)}, f32[64,64]{1,0:T(8,128)}) custom-call(bf16[64,64]{1,0:T(8,128)(2,1)S(1)} %get-tuple-element.22.coef_ref, f32[64,64]{1,0:T(8,128)S(1)} %get-tuple-element.23.hot_ref, f32[8,8,128]{2,1,0:T(8,128)S(1)} %all_to_all.22.score_ref, bf16[128,1024]{1,0:T(8,128)(2,1)S(1)} %back.1.path_grad_ref.refs_0_, ...), custom_call_target="tpu_custom_call" | custom-call | tf_op jit(solution)/shard_map/total/pallas_call | solution.py:476
  (19 shorter events, 0.3 us)
Async XLA Ops:
  0.6 9.6 %collective-permute-start = (bf16[12,32,1024]{2,1,0:T(8,128)(2,1)}, bf16[12,32,1024]{2,1,0:T(8,128)(2,1)S(1)}, u32[]{:S(2)}, u32[]{:S(2)}) collective-permute-start(bf16[12,32,1024]{2,1,0:T(8,128)(2,1)} %own_hbm.3), channel_id=1, source_target_pairs={{0,32},{32,0},{64,96},{96,64},{128,160},{160,128},{192,224},{224,1... | collective-permute-start | bytes 2359304 | tf_op jit(solution)/shard_map/ppermute | solution.py:492
  10.3 29.2 %copy-start.1 = (bf16[12,32,1024]{2,1,0:T(8,128)(2,1)}, bf16[12,32,1024]{2,1,0:T(8,128)(2,1)S(1)}, u32[]{:S(2)}) copy-start(bf16[12,32,1024]{2,1,0:T(8,128)(2,1)S(1)} %collective-permute-done.twin_hbm) | copy-start | bytes 2359300
  12.6 26.9 %all-to-all-start = ((bf16[32,32,256]{2,1,0:T(8,128)(2,1)}), bf16[32,32,256]{2,1,0:T(8,128)(2,1)S(1)}, u32[]{:S(2)}, u32[]{:S(2)}) async-start(bf16[32,32,256]{2,1,0:T(8,128)(2,1)} %bitcast.11), calls=%async_computation | async-start | bytes 1048576 | tf_op jit(solution)/shard_map/all_to_all | solution.py:507
  22.1 8.8 %collective-permute-start.1 = (bf16[3,32,1024]{2,1,0:T(8,128)(2,1)}, bf16[3,32,1024]{2,1,0:T(8,128)(2,1)S(1)}, u32[]{:S(2)}, u32[]{:S(2)}) collective-permute-start(bf16[3,32,1024]{2,1,0:T(8,128)(2,1)} %get-tuple-element.31), channel_id=1, source_target_pairs={{0,64},{32,96},{64,128},{96,160},{128,192},{160,224},{192,0},{224,... | collective-permute-start | bytes 589832 | tf_op jit(solution)/shard_map/ppermute | solution.py:496
  22.2 11.5 %collective-permute-start.2 = (bf16[3,32,1024]{2,1,0:T(8,128)(2,1)}, bf16[3,32,1024]{2,1,0:T(8,128)(2,1)S(1)}, u32[]{:S(2)}, u32[]{:S(2)}) collective-permute-start(bf16[3,32,1024]{2,1,0:T(8,128)(2,1)} %get-tuple-element.32), channel_id=1, source_target_pairs={{0,128},{32,160},{64,192},{96,224},{128,0},{160,32},{192,64},{224,... | collective-permute-start | bytes 589832 | tf_op jit(solution)/shard_map/ppermute | solution.py:496
  24.5 10.4 %collective-permute-start.3 = (bf16[3,32,1024]{2,1,0:T(8,128)(2,1)}, bf16[3,32,1024]{2,1,0:T(8,128)(2,1)}, u32[]{:S(2)}, u32[]{:S(2)}) collective-permute-start(bf16[3,32,1024]{2,1,0:T(8,128)(2,1)} %get-tuple-element.33), channel_id=1, source_target_pairs={{0,192},{32,224},{64,0},{96,32},{128,64},{160,96},{192,128},{224,1... | collective-permute-start | bytes 589832 | tf_op jit(solution)/shard_map/ppermute | solution.py:496
  30.9 2.8 %copy-start.2 = (bf16[3,32,1024]{2,1,0:T(8,128)(2,1)}, bf16[3,32,1024]{2,1,0:T(8,128)(2,1)S(1)}, u32[]{:S(2)}) copy-start(bf16[3,32,1024]{2,1,0:T(8,128)(2,1)S(1)} %collective-permute-done.1.one_hbm) | copy-start | bytes 589828
  33.7 0.7 copy-start.3
  39.5 31.9 %copy-start = (bf16[64,32,1024]{2,1,0:T(8,128)(2,1)S(1)}, bf16[64,32,1024]{2,1,0:T(8,128)(2,1)}, u32[]{:S(2)}) copy-start(bf16[64,32,1024]{2,1,0:T(8,128)(2,1)} %param.7) | copy-start | bytes 12582916
  66.7 20.6 %collective-permute-start.6 = (bf16[128,1024]{1,0:T(8,128)(2,1)S(1)}, bf16[128,1024]{1,0:T(8,128)(2,1)S(1)}, u32[]{:S(2)}, u32[]{:S(2)}) collective-permute-start(bf16[128,1024]{1,0:T(8,128)(2,1)S(1)} %back.1.path_grad_ref.refs_0_), channel_id=1, source_target_pairs={{0,192},{32,224},{64,0},{96,32},{128,64},{160,96},{192,128},{224,1... | collective-permute-start | bytes 786440 | tf_op jit(solution)/shard_map/ppermute | solution.py:496
  70.8 16.5 %collective-permute-start.5 = (bf16[128,1024]{1,0:T(8,128)(2,1)S(1)}, bf16[128,1024]{1,0:T(8,128)(2,1)S(1)}, u32[]{:S(2)}, u32[]{:S(2)}) collective-permute-start(bf16[128,1024]{1,0:T(8,128)(2,1)S(1)} %back.1.path_grad_ref.refs_0_), channel_id=1, source_target_pairs={{0,128},{32,160},{64,192},{96,224},{128,0},{160,32},{192,64},{224,... | collective-permute-start | bytes 786440 | tf_op jit(solution)/shard_map/ppermute | solution.py:496
  70.9 16.3 %collective-permute-start.4 = (bf16[128,1024]{1,0:T(8,128)(2,1)S(1)}, bf16[128,1024]{1,0:T(8,128)(2,1)S(1)}, u32[]{:S(2)}, u32[]{:S(2)}) collective-permute-start(bf16[128,1024]{1,0:T(8,128)(2,1)S(1)} %back.1.path_grad_ref.refs_0_), channel_id=1, source_target_pairs={{0,64},{32,96},{64,128},{96,160},{128,192},{160,224},{192,0},{224,... | collective-permute-start | bytes 786440 | tf_op jit(solution)/shard_map/ppermute | solution.py:496
  87.2 13.2 %collective-permute-start.7 = (bf16[128,1024]{1,0:T(8,128)(2,1)S(1)}, bf16[128,1024]{1,0:T(8,128)(2,1)S(1)}, u32[]{:S(2)}, u32[]{:S(2)}) collective-permute-start(bf16[128,1024]{1,0:T(8,128)(2,1)S(1)} %back.1.path_grad_ref.refs_0_), channel_id=1, source_target_pairs={{0,32},{32,0},{64,96},{96,64},{128,160},{160,128},{192,224},{224,1... | collective-permute-start | bytes 786440 | tf_op jit(solution)/shard_map/ppermute | solution.py:492
  90.8 9.6 %collective-permute-start.8 = (bf16[128,1024]{1,0:T(8,128)(2,1)S(1)}, bf16[128,1024]{1,0:T(8,128)(2,1)S(1)}, u32[]{:S(2)}, u32[]{:S(2)}) collective-permute-start(bf16[128,1024]{1,0:T(8,128)(2,1)S(1)} %collective-permute-done.4.refs_1_), channel_id=1, source_target_pairs={{0,32},{32,0},{64,96},{96,64},{128,160},{160,128},{192,224},{224,1... | collective-permute-start | bytes 786440 | tf_op jit(solution)/shard_map/ppermute | solution.py:492
  90.9 9.5 %collective-permute-start.9 = (bf16[128,1024]{1,0:T(8,128)(2,1)S(1)}, bf16[128,1024]{1,0:T(8,128)(2,1)S(1)}, u32[]{:S(2)}, u32[]{:S(2)}) collective-permute-start(bf16[128,1024]{1,0:T(8,128)(2,1)S(1)} %collective-permute-done.5.refs_2_), channel_id=1, source_target_pairs={{0,32},{32,0},{64,96},{96,64},{128,160},{160,128},{192,224},{224,1... | collective-permute-start | bytes 786440 | tf_op jit(solution)/shard_map/ppermute | solution.py:492
  91.4 9.1 %collective-permute-start.10 = (bf16[128,1024]{1,0:T(8,128)(2,1)S(1)}, bf16[128,1024]{1,0:T(8,128)(2,1)S(1)}, u32[]{:S(2)}, u32[]{:S(2)}) collective-permute-start(bf16[128,1024]{1,0:T(8,128)(2,1)S(1)} %collective-permute-done.6.refs_3_), channel_id=1, source_target_pairs={{0,32},{32,0},{64,96},{96,64},{128,160},{160,128},{192,224},{224,1... | collective-permute-start | bytes 786440 | tf_op jit(solution)/shard_map/ppermute | solution.py:492

commit v5 on v4

--- a/solution.py
+++ b/solution.py
@@ -510,8 +510,8 @@
     path_grad = back(meta, got, tables, frac)
     blocks = [path_grad] + [along_x(path_grad, k) for k in (1, 2, 3)]
     score = lax.all_to_all(score_of(path_grad, maps), "row", 0, 0, tiled=True)
-    score, *blocks = lax.optimization_barrier((score, *blocks))
     blocks = blocks + [swap_cores(block) for block in blocks]
+    score, blocks[MINE] = lax.optimization_barrier((score, blocks[MINE]))
     score = jnp.broadcast_to(jnp.sum(score, 0)[None], (GROUPS, 8, 128))
     score = lax.all_to_all(score, "star", 0, 0, tiled=True)
     map_grad, coef_grad = total(coef, hot, score, blocks)

time: 103 us -> 104 us (level)
  blocking collectives: 43 us -> 34.4 us
  starting transfers between devices: 25.3 us -> 31.8 us
  waiting for transfers between devices: 13.2 us -> 17 us
    all_to_all x1 -> x0, blocking collectives: 14.3 us -> none  [per_device(): score = lax.all_to_all(score_of(path_grad, maps), 'row', 0, 0, tiled=True)]
    all_to_all x0 -> x1, waiting for transfers between devices: none -> 5.06 us  [per_device(): score = lax.all_to_all(score_of(path_grad, maps), 'row', 0, 0, tiled=True)]
    all_to_all x0 -> x1, starting transfers between devices: none -> 4.34 us  [per_device(): score = lax.all_to_all(score_of(path_grad, maps), 'row', 0, 0, tiled=True)]
    all_to_all x1, blocking collectives: 19.8 us -> 23.9 us  [per_device(): lax.all_to_all(sent.reshape(32, BLK, 256), 'row', 0, 0, tiled=True)]
    all_to_all x1, waiting for transfers between devices: 4.59 us -> 1.18 us  [per_device(): lax.all_to_all(sent.reshape(32, BLK, 256), 'row', 0, 0, tiled=True)]
    ppermute x5, starting transfers between devices: 7.56 us -> 10.5 us  [swap_cores(): return lax.ppermute(x, 'star', [(g, g ^ 1) for g in range(GROUPS)])]
    ppermute x6, waiting for transfers between devices: 8.6 us -> 10.7 us  [along_x(): lax.ppermute(x, 'star', [(g, (g + 2 * k) % GROUPS) for g in range(GROUPS)])]
    all_to_all x1, blocking collectives: 8.92 us -> 10.6 us  [per_device(): score = lax.all_to_all(score, 'star', 0, 0, tiled=True)]
  transfers between devices with their start and end apart: 12 -> 13, of which waited for: 4 -> 5; matrix products, arithmetic and copies ran while one was open for 0% -> 0% of each run, Pallas kernels for 8% -> 8%
where the time goes in v5:
time: 104 us
  blocking collectives  34.4 us (33%)
  starting transfers between devices  31.8 us (31%)
  Pallas kernels  19.4 us (19%)
  waiting for transfers between devices  17 us (16%)
    all_to_all x1, blocking collectives, per_device(): lax.all_to_all(sent.reshape(32, BLK, 256), 'row', 0, 0, tiled=True)  23.9 us
    ppermute x6, waiting for transfers between devices, along_x(): lax.ppermute(x, 'star', [(g, (g + 2 * k) % GROUPS) for g in range(GROUPS)])  10.7 us
    all_to_all x1, blocking collectives, per_device(): score = lax.all_to_all(score, 'star', 0, 0, tiled=True)  10.6 us
    ppermute x5, starting transfers between devices, swap_cores(): return lax.ppermute(x, 'star', [(g, g ^ 1) for g in range(GROUPS)])  10.5 us
    all_to_all x1, starting transfers between devices, per_device(): lax.all_to_all(sent.reshape(32, BLK, 256), 'row', 0, 0, tiled=True)  9.49 us
    ppermute x6, starting transfers between devices, along_x(): lax.ppermute(x, 'star', [(g, (g + 2 * k) % GROUPS) for g in range(GROUPS)])  7.5 us
    pallas_call x1, Pallas kernels, pupil(): pl.pallas_call(pupil_kernel, name='pupil', out_shape=[pltpu.HBM((N, 256),...  6.29 us
    all_to_all x1, waiting for transfers between devices, per_device(): score = lax.all_to_all(score_of(path_grad, maps), 'row', 0, 0, tiled=True)  5.06 us
  transfers between devices with their start and end apart: 13, of which 5 were waited for; matrix products, arithmetic and copies ran while one was open for 0% of the time, Pallas kernels for 8%

profile of v5, /device:TPU:1, one launch (start us, length us, event | category | flops | bytes accessed | tf_op | source)
XLA Modules:
  0.0 104.2 jit_solution(2442492739929498981)
XLA Ops:
  0.6 3.3 %collective-permute-start = (bf16[12,32,1024]{2,1,0:T(8,128)(2,1)}, bf16[12,32,1024]{2,1,0:T(8,128)(2,1)S(1)}, u32[]{:S(2)}, u32[]{:S(2)}) collective-permute-start(bf16[12,32,1024]{2,1,0:T(8,128)(2,1)} %own_hbm.3), channel_id=1, source_target_pairs={{0,32},{32,0},{64,96},{96,64},{128,160},{160,128},{192,224},{224,1... | collective-permute-start | bytes 2359304 | tf_op jit(solution)/shard_map/ppermute | solution.py:492
  4.0 6.3 %pupil.1 = (bf16[1024,256]{1,0:T(8,128)(2,1)}, f32[128,1024]{1,0:T(8,128)}, bf16[2,512,1024]{2,1,0:T(8,128)(2,1)S(1)}, f32[64,64]{1,0:T(8,128)S(1)}, bf16[64,64]{1,0:T(8,128)(2,1)S(1)}, /*index=5*/s32[17]{0:T(128)S(1)}) custom-call(s32[8]{0:T(128)} %counts_hbm.1, s32[8,12]{1,0:T(8,128)} %cells_hbm.1, s32[8,12]{1,0:T(8,128)} %bands_hbm.1, ...), custom_call_target="tpu_custom_call" | custom-call | tf_op jit(solution)/shard_map/pupil/pallas_call | solution.py:219
  10.3 1.0 pack.1
  11.3 9.5 %all-to-all-start = ((bf16[32,32,256]{2,1,0:T(8,128)(2,1)}), bf16[32,32,256]{2,1,0:T(8,128)(2,1)S(1)}, u32[]{:S(2)}, u32[]{:S(2)}) async-start(bf16[32,32,256]{2,1,0:T(8,128)(2,1)} %bitcast.11), calls=%async_computation | async-start | bytes 1048576 | tf_op jit(solution)/shard_map/all_to_all | solution.py:507
  20.8 1.3 %collective-permute-start.1 = (bf16[3,32,1024]{2,1,0:T(8,128)(2,1)}, bf16[3,32,1024]{2,1,0:T(8,128)(2,1)S(1)}, u32[]{:S(2)}, u32[]{:S(2)}) collective-permute-start(bf16[3,32,1024]{2,1,0:T(8,128)(2,1)} %get-tuple-element.28), channel_id=1, source_target_pairs={{0,64},{32,96},{64,128},{96,160},{128,192},{160,224},{192,0},{224,... | collective-permute-start | bytes 589832 | tf_op jit(solution)/shard_map/ppermute | solution.py:496
  22.0 3.9 %collective-permute-start.2 = (bf16[3,32,1024]{2,1,0:T(8,128)(2,1)}, bf16[3,32,1024]{2,1,0:T(8,128)(2,1)S(1)}, u32[]{:S(2)}, u32[]{:S(2)}) collective-permute-start(bf16[3,32,1024]{2,1,0:T(8,128)(2,1)} %get-tuple-element.29), channel_id=1, source_target_pairs={{0,128},{32,160},{64,192},{96,224},{128,0},{160,32},{192,64},{224,... | collective-permute-start | bytes 589832 | tf_op jit(solution)/shard_map/ppermute | solution.py:496
  25.9 4.3 %collective-permute-done.1.one_hbm = bf16[3,32,1024]{2,1,0:T(8,128)(2,1)S(1)} collective-permute-done((bf16[3,32,1024]{2,1,0:T(8,128)(2,1)}, bf16[3,32,1024]{2,1,0:T(8,128)(2,1)S(1)}, u32[]{:S(2)}, u32[]{:S(2)}) %collective-permute-start.1) | collective-permute-done | bytes 196640 | tf_op jit(solution)/shard_map/ppermute | solution.py:496
  30.2 5.5 %collective-permute-done.2.two_hbm = bf16[3,32,1024]{2,1,0:T(8,128)(2,1)S(1)} collective-permute-done((bf16[3,32,1024]{2,1,0:T(8,128)(2,1)}, bf16[3,32,1024]{2,1,0:T(8,128)(2,1)S(1)}, u32[]{:S(2)}, u32[]{:S(2)}) %collective-permute-start.2) | collective-permute-done | bytes 196640 | tf_op jit(solution)/shard_map/ppermute | solution.py:496
  35.7 0.7 copy-done.3
  36.4 1.2 %all-to-all-done = bf16[32,32,256]{2,1,0:T(8,128)(2,1)S(1)} async-done(((bf16[32,32,256]{2,1,0:T(8,128)(2,1)}), bf16[32,32,256]{2,1,0:T(8,128)(2,1)S(1)}, u32[]{:S(2)}, u32[]{:S(2)}) %all-to-all-start) | async-done | bytes 524320 | tf_op jit(solution)/shard_map/all_to_all | solution.py:507
  37.6 4.3 %focal.1 = bf16[1024,256]{1,0:T(8,128)(2,1)S(1)} custom-call(s32[17]{0:T(128)S(1)} %get-tuple-element.21.meta_ref, bf16[1024,256]{1,0:T(8,128)(2,1)S(1)} %bitcast.9, bf16[2,512,1024]{2,1,0:T(8,128)(2,1)S(1)} %get-tuple-element.27.tables, bf16[12,32,1024]{2,1,0:T(8,128)(2,1)} %own_hbm.3, bf16[12,32,1024]{2,1,0:T(8,128)(2,1)} %copy-done.1, ...), custom_call_target="tpu_custom_call" | custom-call | tf_op jit(solution)/shard_map/focal/pallas_call | solution.py:367
  41.9 23.9 %all_to_all.20 = bf16[32,32,256]{2,1,0:T(8,128)(2,1)S(1)} all-to-all(bf16[32,32,256]{2,1,0:T(8,128)(2,1)S(1)} %bitcast.10), channel_id=1, replica_groups=mesh['star'=8,'row'=32] {'row'}, dimensions={0} | all-to-all | bytes 1048576 | tf_op jit(solution)/shard_map/all_to_all | solution.py:509
  65.8 2.9 %back.1.path_grad_ref.refs_0_ = bf16[128,1024]{1,0:T(8,128)(2,1)S(1)} custom-call(s32[17]{0:T(128)S(1)} %get-tuple-element.21.meta_ref, bf16[1024,256]{1,0:T(8,128)(2,1)S(1)} %bitcast.8, bf16[2,512,1024]{2,1,0:T(8,128)(2,1)S(1)} %get-tuple-element.27.tables, f32[128,1024]{1,0:T(8,128)} %get-tuple-element.31.frac_hbm), custom_call_target="tpu_custom_call" | custom-call | tf_op jit(solution)/shard_map/back/pallas_call | solution.py:405
  68.7 1.1 %collective-permute-start.7 = (bf16[128,1024]{1,0:T(8,128)(2,1)S(1)}, bf16[128,1024]{1,0:T(8,128)(2,1)S(1)}, u32[]{:S(2)}, u32[]{:S(2)}) collective-permute-start(bf16[128,1024]{1,0:T(8,128)(2,1)S(1)} %back.1.path_grad_ref.refs_0_), channel_id=1, source_target_pairs={{0,192},{32,224},{64,0},{96,32},{128,64},{160,96},{192,128},{224,1... | collective-permute-start | bytes 786440 | tf_op jit(solution)/shard_map/ppermute | solution.py:496
  69.8 1.2 %collective-permute-start.6 = (bf16[128,1024]{1,0:T(8,128)(2,1)S(1)}, bf16[128,1024]{1,0:T(8,128)(2,1)S(1)}, u32[]{:S(2)}, u32[]{:S(2)}) collective-permute-start(bf16[128,1024]{1,0:T(8,128)(2,1)S(1)} %back.1.path_grad_ref.refs_0_), channel_id=1, source_target_pairs={{0,128},{32,160},{64,192},{96,224},{128,0},{160,32},{192,64},{224,... | collective-permute-start | bytes 786440 | tf_op jit(solution)/shard_map/ppermute | solution.py:496
  71.0 3.2 %collective-permute-start.4 = (bf16[128,1024]{1,0:T(8,128)(2,1)S(1)}, bf16[128,1024]{1,0:T(8,128)(2,1)S(1)}, u32[]{:S(2)}, u32[]{:S(2)}) collective-permute-start(bf16[128,1024]{1,0:T(8,128)(2,1)S(1)} %back.1.path_grad_ref.refs_0_), channel_id=1, source_target_pairs={{0,32},{32,0},{64,96},{96,64},{128,160},{160,128},{192,224},{224,1... | collective-permute-start | bytes 786440 | tf_op jit(solution)/shard_map/ppermute | solution.py:492
  74.2 2.2 %score.1 = f32[32,8,128]{2,1,0:T(8,128)} custom-call(bf16[128,1024]{1,0:T(8,128)(2,1)S(1)} %back.1.path_grad_ref.refs_0_, bf16[2048,1024]{1,0:T(8,128)(2,1)S(1)} %bitcast.7), custom_call_target="tpu_custom_call" | custom-call | tf_op jit(solution)/shard_map/score/pallas_call | solution.py:436
  76.4 4.3 %all-to-all-start.2 = ((f32[32,8,128]{2,1,0:T(8,128)}), f32[32,8,128]{2,1,0:T(8,128)S(1)}, u32[]{:S(2)}, u32[]{:S(2)}) async-start(f32[32,8,128]{2,1,0:T(8,128)} %score.1), calls=%async_computation.2 | async-start | bytes 262144 | tf_op jit(solution)/shard_map/all_to_all | solution.py:512
  81.1 1.9 %collective-permute-start.9 = (bf16[128,1024]{1,0:T(8,128)(2,1)S(1)}, bf16[128,1024]{1,0:T(8,128)(2,1)S(1)}, u32[]{:S(2)}, u32[]{:S(2)}) collective-permute-start(bf16[128,1024]{1,0:T(8,128)(2,1)S(1)} %collective-permute-done.6.refs_2_), channel_id=1, source_target_pairs={{0,32},{32,0},{64,96},{96,64},{128,160},{160,128},{192,224},{224,1... | collective-permute-start | bytes 786440 | tf_op jit(solution)/shard_map/ppermute | solution.py:492
  83.0 0.9 collective-permute-done.5.refs_1_
  84.0 1.7 %collective-permute-start.8 = (bf16[128,1024]{1,0:T(8,128)(2,1)S(1)}, bf16[128,1024]{1,0:T(8,128)(2,1)S(1)}, u32[]{:S(2)}, u32[]{:S(2)}) collective-permute-start(bf16[128,1024]{1,0:T(8,128)(2,1)S(1)} %collective-permute-done.5.refs_1_), channel_id=1, source_target_pairs={{0,32},{32,0},{64,96},{96,64},{128,160},{160,128},{192,224},{224,1... | collective-permute-start | bytes 786440 | tf_op jit(solution)/shard_map/ppermute | solution.py:492
  85.7 5.1 %all-to-all-done.2 = f32[32,8,128]{2,1,0:T(8,128)S(1)} async-done(((f32[32,8,128]{2,1,0:T(8,128)}), f32[32,8,128]{2,1,0:T(8,128)S(1)}, u32[]{:S(2)}, u32[]{:S(2)}) %all-to-all-start.2) | async-done | bytes 131104 | tf_op jit(solution)/shard_map/all_to_all | solution.py:512
  90.8 10.6 %all_to_all.21.score_ref = f32[8,8,128]{2,1,0:T(8,128)S(1)} all-to-all(f32[8,8,128]{2,1,0:T(8,128)S(1)} %broadcast_in_dim.2), channel_id=1, replica_groups=mesh['star'=8,'row'=32] {'star'}, dimensions={0} | all-to-all | bytes 65536 | tf_op jit(solution)/shard_map/all_to_all | solution.py:516
  101.3 2.7 %total.1 = (f32[256,1024]{1,0:T(8,128)}, f32[64,64]{1,0:T(8,128)}) custom-call(bf16[64,64]{1,0:T(8,128)(2,1)S(1)} %get-tuple-element.19.coef_ref, f32[64,64]{1,0:T(8,128)S(1)} %get-tuple-element.20.hot_ref, f32[8,8,128]{2,1,0:T(8,128)S(1)} %all_to_all.21.score_ref, bf16[128,1024]{1,0:T(8,128)(2,1)S(1)} %back.1.path_grad_ref.refs_0_, ...), custom_call_target="tpu_custom_call" | custom-call | tf_op jit(solution)/shard_map/total/pallas_call | solution.py:476
  (20 shorter events, 0.4 us)
Async XLA Ops:
  0.6 9.6 %collective-permute-start = (bf16[12,32,1024]{2,1,0:T(8,128)(2,1)}, bf16[12,32,1024]{2,1,0:T(8,128)(2,1)S(1)}, u32[]{:S(2)}, u32[]{:S(2)}) collective-permute-start(bf16[12,32,1024]{2,1,0:T(8,128)(2,1)} %own_hbm.3), channel_id=1, source_target_pairs={{0,32},{32,0},{64,96},{96,64},{128,160},{160,128},{192,224},{224,1... | collective-permute-start | bytes 2359304 | tf_op jit(solution)/shard_map/ppermute | solution.py:492
  10.3 27.3 %copy-start.1 = (bf16[12,32,1024]{2,1,0:T(8,128)(2,1)}, bf16[12,32,1024]{2,1,0:T(8,128)(2,1)S(1)}, u32[]{:S(2)}) copy-start(bf16[12,32,1024]{2,1,0:T(8,128)(2,1)S(1)} %collective-permute-done.twin_hbm) | copy-start | bytes 2359300
  11.3 26.3 %all-to-all-start = ((bf16[32,32,256]{2,1,0:T(8,128)(2,1)}), bf16[32,32,256]{2,1,0:T(8,128)(2,1)S(1)}, u32[]{:S(2)}, u32[]{:S(2)}) async-start(bf16[32,32,256]{2,1,0:T(8,128)(2,1)} %bitcast.11), calls=%async_computation | async-start | bytes 1048576 | tf_op jit(solution)/shard_map/all_to_all | solution.py:507
  20.8 9.5 %collective-permute-start.1 = (bf16[3,32,1024]{2,1,0:T(8,128)(2,1)}, bf16[3,32,1024]{2,1,0:T(8,128)(2,1)S(1)}, u32[]{:S(2)}, u32[]{:S(2)}) collective-permute-start(bf16[3,32,1024]{2,1,0:T(8,128)(2,1)} %get-tuple-element.28), channel_id=1, source_target_pairs={{0,64},{32,96},{64,128},{96,160},{128,192},{160,224},{192,0},{224,... | collective-permute-start | bytes 589832 | tf_op jit(solution)/shard_map/ppermute | solution.py:496
  22.0 13.7 %collective-permute-start.2 = (bf16[3,32,1024]{2,1,0:T(8,128)(2,1)}, bf16[3,32,1024]{2,1,0:T(8,128)(2,1)S(1)}, u32[]{:S(2)}, u32[]{:S(2)}) collective-permute-start(bf16[3,32,1024]{2,1,0:T(8,128)(2,1)} %get-tuple-element.29), channel_id=1, source_target_pairs={{0,128},{32,160},{64,192},{96,224},{128,0},{160,32},{192,64},{224,... | collective-permute-start | bytes 589832 | tf_op jit(solution)/shard_map/ppermute | solution.py:496
  25.9 10.5 %collective-permute-start.3 = (bf16[3,32,1024]{2,1,0:T(8,128)(2,1)}, bf16[3,32,1024]{2,1,0:T(8,128)(2,1)}, u32[]{:S(2)}, u32[]{:S(2)}) collective-permute-start(bf16[3,32,1024]{2,1,0:T(8,128)(2,1)} %get-tuple-element.30), channel_id=1, source_target_pairs={{0,192},{32,224},{64,0},{96,32},{128,64},{160,96},{192,128},{224,1... | collective-permute-start | bytes 589832 | tf_op jit(solution)/shard_map/ppermute | solution.py:496
  30.2 5.5 %copy-start.2 = (bf16[3,32,1024]{2,1,0:T(8,128)(2,1)}, bf16[3,32,1024]{2,1,0:T(8,128)(2,1)S(1)}, u32[]{:S(2)}) copy-start(bf16[3,32,1024]{2,1,0:T(8,128)(2,1)S(1)} %collective-permute-done.1.one_hbm) | copy-start | bytes 589828
  35.7 0.7 copy-start.3
  37.6 36.7 %copy-start = (bf16[64,32,1024]{2,1,0:T(8,128)(2,1)S(1)}, bf16[64,32,1024]{2,1,0:T(8,128)(2,1)}, u32[]{:S(2)}) copy-start(bf16[64,32,1024]{2,1,0:T(8,128)(2,1)} %param.7) | copy-start | bytes 12582916
  68.7 12.1 %collective-permute-start.7 = (bf16[128,1024]{1,0:T(8,128)(2,1)S(1)}, bf16[128,1024]{1,0:T(8,128)(2,1)S(1)}, u32[]{:S(2)}, u32[]{:S(2)}) collective-permute-start(bf16[128,1024]{1,0:T(8,128)(2,1)S(1)} %back.1.path_grad_ref.refs_0_), channel_id=1, source_target_pairs={{0,192},{32,224},{64,0},{96,32},{128,64},{160,96},{192,128},{224,1... | collective-permute-start | bytes 786440 | tf_op jit(solution)/shard_map/ppermute | solution.py:496
  69.8 11.3 %collective-permute-start.6 = (bf16[128,1024]{1,0:T(8,128)(2,1)S(1)}, bf16[128,1024]{1,0:T(8,128)(2,1)S(1)}, u32[]{:S(2)}, u32[]{:S(2)}) collective-permute-start(bf16[128,1024]{1,0:T(8,128)(2,1)S(1)} %back.1.path_grad_ref.refs_0_), channel_id=1, source_target_pairs={{0,128},{32,160},{64,192},{96,224},{128,0},{160,32},{192,64},{224,... | collective-permute-start | bytes 786440 | tf_op jit(solution)/shard_map/ppermute | solution.py:496
  71.0 12.9 %collective-permute-start.5 = (bf16[128,1024]{1,0:T(8,128)(2,1)S(1)}, bf16[128,1024]{1,0:T(8,128)(2,1)S(1)}, u32[]{:S(2)}, u32[]{:S(2)}) collective-permute-start(bf16[128,1024]{1,0:T(8,128)(2,1)S(1)} %back.1.path_grad_ref.refs_0_), channel_id=1, source_target_pairs={{0,64},{32,96},{64,128},{96,160},{128,192},{160,224},{192,0},{224,... | collective-permute-start | bytes 786440 | tf_op jit(solution)/shard_map/ppermute | solution.py:496
  71.0 19.7 %collective-permute-start.4 = (bf16[128,1024]{1,0:T(8,128)(2,1)S(1)}, bf16[128,1024]{1,0:T(8,128)(2,1)S(1)}, u32[]{:S(2)}, u32[]{:S(2)}) collective-permute-start(bf16[128,1024]{1,0:T(8,128)(2,1)S(1)} %back.1.path_grad_ref.refs_0_), channel_id=1, source_target_pairs={{0,32},{32,0},{64,96},{96,64},{128,160},{160,128},{192,224},{224,1... | collective-permute-start | bytes 786440 | tf_op jit(solution)/shard_map/ppermute | solution.py:492
  76.4 14.3 %all-to-all-start.2 = ((f32[32,8,128]{2,1,0:T(8,128)}), f32[32,8,128]{2,1,0:T(8,128)S(1)}, u32[]{:S(2)}, u32[]{:S(2)}) async-start(f32[32,8,128]{2,1,0:T(8,128)} %score.1), calls=%async_computation.2 | async-start | bytes 262144 | tf_op jit(solution)/shard_map/all_to_all | solution.py:512
  80.8 20.6 %collective-permute-start.10 = (bf16[128,1024]{1,0:T(8,128)(2,1)S(1)}, bf16[128,1024]{1,0:T(8,128)(2,1)S(1)}, u32[]{:S(2)}, u32[]{:S(2)}) collective-permute-start(bf16[128,1024]{1,0:T(8,128)(2,1)S(1)} %collective-permute-done.7.refs_3_), channel_id=1, source_target_pairs={{0,32},{32,0},{64,96},{96,64},{128,160},{160,128},{192,224},{224,1... | collective-permute-start | bytes 786440 | tf_op jit(solution)/shard_map/ppermute | solution.py:492
  81.1 20.2 %collective-permute-start.9 = (bf16[128,1024]{1,0:T(8,128)(2,1)S(1)}, bf16[128,1024]{1,0:T(8,128)(2,1)S(1)}, u32[]{:S(2)}, u32[]{:S(2)}) collective-permute-start(bf16[128,1024]{1,0:T(8,128)(2,1)S(1)} %collective-permute-done.6.refs_2_), channel_id=1, source_target_pairs={{0,32},{32,0},{64,96},{96,64},{128,160},{160,128},{192,224},{224,1... | collective-permute-start | bytes 786440 | tf_op jit(solution)/shard_map/ppermute | solution.py:492
  84.0 17.4 %collective-permute-start.8 = (bf16[128,1024]{1,0:T(8,128)(2,1)S(1)}, bf16[128,1024]{1,0:T(8,128)(2,1)S(1)}, u32[]{:S(2)}, u32[]{:S(2)}) collective-permute-start(bf16[128,1024]{1,0:T(8,128)(2,1)S(1)} %collective-permute-done.5.refs_1_), channel_id=1, source_target_pairs={{0,32},{32,0},{64,96},{96,64},{128,160},{160,128},{192,224},{224,1... | collective-permute-start | bytes 786440 | tf_op jit(solution)/shard_map/ppermute | solution.py:492

commit v6 on v4

--- a/solution.py
+++ b/solution.py
@@ -428,15 +428,16 @@
     by_lane = jnp.concatenate(parts, axis=0)
     pick_star = jnp.where((iota((8, 128), 1) >> 5) == iota((8, 128), 0), 1.0, 0.0)
     scores = dot(pick_star, by_lane, NT, lax.Precision.HIGHEST)
-    wide = jnp.concatenate([scores, jnp.zeros_like(scores)], axis=1)
-    score_ref[...] = jnp.broadcast_to(wide[None], score_ref.shape)
+    for j in range(2):
+        pair = jnp.concatenate([scores[2 * j : 2 * j + 1], scores[2 * j + 1 : 2 * j + 2]], axis=1)
+        score_ref[:, j, :] = jnp.broadcast_to(pair, (32, 128))
 
 
 def score_of(path_grad, maps):
     return pl.pallas_call(
         score_kernel,
         name="score",
-        out_shape=jax.ShapeDtypeStruct((32, 8, 128), F32),
+        out_shape=jax.ShapeDtypeStruct((32, 2, 128), F32),
         in_specs=[VMEM_SPEC, VMEM_SPEC],
         out_specs=VMEM_SPEC,
         compiler_params=params(16),
@@ -464,9 +465,15 @@
         store = pltpu.make_async_copy(map_grad.at[at], map_grad_hbm.at[at], out_sem.at[m])
         store.start()
         stores.append(store)
-    scores = score_ref[...].reshape(64, 128)
-    grad = dot(hot_ref[...], scores, TN, lax.Precision.HIGHEST) * (1.0 / (8 * N))
-    coef_grad_ref[...] = grad[:, :MAPS]
+    grads = []
+    for half in range(2):
+        grad = jnp.zeros((64, 128), F32)
+        for j in range(2):
+            place = iota((GROUPS, 64), 0) * 8 + 2 * j + half
+            rows = dot(jnp.where(iota((GROUPS, 64), 1) == place, 1.0, 0.0), hot_ref[...])
+            grad = grad + dot(rows, score_ref[:, j, :], TN, lax.Precision.HIGHEST)
+        grads.append(grad[:, half * MAPS : half * MAPS + MAPS])
+    coef_grad_ref[...] = (grads[0] + grads[1]) * (1.0 / (8 * N))
     for store in stores:
         store.wait()
 
@@ -512,7 +519,7 @@
     score = lax.all_to_all(score_of(path_grad, maps), "row", 0, 0, tiled=True)
     score, *blocks = lax.optimization_barrier((score, *blocks))
     blocks = blocks + [swap_cores(block) for block in blocks]
-    score = jnp.broadcast_to(jnp.sum(score, 0)[None], (GROUPS, 8, 128))
+    score = jnp.broadcast_to(jnp.sum(score, 0)[None], (GROUPS, 2, 128))
     score = lax.all_to_all(score, "star", 0, 0, tiled=True)
     map_grad, coef_grad = total(coef, hot, score, blocks)
     return map_grad.reshape(MAPS // GROUPS, BLK, N), coef_grad

time: 103 us -> 102 us (level)
  waiting for transfers between devices: 13.2 us -> 11.3 us
  blocking collectives: 43 us -> 44.4 us
  Pallas kernels: 20.1 us -> 18.9 us
    pallas_call x1, Pallas kernels: 2.34 us -> 0.97 us  [pack(): pl.pallas_call(pack_kernel, name='pack', out_shape=[pltpu.HBM((3, BLK, N)...]
    all_to_all x1, waiting for transfers between devices: 4.59 us -> 3.23 us  [per_device(): lax.all_to_all(sent.reshape(32, BLK, 256), 'row', 0, 0, tiled=True)]
  transfers between devices with their start and end apart: 12 -> 12, of which waited for: 4 -> 3; matrix products, arithmetic and copies ran while one was open for 0% -> 0% of each run, Pallas kernels for 8% -> 8%
where the time goes in v6:
time: 102 us
  blocking collectives  44.4 us (44%)
  starting transfers between devices  25.5 us (25%)
  Pallas kernels  18.9 us (19%)
  waiting for transfers between devices  11.3 us (11%)
    all_to_all x1, blocking collectives, per_device(): lax.all_to_all(sent.reshape(32, BLK, 256), 'row', 0, 0, tiled=True)  20.8 us
    all_to_all x1, blocking collectives, per_device(): score = lax.all_to_all(score_of(path_grad, maps), 'row', 0, 0, tiled=True)  14.6 us
    all_to_all x1, starting transfers between devices, per_device(): lax.all_to_all(sent.reshape(32, BLK, 256), 'row', 0, 0, tiled=True)  9.49 us
    all_to_all x1, blocking collectives, per_device(): score = lax.all_to_all(score, 'star', 0, 0, tiled=True)  9.12 us
    ppermute x6, starting transfers between devices, along_x(): lax.ppermute(x, 'star', [(g, (g + 2 * k) % GROUPS) for g in range(GROUPS)])  8.16 us
    ppermute x6, waiting for transfers between devices, along_x(): lax.ppermute(x, 'star', [(g, (g + 2 * k) % GROUPS) for g in range(GROUPS)])  8.01 us
    ppermute x5, starting transfers between devices, swap_cores(): return lax.ppermute(x, 'star', [(g, g ^ 1) for g in range(GROUPS)])  7.84 us
    pallas_call x1, Pallas kernels, pupil(): pl.pallas_call(pupil_kernel, name='pupil', out_shape=[pltpu.HBM((N, 256),...  6.3 us
  transfers between devices with their start and end apart: 12, of which 3 were waited for; matrix products, arithmetic and copies ran while one was open for 0% of the time, Pallas kernels for 8%

profile of v6, /device:TPU:1, one launch (start us, length us, event | category | flops | bytes accessed | tf_op | source)
XLA Modules:
  0.0 101.7 jit_solution(7005428019558467665)
XLA Ops:
  0.6 3.3 %collective-permute-start = (bf16[12,32,1024]{2,1,0:T(8,128)(2,1)}, bf16[12,32,1024]{2,1,0:T(8,128)(2,1)S(1)}, u32[]{:S(2)}, u32[]{:S(2)}) collective-permute-start(bf16[12,32,1024]{2,1,0:T(8,128)(2,1)} %own_hbm.3), channel_id=1, source_target_pairs={{0,32},{32,0},{64,96},{96,64},{128,160},{160,128},{192,224},{224,1... | collective-permute-start | bytes 2359304 | tf_op jit(solution)/shard_map/ppermute | solution.py:499
  4.0 6.3 %pupil.1 = (bf16[1024,256]{1,0:T(8,128)(2,1)}, f32[128,1024]{1,0:T(8,128)}, bf16[2,512,1024]{2,1,0:T(8,128)(2,1)S(1)}, f32[64,64]{1,0:T(8,128)S(1)}, bf16[64,64]{1,0:T(8,128)(2,1)S(1)}, /*index=5*/s32[17]{0:T(128)S(1)}) custom-call(s32[8]{0:T(128)} %counts_hbm.1, s32[8,12]{1,0:T(8,128)} %cells_hbm.1, s32[8,12]{1,0:T(8,128)} %bands_hbm.1, ...), custom_call_target="tpu_custom_call" | custom-call | tf_op jit(solution)/shard_map/pupil/pallas_call | solution.py:219
  10.3 1.0 pack.1
  11.3 9.5 %all-to-all-start = ((bf16[32,32,256]{2,1,0:T(8,128)(2,1)}), bf16[32,32,256]{2,1,0:T(8,128)(2,1)S(1)}, u32[]{:S(2)}, u32[]{:S(2)}) async-start(bf16[32,32,256]{2,1,0:T(8,128)(2,1)} %bitcast.11), calls=%async_computation | async-start | bytes 1048576 | tf_op jit(solution)/shard_map/all_to_all | solution.py:514
  20.8 2.1 %collective-permute-start.1 = (bf16[3,32,1024]{2,1,0:T(8,128)(2,1)}, bf16[3,32,1024]{2,1,0:T(8,128)(2,1)S(1)}, u32[]{:S(2)}, u32[]{:S(2)}) collective-permute-start(bf16[3,32,1024]{2,1,0:T(8,128)(2,1)} %get-tuple-element.31), channel_id=1, source_target_pairs={{0,64},{32,96},{64,128},{96,160},{128,192},{160,224},{192,0},{224,... | collective-permute-start | bytes 589832 | tf_op jit(solution)/shard_map/ppermute | solution.py:503
  22.9 1.6 %collective-permute-start.2 = (bf16[3,32,1024]{2,1,0:T(8,128)(2,1)}, bf16[3,32,1024]{2,1,0:T(8,128)(2,1)S(1)}, u32[]{:S(2)}, u32[]{:S(2)}) collective-permute-start(bf16[3,32,1024]{2,1,0:T(8,128)(2,1)} %get-tuple-element.32), channel_id=1, source_target_pairs={{0,128},{32,160},{64,192},{96,224},{128,0},{160,32},{192,64},{224,... | collective-permute-start | bytes 589832 | tf_op jit(solution)/shard_map/ppermute | solution.py:503
  24.5 1.2 %collective-permute-start.3 = (bf16[3,32,1024]{2,1,0:T(8,128)(2,1)}, bf16[3,32,1024]{2,1,0:T(8,128)(2,1)}, u32[]{:S(2)}, u32[]{:S(2)}) collective-permute-start(bf16[3,32,1024]{2,1,0:T(8,128)(2,1)} %get-tuple-element.33), channel_id=1, source_target_pairs={{0,192},{32,224},{64,0},{96,32},{128,64},{160,96},{192,128},{224,1... | collective-permute-start | bytes 589832 | tf_op jit(solution)/shard_map/ppermute | solution.py:503
  25.7 2.8 %collective-permute-done.1.one_hbm = bf16[3,32,1024]{2,1,0:T(8,128)(2,1)S(1)} collective-permute-done((bf16[3,32,1024]{2,1,0:T(8,128)(2,1)}, bf16[3,32,1024]{2,1,0:T(8,128)(2,1)S(1)}, u32[]{:S(2)}, u32[]{:S(2)}) %collective-permute-start.1) | collective-permute-done | bytes 196640 | tf_op jit(solution)/shard_map/ppermute | solution.py:503
  28.5 5.2 %collective-permute-done.2.two_hbm = bf16[3,32,1024]{2,1,0:T(8,128)(2,1)S(1)} collective-permute-done((bf16[3,32,1024]{2,1,0:T(8,128)(2,1)}, bf16[3,32,1024]{2,1,0:T(8,128)(2,1)S(1)}, u32[]{:S(2)}, u32[]{:S(2)}) %collective-permute-start.2) | collective-permute-done | bytes 196640 | tf_op jit(solution)/shard_map/ppermute | solution.py:503
  33.7 0.7 copy-done.3
  34.3 3.2 %all-to-all-done = bf16[32,32,256]{2,1,0:T(8,128)(2,1)S(1)} async-done(((bf16[32,32,256]{2,1,0:T(8,128)(2,1)}), bf16[32,32,256]{2,1,0:T(8,128)(2,1)S(1)}, u32[]{:S(2)}, u32[]{:S(2)}) %all-to-all-start) | async-done | bytes 524320 | tf_op jit(solution)/shard_map/all_to_all | solution.py:514
  37.6 4.3 %focal.1 = bf16[1024,256]{1,0:T(8,128)(2,1)S(1)} custom-call(s32[17]{0:T(128)S(1)} %get-tuple-element.24.meta_ref, bf16[1024,256]{1,0:T(8,128)(2,1)S(1)} %bitcast.9, bf16[2,512,1024]{2,1,0:T(8,128)(2,1)S(1)} %get-tuple-element.30.tables, bf16[12,32,1024]{2,1,0:T(8,128)(2,1)} %own_hbm.3, bf16[12,32,1024]{2,1,0:T(8,128)(2,1)} %copy-done.1, ...), custom_call_target="tpu_custom_call" | custom-call | tf_op jit(solution)/shard_map/focal/pallas_call | solution.py:367
  41.9 20.8 %all_to_all.20 = bf16[32,32,256]{2,1,0:T(8,128)(2,1)S(1)} all-to-all(bf16[32,32,256]{2,1,0:T(8,128)(2,1)S(1)} %bitcast.10), channel_id=1, replica_groups=mesh['star'=8,'row'=32] {'row'}, dimensions={0} | all-to-all | bytes 1048576 | tf_op jit(solution)/shard_map/all_to_all | solution.py:516
  62.7 2.9 %back.1.path_grad_ref.refs_0_ = bf16[128,1024]{1,0:T(8,128)(2,1)S(1)} custom-call(s32[17]{0:T(128)S(1)} %get-tuple-element.24.meta_ref, bf16[1024,256]{1,0:T(8,128)(2,1)S(1)} %bitcast.8, bf16[2,512,1024]{2,1,0:T(8,128)(2,1)S(1)} %get-tuple-element.30.tables, f32[128,1024]{1,0:T(8,128)} %get-tuple-element.34.frac_hbm), custom_call_target="tpu_custom_call" | custom-call | tf_op jit(solution)/shard_map/back/pallas_call | solution.py:405
  65.6 2.6 %collective-permute-start.6 = (bf16[128,1024]{1,0:T(8,128)(2,1)S(1)}, bf16[128,1024]{1,0:T(8,128)(2,1)S(1)}, u32[]{:S(2)}, u32[]{:S(2)}) collective-permute-start(bf16[128,1024]{1,0:T(8,128)(2,1)S(1)} %back.1.path_grad_ref.refs_0_), channel_id=1, source_target_pairs={{0,192},{32,224},{64,0},{96,32},{128,64},{160,96},{192,128},{224,1... | collective-permute-start | bytes 786440 | tf_op jit(solution)/shard_map/ppermute | solution.py:503
  68.2 0.4 collective-permute-start.5
  68.6 0.3 collective-permute-start.4
  68.9 1.6 %score.1 = f32[32,2,128]{2,1,0:T(2,128)S(1)} custom-call(bf16[128,1024]{1,0:T(8,128)(2,1)S(1)} %back.1.path_grad_ref.refs_0_, bf16[2048,1024]{1,0:T(8,128)(2,1)S(1)} %bitcast.7), custom_call_target="tpu_custom_call" | custom-call | tf_op jit(solution)/shard_map/score/pallas_call | solution.py:437
  70.5 14.6 %all_to_all.21 = f32[32,2,128]{2,1,0:T(2,128)S(1)} all-to-all(f32[32,2,128]{2,1,0:T(2,128)S(1)} %score.1), channel_id=1, replica_groups=mesh['star'=8,'row'=32] {'row'}, dimensions={0} | all-to-all | bytes 65536 | tf_op jit(solution)/shard_map/all_to_all | solution.py:519
  85.0 3.9 %collective-permute-start.7 = (bf16[128,1024]{1,0:T(8,128)(2,1)S(1)}, bf16[128,1024]{1,0:T(8,128)(2,1)S(1)}, u32[]{:S(2)}, u32[]{:S(2)}) collective-permute-start(bf16[128,1024]{1,0:T(8,128)(2,1)S(1)} %back.1.path_grad_ref.refs_0_), channel_id=1, source_target_pairs={{0,32},{32,0},{64,96},{96,64},{128,160},{160,128},{192,224},{224,1... | collective-permute-start | bytes 786440 | tf_op jit(solution)/shard_map/ppermute | solution.py:499
  88.9 0.1 collective-permute-start.8
  89.0 0.4 collective-permute-start.9
  89.6 9.1 %all_to_all.22.score_ref = f32[8,2,128]{2,1,0:T(2,128)S(1)} all-to-all(f32[8,2,128]{2,1,0:T(2,128)S(1)} %broadcast_in_dim.2), channel_id=1, replica_groups=mesh['star'=8,'row'=32] {'star'}, dimensions={0} | all-to-all | bytes 16384 | tf_op jit(solution)/shard_map/all_to_all | solution.py:523
  98.8 2.7 %total.1 = (f32[256,1024]{1,0:T(8,128)}, f32[64,64]{1,0:T(8,128)}) custom-call(bf16[64,64]{1,0:T(8,128)(2,1)S(1)} %get-tuple-element.22.coef_ref, f32[64,64]{1,0:T(8,128)S(1)} %get-tuple-element.23.hot_ref, f32[8,2,128]{2,1,0:T(2,128)S(1)} %all_to_all.22.score_ref, bf16[128,1024]{1,0:T(8,128)(2,1)S(1)} %back.1.path_grad_ref.refs_0_, ...), custom_call_target="tpu_custom_call" | custom-call | tf_op jit(solution)/shard_map/total/pallas_call | solution.py:483
  (19 shorter events, 0.2 us)
Async XLA Ops:
  0.6 9.6 %collective-permute-start = (bf16[12,32,1024]{2,1,0:T(8,128)(2,1)}, bf16[12,32,1024]{2,1,0:T(8,128)(2,1)S(1)}, u32[]{:S(2)}, u32[]{:S(2)}) collective-permute-start(bf16[12,32,1024]{2,1,0:T(8,128)(2,1)} %own_hbm.3), channel_id=1, source_target_pairs={{0,32},{32,0},{64,96},{96,64},{128,160},{160,128},{192,224},{224,1... | collective-permute-start | bytes 2359304 | tf_op jit(solution)/shard_map/ppermute | solution.py:499
  10.3 27.3 %copy-start.1 = (bf16[12,32,1024]{2,1,0:T(8,128)(2,1)}, bf16[12,32,1024]{2,1,0:T(8,128)(2,1)S(1)}, u32[]{:S(2)}) copy-start(bf16[12,32,1024]{2,1,0:T(8,128)(2,1)S(1)} %collective-permute-done.twin_hbm) | copy-start | bytes 2359300
  11.3 26.3 %all-to-all-start = ((bf16[32,32,256]{2,1,0:T(8,128)(2,1)}), bf16[32,32,256]{2,1,0:T(8,128)(2,1)S(1)}, u32[]{:S(2)}, u32[]{:S(2)}) async-start(bf16[32,32,256]{2,1,0:T(8,128)(2,1)} %bitcast.11), calls=%async_computation | async-start | bytes 1048576 | tf_op jit(solution)/shard_map/all_to_all | solution.py:514
  20.8 7.7 %collective-permute-start.1 = (bf16[3,32,1024]{2,1,0:T(8,128)(2,1)}, bf16[3,32,1024]{2,1,0:T(8,128)(2,1)S(1)}, u32[]{:S(2)}, u32[]{:S(2)}) collective-permute-start(bf16[3,32,1024]{2,1,0:T(8,128)(2,1)} %get-tuple-element.31), channel_id=1, source_target_pairs={{0,64},{32,96},{64,128},{96,160},{128,192},{160,224},{192,0},{224,... | collective-permute-start | bytes 589832 | tf_op jit(solution)/shard_map/ppermute | solution.py:503
  22.9 10.8 %collective-permute-start.2 = (bf16[3,32,1024]{2,1,0:T(8,128)(2,1)}, bf16[3,32,1024]{2,1,0:T(8,128)(2,1)S(1)}, u32[]{:S(2)}, u32[]{:S(2)}) collective-permute-start(bf16[3,32,1024]{2,1,0:T(8,128)(2,1)} %get-tuple-element.32), channel_id=1, source_target_pairs={{0,128},{32,160},{64,192},{96,224},{128,0},{160,32},{192,64},{224,... | collective-permute-start | bytes 589832 | tf_op jit(solution)/shard_map/ppermute | solution.py:503
  24.5 9.8 %collective-permute-start.3 = (bf16[3,32,1024]{2,1,0:T(8,128)(2,1)}, bf16[3,32,1024]{2,1,0:T(8,128)(2,1)}, u32[]{:S(2)}, u32[]{:S(2)}) collective-permute-start(bf16[3,32,1024]{2,1,0:T(8,128)(2,1)} %get-tuple-element.33), channel_id=1, source_target_pairs={{0,192},{32,224},{64,0},{96,32},{128,64},{160,96},{192,128},{224,1... | collective-permute-start | bytes 589832 | tf_op jit(solution)/shard_map/ppermute | solution.py:503
  28.5 5.2 %copy-start.2 = (bf16[3,32,1024]{2,1,0:T(8,128)(2,1)}, bf16[3,32,1024]{2,1,0:T(8,128)(2,1)S(1)}, u32[]{:S(2)}) copy-start(bf16[3,32,1024]{2,1,0:T(8,128)(2,1)S(1)} %collective-permute-done.1.one_hbm) | copy-start | bytes 589828
  33.7 0.7 copy-start.3
  37.6 31.3 %copy-start = (bf16[64,32,1024]{2,1,0:T(8,128)(2,1)S(1)}, bf16[64,32,1024]{2,1,0:T(8,128)(2,1)}, u32[]{:S(2)}) copy-start(bf16[64,32,1024]{2,1,0:T(8,128)(2,1)} %param.7) | copy-start | bytes 12582916
  65.6 19.4 %collective-permute-start.6 = (bf16[128,1024]{1,0:T(8,128)(2,1)S(1)}, bf16[128,1024]{1,0:T(8,128)(2,1)S(1)}, u32[]{:S(2)}, u32[]{:S(2)}) collective-permute-start(bf16[128,1024]{1,0:T(8,128)(2,1)S(1)} %back.1.path_grad_ref.refs_0_), channel_id=1, source_target_pairs={{0,192},{32,224},{64,0},{96,32},{128,64},{160,96},{192,128},{224,1... | collective-permute-start | bytes 786440 | tf_op jit(solution)/shard_map/ppermute | solution.py:503
  68.2 16.9 %collective-permute-start.5 = (bf16[128,1024]{1,0:T(8,128)(2,1)S(1)}, bf16[128,1024]{1,0:T(8,128)(2,1)S(1)}, u32[]{:S(2)}, u32[]{:S(2)}) collective-permute-start(bf16[128,1024]{1,0:T(8,128)(2,1)S(1)} %back.1.path_grad_ref.refs_0_), channel_id=1, source_target_pairs={{0,128},{32,160},{64,192},{96,224},{128,0},{160,32},{192,64},{224,... | collective-permute-start | bytes 786440 | tf_op jit(solution)/shard_map/ppermute | solution.py:503
  68.6 16.4 %collective-permute-start.4 = (bf16[128,1024]{1,0:T(8,128)(2,1)S(1)}, bf16[128,1024]{1,0:T(8,128)(2,1)S(1)}, u32[]{:S(2)}, u32[]{:S(2)}) collective-permute-start(bf16[128,1024]{1,0:T(8,128)(2,1)S(1)} %back.1.path_grad_ref.refs_0_), channel_id=1, source_target_pairs={{0,64},{32,96},{64,128},{96,160},{128,192},{160,224},{192,0},{224,... | collective-permute-start | bytes 786440 | tf_op jit(solution)/shard_map/ppermute | solution.py:503
  85.0 13.7 %collective-permute-start.7 = (bf16[128,1024]{1,0:T(8,128)(2,1)S(1)}, bf16[128,1024]{1,0:T(8,128)(2,1)S(1)}, u32[]{:S(2)}, u32[]{:S(2)}) collective-permute-start(bf16[128,1024]{1,0:T(8,128)(2,1)S(1)} %back.1.path_grad_ref.refs_0_), channel_id=1, source_target_pairs={{0,32},{32,0},{64,96},{96,64},{128,160},{160,128},{192,224},{224,1... | collective-permute-start | bytes 786440 | tf_op jit(solution)/shard_map/ppermute | solution.py:499
  88.9 9.8 %collective-permute-start.8 = (bf16[128,1024]{1,0:T(8,128)(2,1)S(1)}, bf16[128,1024]{1,0:T(8,128)(2,1)S(1)}, u32[]{:S(2)}, u32[]{:S(2)}) collective-permute-start(bf16[128,1024]{1,0:T(8,128)(2,1)S(1)} %collective-permute-done.4.refs_1_), channel_id=1, source_target_pairs={{0,32},{32,0},{64,96},{96,64},{128,160},{160,128},{192,224},{224,1... | collective-permute-start | bytes 786440 | tf_op jit(solution)/shard_map/ppermute | solution.py:499
  89.0 9.7 %collective-permute-start.9 = (bf16[128,1024]{1,0:T(8,128)(2,1)S(1)}, bf16[128,1024]{1,0:T(8,128)(2,1)S(1)}, u32[]{:S(2)}, u32[]{:S(2)}) collective-permute-start(bf16[128,1024]{1,0:T(8,128)(2,1)S(1)} %collective-permute-done.5.refs_2_), channel_id=1, source_target_pairs={{0,32},{32,0},{64,96},{96,64},{128,160},{160,128},{192,224},{224,1... | collective-permute-start | bytes 786440 | tf_op jit(solution)/shard_map/ppermute | solution.py:499
  89.5 9.3 %collective-permute-start.10 = (bf16[128,1024]{1,0:T(8,128)(2,1)S(1)}, bf16[128,1024]{1,0:T(8,128)(2,1)S(1)}, u32[]{:S(2)}, u32[]{:S(2)}) collective-permute-start(bf16[128,1024]{1,0:T(8,128)(2,1)S(1)} %collective-permute-done.6.refs_3_), channel_id=1, source_target_pairs={{0,32},{32,0},{64,96},{96,64},{128,160},{160,128},{192,224},{224,1... | collective-permute-start | bytes 786440 | tf_op jit(solution)/shard_map/ppermute | solution.py:499

commit v7 on v6

--- a/solution.py
+++ b/solution.py
@@ -459,8 +459,7 @@
     wide = dot(rows, each)
     spread = jnp.where(same_pixel(wide.shape), wide, 0.0).astype(BF)
     stores = []
-    for m in range(2):
-        at = slice(m * 128, m * 128 + 128)
+    for m, at in enumerate((slice(0, 128), slice(128, 192), slice(192, 256))):
         map_grad[at, :] = dot(spread[at], path_grad[...])
         store = pltpu.make_async_copy(map_grad.at[at], map_grad_hbm.at[at], out_sem.at[m])
         store.start()
@@ -489,7 +488,7 @@
         scratch_shapes=[
             pltpu.VMEM((N, N), BF),
             pltpu.VMEM((rows, N), F32),
-            pltpu.SemaphoreType.DMA((2,)),
+            pltpu.SemaphoreType.DMA((3,)),
         ],
         compiler_params=params(16),
     )(coef, hot, scores, *blocks)

time: 102 us -> 102 us (level)
  starting transfers between devices: 25.5 us -> 27.5 us
  blocking collectives: 44.4 us -> 43.1 us
    ppermute x6, starting transfers between devices: 8.16 us -> 10.2 us  [along_x(): lax.ppermute(x, 'star', [(g, (g + 2 * k) % GROUPS) for g in range(GROUPS)])]
    ppermute x6, waiting for transfers between devices: 8.01 us -> 6.9 us  [along_x(): lax.ppermute(x, 'star', [(g, (g + 2 * k) % GROUPS) for g in range(GROUPS)])]
    all_to_all x1, blocking collectives: 9.12 us -> 8.06 us  [per_device(): score = lax.all_to_all(score, 'star', 0, 0, tiled=True)]
where the time goes in v7:
time: 102 us
  blocking collectives  43.1 us (42%)
  starting transfers between devices  27.5 us (27%)
  Pallas kernels  19 us (19%)
  waiting for transfers between devices  10.3 us (10%)
    all_to_all x1, blocking collectives, per_device(): lax.all_to_all(sent.reshape(32, BLK, 256), 'row', 0, 0, tiled=True)  20.3 us
    all_to_all x1, blocking collectives, per_device(): score = lax.all_to_all(score_of(path_grad, maps), 'row', 0, 0, tiled=True)  14.7 us
    ppermute x6, starting transfers between devices, along_x(): lax.ppermute(x, 'star', [(g, (g + 2 * k) % GROUPS) for g in range(GROUPS)])  10.2 us
    all_to_all x1, starting transfers between devices, per_device(): lax.all_to_all(sent.reshape(32, BLK, 256), 'row', 0, 0, tiled=True)  9.49 us
    all_to_all x1, blocking collectives, per_device(): score = lax.all_to_all(score, 'star', 0, 0, tiled=True)  8.06 us
    ppermute x5, starting transfers between devices, swap_cores(): return lax.ppermute(x, 'star', [(g, g ^ 1) for g in range(GROUPS)])  7.84 us
    ppermute x6, waiting for transfers between devices, along_x(): lax.ppermute(x, 'star', [(g, (g + 2 * k) % GROUPS) for g in range(GROUPS)])  6.9 us
    pallas_call x1, Pallas kernels, pupil(): pl.pallas_call(pupil_kernel, name='pupil', out_shape=[pltpu.HBM((N, 256),...  6.3 us
  transfers between devices with their start and end apart: 12, of which 3 were waited for; matrix products, arithmetic and copies ran while one was open for 0% of the time, Pallas kernels for 8%

profile of v7, /device:TPU:1, one launch (start us, length us, event | category | flops | bytes accessed | tf_op | source)
XLA Modules:
  0.0 101.6 jit_solution(8033209252482078127)
XLA Ops:
  0.6 3.3 %collective-permute-start = (bf16[12,32,1024]{2,1,0:T(8,128)(2,1)}, bf16[12,32,1024]{2,1,0:T(8,128)(2,1)S(1)}, u32[]{:S(2)}, u32[]{:S(2)}) collective-permute-start(bf16[12,32,1024]{2,1,0:T(8,128)(2,1)} %own_hbm.3), channel_id=1, source_target_pairs={{0,32},{32,0},{64,96},{96,64},{128,160},{160,128},{192,224},{224,1... | collective-permute-start | bytes 2359304 | tf_op jit(solution)/shard_map/ppermute | solution.py:498
  4.0 6.3 %pupil.1 = (bf16[1024,256]{1,0:T(8,128)(2,1)}, f32[128,1024]{1,0:T(8,128)}, bf16[2,512,1024]{2,1,0:T(8,128)(2,1)S(1)}, f32[64,64]{1,0:T(8,128)S(1)}, bf16[64,64]{1,0:T(8,128)(2,1)S(1)}, /*index=5*/s32[17]{0:T(128)S(1)}) custom-call(s32[8]{0:T(128)} %counts_hbm.1, s32[8,12]{1,0:T(8,128)} %cells_hbm.1, s32[8,12]{1,0:T(8,128)} %bands_hbm.1, ...), custom_call_target="tpu_custom_call" | custom-call | tf_op jit(solution)/shard_map/pupil/pallas_call | solution.py:219
  10.3 1.0 pack.1
  11.3 9.5 %all-to-all-start = ((bf16[32,32,256]{2,1,0:T(8,128)(2,1)}), bf16[32,32,256]{2,1,0:T(8,128)(2,1)S(1)}, u32[]{:S(2)}, u32[]{:S(2)}) async-start(bf16[32,32,256]{2,1,0:T(8,128)(2,1)} %bitcast.11), calls=%async_computation | async-start | bytes 1048576 | tf_op jit(solution)/shard_map/all_to_all | solution.py:513
  20.8 1.3 %collective-permute-start.1 = (bf16[3,32,1024]{2,1,0:T(8,128)(2,1)}, bf16[3,32,1024]{2,1,0:T(8,128)(2,1)S(1)}, u32[]{:S(2)}, u32[]{:S(2)}) collective-permute-start(bf16[3,32,1024]{2,1,0:T(8,128)(2,1)} %get-tuple-element.31), channel_id=1, source_target_pairs={{0,64},{32,96},{64,128},{96,160},{128,192},{160,224},{192,0},{224,... | collective-permute-start | bytes 589832 | tf_op jit(solution)/shard_map/ppermute | solution.py:502
  22.0 2.6 %collective-permute-start.2 = (bf16[3,32,1024]{2,1,0:T(8,128)(2,1)}, bf16[3,32,1024]{2,1,0:T(8,128)(2,1)S(1)}, u32[]{:S(2)}, u32[]{:S(2)}) collective-permute-start(bf16[3,32,1024]{2,1,0:T(8,128)(2,1)} %get-tuple-element.32), channel_id=1, source_target_pairs={{0,128},{32,160},{64,192},{96,224},{128,0},{160,32},{192,64},{224,... | collective-permute-start | bytes 589832 | tf_op jit(solution)/shard_map/ppermute | solution.py:502
  24.6 2.0 %collective-permute-start.3 = (bf16[3,32,1024]{2,1,0:T(8,128)(2,1)}, bf16[3,32,1024]{2,1,0:T(8,128)(2,1)}, u32[]{:S(2)}, u32[]{:S(2)}) collective-permute-start(bf16[3,32,1024]{2,1,0:T(8,128)(2,1)} %get-tuple-element.33), channel_id=1, source_target_pairs={{0,192},{32,224},{64,0},{96,32},{128,64},{160,96},{192,128},{224,1... | collective-permute-start | bytes 589832 | tf_op jit(solution)/shard_map/ppermute | solution.py:502
  26.6 1.9 %collective-permute-done.1.one_hbm = bf16[3,32,1024]{2,1,0:T(8,128)(2,1)S(1)} collective-permute-done((bf16[3,32,1024]{2,1,0:T(8,128)(2,1)}, bf16[3,32,1024]{2,1,0:T(8,128)(2,1)S(1)}, u32[]{:S(2)}, u32[]{:S(2)}) %collective-permute-start.1) | collective-permute-done | bytes 196640 | tf_op jit(solution)/shard_map/ppermute | solution.py:502
  28.5 5.0 %collective-permute-done.2.two_hbm = bf16[3,32,1024]{2,1,0:T(8,128)(2,1)S(1)} collective-permute-done((bf16[3,32,1024]{2,1,0:T(8,128)(2,1)}, bf16[3,32,1024]{2,1,0:T(8,128)(2,1)S(1)}, u32[]{:S(2)}, u32[]{:S(2)}) %collective-permute-start.2) | collective-permute-done | bytes 196640 | tf_op jit(solution)/shard_map/ppermute | solution.py:502
  33.5 0.7 copy-done.3
  34.2 3.4 %all-to-all-done = bf16[32,32,256]{2,1,0:T(8,128)(2,1)S(1)} async-done(((bf16[32,32,256]{2,1,0:T(8,128)(2,1)}), bf16[32,32,256]{2,1,0:T(8,128)(2,1)S(1)}, u32[]{:S(2)}, u32[]{:S(2)}) %all-to-all-start) | async-done | bytes 524320 | tf_op jit(solution)/shard_map/all_to_all | solution.py:513
  37.6 4.3 %focal.1 = bf16[1024,256]{1,0:T(8,128)(2,1)S(1)} custom-call(s32[17]{0:T(128)S(1)} %get-tuple-element.24.meta_ref, bf16[1024,256]{1,0:T(8,128)(2,1)S(1)} %bitcast.9, bf16[2,512,1024]{2,1,0:T(8,128)(2,1)S(1)} %get-tuple-element.30.tables, bf16[12,32,1024]{2,1,0:T(8,128)(2,1)} %own_hbm.3, bf16[12,32,1024]{2,1,0:T(8,128)(2,1)} %copy-done.1, ...), custom_call_target="tpu_custom_call" | custom-call | tf_op jit(solution)/shard_map/focal/pallas_call | solution.py:367
  41.9 20.3 %all_to_all.20 = bf16[32,32,256]{2,1,0:T(8,128)(2,1)S(1)} all-to-all(bf16[32,32,256]{2,1,0:T(8,128)(2,1)S(1)} %bitcast.10), channel_id=1, replica_groups=mesh['star'=8,'row'=32] {'row'}, dimensions={0} | all-to-all | bytes 1048576 | tf_op jit(solution)/shard_map/all_to_all | solution.py:515
  62.2 2.9 %back.1.path_grad_ref.refs_0_ = bf16[128,1024]{1,0:T(8,128)(2,1)S(1)} custom-call(s32[17]{0:T(128)S(1)} %get-tuple-element.24.meta_ref, bf16[1024,256]{1,0:T(8,128)(2,1)S(1)} %bitcast.8, bf16[2,512,1024]{2,1,0:T(8,128)(2,1)S(1)} %get-tuple-element.30.tables, f32[128,1024]{1,0:T(8,128)} %get-tuple-element.34.frac_hbm), custom_call_target="tpu_custom_call" | custom-call | tf_op jit(solution)/shard_map/back/pallas_call | solution.py:405
  65.2 2.6 %collective-permute-start.6 = (bf16[128,1024]{1,0:T(8,128)(2,1)S(1)}, bf16[128,1024]{1,0:T(8,128)(2,1)S(1)}, u32[]{:S(2)}, u32[]{:S(2)}) collective-permute-start(bf16[128,1024]{1,0:T(8,128)(2,1)S(1)} %back.1.path_grad_ref.refs_0_), channel_id=1, source_target_pairs={{0,192},{32,224},{64,0},{96,32},{128,64},{160,96},{192,128},{224,1... | collective-permute-start | bytes 786440 | tf_op jit(solution)/shard_map/ppermute | solution.py:502
  67.8 1.0 collective-permute-start.5
  68.7 0.8 collective-permute-start.4
  69.5 1.6 %score.1 = f32[32,2,128]{2,1,0:T(2,128)S(1)} custom-call(bf16[128,1024]{1,0:T(8,128)(2,1)S(1)} %back.1.path_grad_ref.refs_0_, bf16[2048,1024]{1,0:T(8,128)(2,1)S(1)} %bitcast.7), custom_call_target="tpu_custom_call" | custom-call | tf_op jit(solution)/shard_map/score/pallas_call | solution.py:437
  71.1 14.7 %all_to_all.21 = f32[32,2,128]{2,1,0:T(2,128)S(1)} all-to-all(f32[32,2,128]{2,1,0:T(2,128)S(1)} %score.1), channel_id=1, replica_groups=mesh['star'=8,'row'=32] {'row'}, dimensions={0} | all-to-all | bytes 65536 | tf_op jit(solution)/shard_map/all_to_all | solution.py:518
  85.8 3.9 %collective-permute-start.7 = (bf16[128,1024]{1,0:T(8,128)(2,1)S(1)}, bf16[128,1024]{1,0:T(8,128)(2,1)S(1)}, u32[]{:S(2)}, u32[]{:S(2)}) collective-permute-start(bf16[128,1024]{1,0:T(8,128)(2,1)S(1)} %back.1.path_grad_ref.refs_0_), channel_id=1, source_target_pairs={{0,32},{32,0},{64,96},{96,64},{128,160},{160,128},{192,224},{224,1... | collective-permute-start | bytes 786440 | tf_op jit(solution)/shard_map/ppermute | solution.py:498
  89.7 0.1 collective-permute-start.8
  89.8 0.4 collective-permute-start.9
  90.4 8.1 %all_to_all.22.score_ref = f32[8,2,128]{2,1,0:T(2,128)S(1)} all-to-all(f32[8,2,128]{2,1,0:T(2,128)S(1)} %broadcast_in_dim.2), channel_id=1, replica_groups=mesh['star'=8,'row'=32] {'star'}, dimensions={0} | all-to-all | bytes 16384 | tf_op jit(solution)/shard_map/all_to_all | solution.py:522
  98.5 2.9 %total.1 = (f32[256,1024]{1,0:T(8,128)}, f32[64,64]{1,0:T(8,128)}) custom-call(bf16[64,64]{1,0:T(8,128)(2,1)S(1)} %get-tuple-element.22.coef_ref, f32[64,64]{1,0:T(8,128)S(1)} %get-tuple-element.23.hot_ref, f32[8,2,128]{2,1,0:T(2,128)S(1)} %all_to_all.22.score_ref, bf16[128,1024]{1,0:T(8,128)(2,1)S(1)} %back.1.path_grad_ref.refs_0_, ...), custom_call_target="tpu_custom_call" | custom-call | tf_op jit(solution)/shard_map/total/pallas_call | solution.py:482
  (19 shorter events, 0.2 us)
Async XLA Ops:
  0.6 9.6 %collective-permute-start = (bf16[12,32,1024]{2,1,0:T(8,128)(2,1)}, bf16[12,32,1024]{2,1,0:T(8,128)(2,1)S(1)}, u32[]{:S(2)}, u32[]{:S(2)}) collective-permute-start(bf16[12,32,1024]{2,1,0:T(8,128)(2,1)} %own_hbm.3), channel_id=1, source_target_pairs={{0,32},{32,0},{64,96},{96,64},{128,160},{160,128},{192,224},{224,1... | collective-permute-start | bytes 2359304 | tf_op jit(solution)/shard_map/ppermute | solution.py:498
  10.3 27.3 %copy-start.1 = (bf16[12,32,1024]{2,1,0:T(8,128)(2,1)}, bf16[12,32,1024]{2,1,0:T(8,128)(2,1)S(1)}, u32[]{:S(2)}) copy-start(bf16[12,32,1024]{2,1,0:T(8,128)(2,1)S(1)} %collective-permute-done.twin_hbm) | copy-start | bytes 2359300
  11.3 26.3 %all-to-all-start = ((bf16[32,32,256]{2,1,0:T(8,128)(2,1)}), bf16[32,32,256]{2,1,0:T(8,128)(2,1)S(1)}, u32[]{:S(2)}, u32[]{:S(2)}) async-start(bf16[32,32,256]{2,1,0:T(8,128)(2,1)} %bitcast.11), calls=%async_computation | async-start | bytes 1048576 | tf_op jit(solution)/shard_map/all_to_all | solution.py:513
  20.8 7.7 %collective-permute-start.1 = (bf16[3,32,1024]{2,1,0:T(8,128)(2,1)}, bf16[3,32,1024]{2,1,0:T(8,128)(2,1)S(1)}, u32[]{:S(2)}, u32[]{:S(2)}) collective-permute-start(bf16[3,32,1024]{2,1,0:T(8,128)(2,1)} %get-tuple-element.31), channel_id=1, source_target_pairs={{0,64},{32,96},{64,128},{96,160},{128,192},{160,224},{192,0},{224,... | collective-permute-start | bytes 589832 | tf_op jit(solution)/shard_map/ppermute | solution.py:502
  22.0 11.5 %collective-permute-start.2 = (bf16[3,32,1024]{2,1,0:T(8,128)(2,1)}, bf16[3,32,1024]{2,1,0:T(8,128)(2,1)S(1)}, u32[]{:S(2)}, u32[]{:S(2)}) collective-permute-start(bf16[3,32,1024]{2,1,0:T(8,128)(2,1)} %get-tuple-element.32), channel_id=1, source_target_pairs={{0,128},{32,160},{64,192},{96,224},{128,0},{160,32},{192,64},{224,... | collective-permute-start | bytes 589832 | tf_op jit(solution)/shard_map/ppermute | solution.py:502
  24.6 9.5 %collective-permute-start.3 = (bf16[3,32,1024]{2,1,0:T(8,128)(2,1)}, bf16[3,32,1024]{2,1,0:T(8,128)(2,1)}, u32[]{:S(2)}, u32[]{:S(2)}) collective-permute-start(bf16[3,32,1024]{2,1,0:T(8,128)(2,1)} %get-tuple-element.33), channel_id=1, source_target_pairs={{0,192},{32,224},{64,0},{96,32},{128,64},{160,96},{192,128},{224,1... | collective-permute-start | bytes 589832 | tf_op jit(solution)/shard_map/ppermute | solution.py:502
  28.5 5.0 %copy-start.2 = (bf16[3,32,1024]{2,1,0:T(8,128)(2,1)}, bf16[3,32,1024]{2,1,0:T(8,128)(2,1)S(1)}, u32[]{:S(2)}) copy-start(bf16[3,32,1024]{2,1,0:T(8,128)(2,1)S(1)} %collective-permute-done.1.one_hbm) | copy-start | bytes 589828
  33.5 0.7 copy-start.3
  37.6 31.9 %copy-start = (bf16[64,32,1024]{2,1,0:T(8,128)(2,1)S(1)}, bf16[64,32,1024]{2,1,0:T(8,128)(2,1)}, u32[]{:S(2)}) copy-start(bf16[64,32,1024]{2,1,0:T(8,128)(2,1)} %param.7) | copy-start | bytes 12582916
  65.2 20.6 %collective-permute-start.6 = (bf16[128,1024]{1,0:T(8,128)(2,1)S(1)}, bf16[128,1024]{1,0:T(8,128)(2,1)S(1)}, u32[]{:S(2)}, u32[]{:S(2)}) collective-permute-start(bf16[128,1024]{1,0:T(8,128)(2,1)S(1)} %back.1.path_grad_ref.refs_0_), channel_id=1, source_target_pairs={{0,192},{32,224},{64,0},{96,32},{128,64},{160,96},{192,128},{224,1... | collective-permute-start | bytes 786440 | tf_op jit(solution)/shard_map/ppermute | solution.py:502
  67.8 18.0 %collective-permute-start.5 = (bf16[128,1024]{1,0:T(8,128)(2,1)S(1)}, bf16[128,1024]{1,0:T(8,128)(2,1)S(1)}, u32[]{:S(2)}, u32[]{:S(2)}) collective-permute-start(bf16[128,1024]{1,0:T(8,128)(2,1)S(1)} %back.1.path_grad_ref.refs_0_), channel_id=1, source_target_pairs={{0,128},{32,160},{64,192},{96,224},{128,0},{160,32},{192,64},{224,... | collective-permute-start | bytes 786440 | tf_op jit(solution)/shard_map/ppermute | solution.py:502
  68.7 17.1 %collective-permute-start.4 = (bf16[128,1024]{1,0:T(8,128)(2,1)S(1)}, bf16[128,1024]{1,0:T(8,128)(2,1)S(1)}, u32[]{:S(2)}, u32[]{:S(2)}) collective-permute-start(bf16[128,1024]{1,0:T(8,128)(2,1)S(1)} %back.1.path_grad_ref.refs_0_), channel_id=1, source_target_pairs={{0,64},{32,96},{64,128},{96,160},{128,192},{160,224},{192,0},{224,... | collective-permute-start | bytes 786440 | tf_op jit(solution)/shard_map/ppermute | solution.py:502
  85.8 12.6 %collective-permute-start.7 = (bf16[128,1024]{1,0:T(8,128)(2,1)S(1)}, bf16[128,1024]{1,0:T(8,128)(2,1)S(1)}, u32[]{:S(2)}, u32[]{:S(2)}) collective-permute-start(bf16[128,1024]{1,0:T(8,128)(2,1)S(1)} %back.1.path_grad_ref.refs_0_), channel_id=1, source_target_pairs={{0,32},{32,0},{64,96},{96,64},{128,160},{160,128},{192,224},{224,1... | collective-permute-start | bytes 786440 | tf_op jit(solution)/shard_map/ppermute | solution.py:498
  89.7 8.7 %collective-permute-start.8 = (bf16[128,1024]{1,0:T(8,128)(2,1)S(1)}, bf16[128,1024]{1,0:T(8,128)(2,1)S(1)}, u32[]{:S(2)}, u32[]{:S(2)}) collective-permute-start(bf16[128,1024]{1,0:T(8,128)(2,1)S(1)} %collective-permute-done.4.refs_1_), channel_id=1, source_target_pairs={{0,32},{32,0},{64,96},{96,64},{128,160},{160,128},{192,224},{224,1... | collective-permute-start | bytes 786440 | tf_op jit(solution)/shard_map/ppermute | solution.py:498
  89.8 8.6 %collective-permute-start.9 = (bf16[128,1024]{1,0:T(8,128)(2,1)S(1)}, bf16[128,1024]{1,0:T(8,128)(2,1)S(1)}, u32[]{:S(2)}, u32[]{:S(2)}) collective-permute-start(bf16[128,1024]{1,0:T(8,128)(2,1)S(1)} %collective-permute-done.5.refs_2_), channel_id=1, source_target_pairs={{0,32},{32,0},{64,96},{96,64},{128,160},{160,128},{192,224},{224,1... | collective-permute-start | bytes 786440 | tf_op jit(solution)/shard_map/ppermute | solution.py:498
  90.2 8.2 %collective-permute-start.10 = (bf16[128,1024]{1,0:T(8,128)(2,1)S(1)}, bf16[128,1024]{1,0:T(8,128)(2,1)S(1)}, u32[]{:S(2)}, u32[]{:S(2)}) collective-permute-start(bf16[128,1024]{1,0:T(8,128)(2,1)S(1)} %collective-permute-done.6.refs_3_), channel_id=1, source_target_pairs={{0,32},{32,0},{64,96},{96,64},{128,160},{160,128},{192,224},{224,1... | collective-permute-start | bytes 786440 | tf_op jit(solution)/shard_map/ppermute | solution.py:498
